TPU v7x, 32 devices: a whole 2x2x4 slice. The times are simulated.
32 devices in a mesh: fsdp: 8 (over y, x, core), ctx: 2 (over z_hi), tp: 2 (over z_lo).
Axes of the slice: x: 2, y: 2, z: 4 (z_hi: 2, z_lo: 2; z = z_hi * 2 + z_lo), core: 2. Of those that a mesh axis runs over, the one named last changes fastest.
Arguments:
- layer_in: bfloat16 [16, 1024, 1024], P('fsdp', 'ctx'), may hold values from -6 to 6
- lengths: int32 [16], P('fsdp'), may hold values from 256 to 1024, as said below
- out_grad: bfloat16 [16, 1024, 1024], P('fsdp', 'ctx'), may hold values from -6 to 6
- query_weight: bfloat16 [1024, 1024], P('fsdp', 'tp'), may hold values from -0.1875 to 0.1875
- key_weight: bfloat16 [1024, 1024], P('fsdp', 'tp'), may hold values from -0.1875 to 0.1875
- value_weight: bfloat16 [1024, 1024], P('fsdp', 'tp'), may hold values from -0.1875 to 0.1875
- out_weight: bfloat16 [1024, 1024], P('tp', 'fsdp'), may hold values from -3 to 3
- up_weight: bfloat16 [1024, 4096], P('fsdp', 'tp'), may hold values from -0.1875 to 0.1875
- down_weight: bfloat16 [4096, 1024], P('tp', 'fsdp'), may hold values from -0.09375 to 0.09375
- query_bias: float32 [1024], P('tp'), may hold values from -4 to 4
- value_bias: float32 [1024], P('tp'), may hold values from -4 to 4
- out_bias: float32 [1024], replicated, may hold values from -4 to 4
- up_bias: float32 [4096], P('tp'), may hold values from -4 to 4
- down_bias: float32 [1024], replicated, may hold values from -4 to 4
- norm_gain: float32 [1024], replicated, may hold values from 0.5 to 1.5
- norm_bias: float32 [1024], replicated, may hold values from -0.5 to 0.5
- final_gain: float32 [1024], replicated, may hold values from 0.5 to 1.5
- final_bias: float32 [1024], replicated, may hold values from -0.5 to 0.5
Outputs:
- layer_out: bfloat16 [16, 1024, 1024], P('fsdp', 'ctx')
- input_grad: float32 [16, 1024, 1024], P('fsdp', 'ctx')
- query_weight_grad: float32 [1024, 1024], P('fsdp', 'tp')
- key_weight_grad: float32 [1024, 1024], P('fsdp', 'tp')
- value_weight_grad: float32 [1024, 1024], P('fsdp', 'tp')
- out_weight_grad: float32 [1024, 1024], P('tp', 'fsdp')
- up_weight_grad: float32 [1024, 4096], P('fsdp', 'tp')
- down_weight_grad: float32 [4096, 1024], P('tp', 'fsdp')
- query_bias_grad: float32 [1024], P('tp')
- value_bias_grad: float32 [1024], P('tp')
- out_bias_grad: float32 [1024], replicated
- up_bias_grad: float32 [4096], P('tp')
- down_bias_grad: float32 [1024], replicated
- norm_gain_grad: float32 [1024], replicated
- norm_bias_grad: float32 [1024], replicated
- final_gain_grad: float32 [1024], replicated
- final_bias_grad: float32 [1024], replicated
Inputs may be any that keep to these rules, and one draw needn't show every extreme that they name: Sequence lengths; some sequence has exactly 256 and some exactly 1024.
All inputs are finite; a program needn't handle non-finite values.
Results may differ from a plain program's by a relative error of at most 0.03.
Values may be sent and summed in bfloat16 or wider, within the bound.
No kernel may reach another device: no remote copies, remote signals or barrier semaphores. Data moves between devices by JAX's collectives and lax.ppermute only.
A program may use at most 256 MiB of HBM per device.

v0:
```python
import jax
import jax.numpy as jnp
from jax import lax
from jax.sharding import PartitionSpec as P

DH = 64


norm_eps = 1e-05
masked_score = -1e30


def from_behind(value, axis, by):
    count = lax.axis_size(axis)
    return lax.ppermute(value, axis, [(i, (i + by) % count) for i in range(count)])


def layer_norm(hidden, gain, offset):
    centred = hidden - jnp.mean(hidden, axis=-1, keepdims=True)
    spread = jnp.mean(centred * centred, axis=-1, keepdims=True)
    return centred * lax.rsqrt(spread + norm_eps) * gain + offset


def gelu_exact(value):
    return jax.nn.gelu(value, approximate=False)


def product(left, right):
    return jnp.dot(left, right, preferred_element_type=jnp.float32)


def product_back(left, right):
    return jnp.einsum("srn,dn->srd", left, right, preferred_element_type=jnp.float32)


def row_product(left, right):
    return jnp.einsum("sra,srb->ab", left, right, preferred_element_type=jnp.float32)


def split_heads(block):
    return block.reshape(block.shape[0], block.shape[1], block.shape[2] // DH, DH)


def join_rows(block):
    return block.reshape(block.shape[0], block.shape[1], block.shape[2] * block.shape[3])


def key_valid(lengths, source, rows):
    places = source * rows + lax.iota(jnp.int32, rows)
    return places[None, :] < lengths[:, None]


def collect(shards):
    return (
        lax.all_gather(shards[0], "fsdp", axis=0, tiled=True),
        lax.all_gather(shards[1], "fsdp", axis=0, tiled=True),
        lax.all_gather(shards[2], "fsdp", axis=0, tiled=True),
        lax.all_gather(shards[3], "fsdp", axis=1, tiled=True),
        lax.all_gather(shards[4], "fsdp", axis=0, tiled=True),
        lax.all_gather(shards[5], "fsdp", axis=1, tiled=True),
    )


def forward(stream, lengths, mats, smalls):
    query_weight, key_weight, value_weight, out_weight, up_weight, down_weight = mats
    (
        query_bias,
        value_bias,
        out_bias,
        up_bias,
        down_bias,
        norm_gain,
        norm_bias,
        final_gain,
        final_bias,
    ) = smalls
    seqs = stream.shape[0]
    rows = stream.shape[1]
    blocks = lax.axis_size("ctx")
    here = lax.axis_index("ctx")
    scale = DH ** (-0.5)
    queries = ((product(stream, query_weight) + query_bias) * scale).astype(jnp.bfloat16)
    keys = product(stream, key_weight).astype(jnp.bfloat16)
    values = (product(stream, value_weight) + value_bias).astype(jnp.bfloat16)
    query_heads = split_heads(queries)
    heads = query_heads.shape[2]
    held = jnp.stack([keys, values])
    run_max = jnp.full((seqs, heads, rows, 1), masked_score, jnp.float32)
    run_total = jnp.zeros((seqs, heads, rows, 1), jnp.float32)
    totals = jnp.zeros((seqs, heads, rows, DH), jnp.float32)
    kept = []
    for step in range(blocks):
        source = (here - step) % blocks
        kept.append((held, source))
        key_heads = split_heads(held[0])
        value_heads = split_heads(held[1])
        scores = jnp.einsum(
            "sqhd,skhd->shqk", query_heads, key_heads, preferred_element_type=jnp.float32
        )
        valid = key_valid(lengths, source, rows)[:, None, None, :]
        scores = jnp.where(valid, scores, masked_score)
        new_max = jnp.maximum(run_max, jnp.max(scores, axis=-1, keepdims=True))
        factor = jnp.exp(run_max - new_max)
        weights = jnp.exp(scores - new_max)
        run_total = run_total * factor + jnp.sum(weights, axis=-1, keepdims=True)
        totals = totals * factor + jnp.einsum(
            "shqk,skhd->shqd",
            weights.astype(jnp.bfloat16),
            value_heads,
            preferred_element_type=jnp.float32,
        )
        run_max = new_max
        if step + 1 < blocks:
            held = from_behind(held, "ctx", 1)
    attended = totals / run_total
    log_total = run_max + jnp.log(run_total)
    merged = join_rows(jnp.transpose(attended, (0, 2, 1, 3))).astype(jnp.bfloat16)
    attn = (
        lax.psum(product(merged, out_weight).astype(jnp.bfloat16), "tp").astype(jnp.float32)
        + out_bias
    )
    first = stream.astype(jnp.float32) + attn
    normed = layer_norm(first, norm_gain, norm_bias)
    normed_low = normed.astype(jnp.bfloat16)
    upper = product(normed_low, up_weight) + up_bias
    activated = gelu_exact(upper).astype(jnp.bfloat16)
    ffn = (
        lax.psum(product(activated, down_weight).astype(jnp.bfloat16), "tp").astype(jnp.float32)
        + down_bias
    )
    second = normed + ffn
    result = layer_norm(second, final_gain, final_bias)
    return {
        "mats": mats,
        "queries": query_heads,
        "kept": kept,
        "attended": attended,
        "log_total": log_total,
        "merged": merged,
        "first": first,
        "normed": normed,
        "normed_low": normed_low,
        "upper": upper,
        "activated": activated,
        "second": second,
        "result": result,
    }


def per_device(
    layer_in,
    lengths,
    out_grad,
    query_weight,
    key_weight,
    value_weight,
    out_weight,
    up_weight,
    down_weight,
    query_bias,
    value_bias,
    out_bias,
    up_bias,
    down_bias,
    norm_gain,
    norm_bias,
    final_gain,
    final_bias,
):
    shards = (query_weight, key_weight, value_weight, out_weight, up_weight, down_weight)
    smalls = (
        query_bias,
        value_bias,
        out_bias,
        up_bias,
        down_bias,
        norm_gain,
        norm_bias,
        final_gain,
        final_bias,
    )
    again = forward(layer_in, lengths, collect(shards), smalls)
    full_query, full_key, full_value, full_out, full_up, full_down = again["mats"]
    seqs = layer_in.shape[0]
    rows = layer_in.shape[1]
    blocks = lax.axis_size("ctx")
    here = lax.axis_index("ctx")
    scale = DH ** (-0.5)
    row_valid = key_valid(lengths, here, rows).astype(jnp.float32)
    cotangent = out_grad.astype(jnp.float32) * row_valid[:, :, None]
    final_fn = jax.vjp(layer_norm, again["second"], final_gain, final_bias)[1]
    d_second, final_gain_grad, final_bias_grad = final_fn(cotangent)
    d_ffn = d_second.astype(jnp.bfloat16)
    down_bias_grad = jnp.sum(d_ffn.astype(jnp.float32), axis=(0, 1))
    down_weight_grad = row_product(again["activated"], d_ffn)
    d_activated = product_back(d_ffn, full_down)
    gelu_fn = jax.vjp(gelu_exact, again["upper"])[1]
    d_upper = gelu_fn(d_activated)[0].astype(jnp.bfloat16)
    up_bias_grad = jnp.sum(d_upper.astype(jnp.float32), axis=(0, 1))
    up_weight_grad = row_product(again["normed_low"], d_upper)
    d_normed = d_second + lax.psum(
        product_back(d_upper, full_up).astype(jnp.bfloat16), "tp"
    ).astype(jnp.float32)
    norm_fn = jax.vjp(layer_norm, again["first"], norm_gain, norm_bias)[1]
    d_first, norm_gain_grad, norm_bias_grad = norm_fn(d_normed)
    d_attn = d_first.astype(jnp.bfloat16)
    out_bias_grad = jnp.sum(d_attn.astype(jnp.float32), axis=(0, 1))
    out_weight_grad = row_product(again["merged"], d_attn)
    d_merged = product_back(d_attn, full_out).astype(jnp.bfloat16)
    d_heads = split_heads(d_merged)
    query_heads = again["queries"]
    heads = query_heads.shape[2]
    delta = jnp.einsum(
        "sqhd,shqd->shq", d_heads, again["attended"], preferred_element_type=jnp.float32
    )[:, :, :, None]
    log_total = again["log_total"]
    query_acc = jnp.zeros((seqs, rows, heads, DH), jnp.float32)
    travel = jnp.zeros((2, seqs, rows, heads * DH), jnp.float32)
    for step in range(blocks):
        held, source = again["kept"][step]
        key_heads = split_heads(held[0])
        value_heads = split_heads(held[1])
        scores = jnp.einsum(
            "sqhd,skhd->shqk", query_heads, key_heads, preferred_element_type=jnp.float32
        )
        valid = key_valid(lengths, source, rows)[:, None, None, :]
        scores = jnp.where(valid, scores, masked_score)
        prob = jnp.exp(scores - log_total)
        d_prob = jnp.einsum(
            "sqhd,skhd->shqk", d_heads, value_heads, preferred_element_type=jnp.float32
        )
        d_scores = (prob * (d_prob - delta)).astype(jnp.bfloat16)
        query_acc = query_acc + jnp.einsum(
            "shqk,skhd->sqhd", d_scores, key_heads, preferred_element_type=jnp.float32
        )
        d_keys = jnp.einsum(
            "shqk,sqhd->skhd", d_scores, query_heads, preferred_element_type=jnp.float32
        )
        d_values = jnp.einsum(
            "shqk,sqhd->skhd",
            prob.astype(jnp.bfloat16),
            d_heads,
            preferred_element_type=jnp.float32,
        )
        travel = travel + jnp.stack([join_rows(d_keys), join_rows(d_values)])
        travel = from_behind(travel.astype(jnp.bfloat16), "ctx", 1).astype(travel.dtype)
    query_grad_low = (join_rows(query_acc) * scale).astype(jnp.bfloat16)
    key_grad_low = travel[0].astype(jnp.bfloat16)
    value_grad_low = travel[1].astype(jnp.bfloat16)
    query_bias_grad = jnp.sum(query_grad_low.astype(jnp.float32), axis=(0, 1))
    value_bias_grad = jnp.sum(value_grad_low.astype(jnp.float32), axis=(0, 1))
    query_weight_grad = row_product(layer_in, query_grad_low)
    key_weight_grad = row_product(layer_in, key_grad_low)
    value_weight_grad = row_product(layer_in, value_grad_low)
    back_terms = product_back(query_grad_low, full_query) + product_back(key_grad_low, full_key)
    back_terms = back_terms + product_back(value_grad_low, full_value)
    input_grad = d_first + lax.psum(back_terms.astype(jnp.bfloat16), "tp").astype(jnp.float32)
    owned = (
        lax.psum_scatter(
            query_weight_grad.astype(jnp.bfloat16), "fsdp", scatter_dimension=0, tiled=True
        ).astype(jnp.float32),
        lax.psum_scatter(
            key_weight_grad.astype(jnp.bfloat16), "fsdp", scatter_dimension=0, tiled=True
        ).astype(jnp.float32),
        lax.psum_scatter(
            value_weight_grad.astype(jnp.bfloat16), "fsdp", scatter_dimension=0, tiled=True
        ).astype(jnp.float32),
        lax.psum_scatter(
            out_weight_grad.astype(jnp.bfloat16), "fsdp", scatter_dimension=1, tiled=True
        ).astype(jnp.float32),
        lax.psum_scatter(
            up_weight_grad.astype(jnp.bfloat16), "fsdp", scatter_dimension=0, tiled=True
        ).astype(jnp.float32),
        lax.psum_scatter(
            down_weight_grad.astype(jnp.bfloat16), "fsdp", scatter_dimension=1, tiled=True
        ).astype(jnp.float32),
    )
    owned = (
        lax.psum(owned[0].astype(jnp.bfloat16), "ctx").astype(jnp.float32),
        lax.psum(owned[1].astype(jnp.bfloat16), "ctx").astype(jnp.float32),
        lax.psum(owned[2].astype(jnp.bfloat16), "ctx").astype(jnp.float32),
        lax.psum(owned[3].astype(jnp.bfloat16), "ctx").astype(jnp.float32),
        lax.psum(owned[4].astype(jnp.bfloat16), "ctx").astype(jnp.float32),
        lax.psum(owned[5].astype(jnp.bfloat16), "ctx").astype(jnp.float32),
    )
    small = lax.psum(
        (
            query_bias_grad,
            value_bias_grad,
            out_bias_grad,
            up_bias_grad,
            down_bias_grad,
            norm_gain_grad,
            norm_bias_grad,
            final_gain_grad,
            final_bias_grad,
        ),
        ("fsdp", "ctx"),
    )
    return (
        again["result"].astype(jnp.bfloat16),
        input_grad,
        owned[0],
        owned[1],
        owned[2],
        owned[3],
        owned[4],
        owned[5],
        small[0],
        small[1],
        small[2],
        small[3],
        small[4],
        small[5],
        small[6],
        small[7],
        small[8],
    )


def solution(mesh):
    in_specs = (
        P("fsdp", "ctx", None),
        P("fsdp"),
        P("fsdp", "ctx", None),
        P("fsdp", "tp"),
        P("fsdp", "tp"),
        P("fsdp", "tp"),
        P("tp", "fsdp"),
        P("fsdp", "tp"),
        P("tp", "fsdp"),
        P("tp"),
        P("tp"),
        P(),
        P("tp"),
        P(),
        P(),
        P(),
        P(),
        P(),
    )
    out_specs = (
        P("fsdp", "ctx", None),
        P("fsdp", "ctx", None),
        P("fsdp", "tp"),
        P("fsdp", "tp"),
        P("fsdp", "tp"),
        P("tp", "fsdp"),
        P("fsdp", "tp"),
        P("tp", "fsdp"),
        P("tp"),
        P("tp"),
        P(),
        P("tp"),
        P(),
        P(),
        P(),
        P(),
        P(),
    )
    return jax.shard_map(
        per_device, mesh=mesh, in_specs=in_specs, out_specs=out_specs, check_vma=False
    )
```

profile of v0, /device:TPU:8, one launch (start us, length us, event | category | flops | bytes accessed | tf_op | source)
XLA Modules:
  0.0 1103.3 jit_solution(6106917210593896654)
XLA Ops:
  12.6 22.5 %all-gather.9.cloned.1.call-done = bf16[1024,512]{0,1:T(8,128)(2,1)} async-done(((bf16[128,512]{0,1:T(8,128)(2,1)}), bf16[1024,512]{0,1:T(8,128)(2,1)}) %all-gather.9.cloned.1.call-update) | async-done | bytes 1048592 | tf_op jit(solution)/shard_map/all_gather | solution.py:56
  38.3 22.8 %all-gather.11.cloned.1.call-done = bf16[1024,512]{0,1:T(8,128)(2,1)} async-done(((bf16[128,512]{0,1:T(8,128)(2,1)}), bf16[1024,512]{0,1:T(8,128)(2,1)}) %all-gather.11.cloned.1.call-update) | async-done | bytes 1048592 | tf_op jit(solution)/shard_map/all_gather | solution.py:57
  68.9 18.2 %all-gather.7.cloned.1.call-done = bf16[1024,512]{0,1:T(8,128)(2,1)} async-done(((bf16[128,512]{0,1:T(8,128)(2,1)}), bf16[1024,512]{0,1:T(8,128)(2,1)}) %all-gather.7.cloned.1.call-update) | async-done | bytes 1048592 | tf_op jit(solution)/shard_map/all_gather | solution.py:55
  89.6 7.5 select_reduce_fusion.1
  97.1 61.9 %collective-permute-done = bf16[2,2,512,512]{2,3,1,0:T(8,128)(2,1)} collective-permute-done((bf16[2,2,512,512]{2,3,1,0:T(8,128)(2,1)}, bf16[2,2,512,512]{2,3,1,0:T(8,128)(2,1)}, u32[]{:S(2)}, u32[]{:S(2)}) %collective-permute-start) | collective-permute-done | bytes 2097184 | tf_op jit(solution)/shard_map/ppermute | solution.py:15
  165.1 15.1 %fusion = (f32[2,8,512]{2,1,0:T(8,128)S(1)}, f32[2,8,512]{2,1,0:T(8,128)S(1)}) fusion(f32[2,8,512,512]{2,3,1,0:T(8,128)} %get-tuple-element.102, f32[2,8,512]{2,1,0:T(8,128)S(1)} %get-tuple-element.97, pred[2,512]{1,0:T(4,128)(4,1)S(1)} %get-tuple-element.100, f32[2,8,512]{2,1,0:T(8,128)S(1)} %get-tuple-element.85, ...), kind=kLoop, calls=%fused_computation.6 | loop fusion | flops 25149440 | bytes 33687552 | tf_op jit(solution)/shard_map/reduce_sum | solution.py:105
  180.2 7.5 fusion.13
  200.8 61.9 %all-reduce.8.cloned.1.call-done = bf16[2,512,1024]{2,1,0:T(8,128)(2,1)} async-done(((bf16[2,512,1024]{2,1,0:T(8,128)(2,1)}), bf16[2,512,1024]{2,1,0:T(8,128)(2,1)}) %all-reduce.8.cloned.1.call-update) | async-done | bytes 2097168 | tf_op jit(solution)/shard_map/psum | solution.py:119
  266.4 35.9 %all-gather.15.cloned.1.call-done = bf16[1024,2048]{1,0:T(8,128)(2,1)} async-done(((bf16[128,2048]{1,0:T(8,128)(2,1)}), bf16[1024,2048]{1,0:T(8,128)(2,1)}) %all-gather.15.cloned.1.call-update) | async-done | bytes 4194320 | tf_op jit(solution)/shard_map/all_gather | solution.py:59
  302.3 10.1 fusion.50
  315.6 20.6 %multiply_convert_fusion.2 = (bf16[2,512,2048]{2,1,0:T(8,128)(2,1)}, f32[2,512,2048]{2,1,0:T(8,128)}) fusion(f32[2,512,2048]{2,1,0:T(8,128)S(1)} %get-tuple-element.107, f32[2048]{0:T(1024)S(1)} %copy-done.33, u8[512,2048]{1,0:T(8,128)(4,1)S(1)} %get-tuple-element.54, u8[512,2048]{1,0:T(8,128)(4,1)S(1)} %get-tuple-element.53), kind=kLoop, calls=%fused_computation.31 | loop fusion | flops 148897792 | bytes 23076864 | tf_op jit(solution)/shard_map/convert_element_type | solution.py:126
  341.5 9.3 fusion.54
  350.9 62.5 %all-reduce.10.cloned.1.call-done = bf16[2,512,1024]{2,1,0:T(8,128)(2,1)} async-done(((bf16[2,512,1024]{2,1,0:T(8,128)(2,1)}), bf16[2,512,1024]{2,1,0:T(8,128)(2,1)}) %all-reduce.10.cloned.1.call-update) | async-done | bytes 2097168 | tf_op jit(solution)/shard_map/psum | solution.py:128
  428.1 11.1 %convert_reduce_fusion = (f32[2048]{0:T(1024)S(1)}, bf16[2,512,2048]{2,1,0:T(8,128)(2,1)}) fusion(f32[2,512,2048]{2,1,0:T(8,128)S(1)} %bitcast.197, bf16[2,512,1024]{2,1,0:T(8,128)(2,1)} %get-tuple-element.75, bf16[2048,1024]{1,0:T(8,128)(2,1)} %all-gather.17.cloned.1.call-done, f32[2,512,2048]{2,1,0:T(8,128)S(1)} %bitcast.195, f32[2048]{0:T(1024)S(1)} %copy-done.33), kind=kOutput, calls=%fused_computation.27 | convolution fusion | flops 4330616832 | bytes 27279360 | tf_op jit(solution)/shard_map/srn,dn->srd/dot_general | solution.py:33
  439.2 9.3 fusion.51
  448.6 63.6 %all-reduce.12.cloned.1.call-done = bf16[2,512,1024]{2,1,0:T(8,128)(2,1)} async-done(((bf16[2,512,1024]{2,1,0:T(8,128)(2,1)}), bf16[2,512,1024]{2,1,0:T(8,128)(2,1)}) %all-reduce.12.cloned.1.call-update) | async-done | bytes 2097168 | tf_op jit(solution)/shard_map/psum | solution.py:201
  526.7 11.0 multiply_convert_fusion.1
  537.7 10.7 multiply_convert_fusion
  564.7 9.4 bitcast_convert_fusion
  574.1 6.5 copy.129
  581.1 10.5 fusion.57
  593.8 7.0 convolution_convert_fusion.1
  608.9 7.5 fusion.94
  619.4 9.0 fusion.7
  631.4 67.4 %collective-permute-done.1 = bf16[2,2,512,512]{3,2,1,0:T(8,128)(2,1)} collective-permute-done((bf16[2,2,512,512]{3,2,1,0:T(8,128)(2,1)}, bf16[2,2,512,512]{3,2,1,0:T(8,128)(2,1)}, u32[]{:S(2)}, u32[]{:S(2)}) %collective-permute-start.1) | collective-permute-done | bytes 2097184 | tf_op jit(solution)/shard_map/ppermute | solution.py:15
  705.8 88.8 %collective-permute-done.2 = bf16[2,2,512,512]{3,2,1,0:T(8,128)(2,1)S(1)} collective-permute-done((bf16[2,2,512,512]{3,2,1,0:T(8,128)(2,1)S(1)}, bf16[2,2,512,512]{3,2,1,0:T(8,128)(2,1)S(1)}, u32[]{:S(2)}, u32[]{:S(2)}) %collective-permute-start.2) | collective-permute-done | bytes 2097184 | tf_op jit(solution)/shard_map/ppermute | solution.py:15
  802.7 9.8 bitcast_convert_fusion.1
  825.8 10.9 reduce-scatter.23.cloned.1.call-done
  838.3 37.9 %reduce-scatter.21.cloned.1.call-done = bf16[128,512]{1,0:T(8,128)(2,1)} async-done(((bf16[1024,512]{1,0:T(8,128)(2,1)}), bf16[128,512]{1,0:T(8,128)(2,1)}) %reduce-scatter.21.cloned.1.call-update) | async-done | bytes 131088
  877.9 53.3 %reduce-scatter.17.cloned.1.call-done = bf16[128,2048]{1,0:T(8,128)(2,1)} async-done(((bf16[1024,2048]{1,0:T(8,128)(2,1)}), bf16[128,2048]{1,0:T(8,128)(2,1)}) %reduce-scatter.17.cloned.1.call-update) | async-done | bytes 524304 | tf_op jit(solution)/shard_map/reduce_scatter | solution.py:271
  931.5 62.6 %all-reduce = (f32[512]{0:T(512)}, f32[512]{0:T(512)}, f32[1024]{0:T(1024)}, f32[2048]{0:T(1024)}, f32[1024]{0:T(1024)}, /*index=5*/f32[1024]{0:T(1024)}, f32[1024]{0:T(1024)}, f32[1024]{0:T(1024)}, f32[1024]{0:T(1024)}) all-reduce(f32[512]{0:T(512)S(1)} %reduce_sum.198, ...), channel_id=1, replica_groups=mesh['fsdp'=8,'ctx'=2,'tp'=2] {'fsdp','ctx'}, use_global_device_ids=true, to_apply=%region_29.30 | all-reduce | flops 9216 | bytes 73728 | tf_op jit(solution)/shard_map/psum | solution.py:286
  1003.1 82.5 %all-reduce.16.cloned.1.call-done = (bf16[128,512]{0,1:T(8,128)(2,1)}, bf16[128,512]{0,1:T(8,128)(2,1)}, bf16[128,512]{0,1:T(8,128)(2,1)}, bf16[512,128]{1,0:T(8...) async-done(((bf16[128,512]{0,1:T(8,128)(2,1)}, bf16[128,512]{0,1:T(8,128)(2,1)}, bf16[128,512]{0,1:T(8,128)(2,1)}, bf16[512,128]{1,0:T(8,128)(2,1)}, ...) | async-done | bytes 1572880 | tf_op jit(solution)/shard_map/psum | solution.py:279
  (205 shorter events, 163.8 us)
Async XLA Ops:
  7.2 53.9 %copy-start.1 = (bf16[2,512,1024]{2,1,0:T(8,128)(2,1)S(1)}, bf16[2,512,1024]{2,1,0:T(8,128)(2,1)}, u32[]{:S(2)}) copy-start(bf16[2,512,1024]{2,1,0:T(8,128)(2,1)} %param.18) | copy-start | bytes 6291460
  7.2 53.9 %copy-start.38 = (f32[512]{0:T(512)S(1)}, f32[512]{0:T(512)}, u32[]{:S(2)}) copy-start(f32[512]{0:T(512)} %param.28) | copy-start | bytes 6148
  7.2 27.9 %all-gather.9.cloned.1.call-start = ((), (), s32[]{:S(2)}) async-start(), calls=%async_computation.7 | async-start | bytes 1179648 | tf_op jit(solution)/shard_map/all_gather | solution.py:56
  9.1 52.0 %all-gather.11.cloned.1.call-start = ((), (), s32[]{:S(2)}) async-start(), calls=%async_computation.8 | async-start | bytes 1179648 | tf_op jit(solution)/shard_map/all_gather | solution.py:57
  10.8 76.3 %all-gather.7.cloned.1.call-start = ((), (), s32[]{:S(2)}) async-start(), calls=%async_computation.6 | async-start | bytes 1179648 | tf_op jit(solution)/shard_map/all_gather | solution.py:55
  12.6 182.5 %all-gather.13.cloned.1.call-start = ((), (), s32[]{:S(2)}) async-start(), calls=%async_computation.9 | async-start | bytes 1179648 | tf_op jit(solution)/shard_map/all_gather | solution.py:58
  38.3 30.5 %copy-start.37 = (s32[2]{0:T(128)S(1)}, s32[2]{0:T(128)}, u32[]{:S(2)}) copy-start(s32[2]{0:T(128)} %param.19) | copy-start | bytes 28
  38.3 48.8 %copy-start.39 = (f32[512]{0:T(512)S(1)}, f32[512]{0:T(512)}, u32[]{:S(2)}) copy-start(f32[512]{0:T(512)} %param.27) | copy-start | bytes 6148
  66.1 92.9 %collective-permute-start = (bf16[2,2,512,512]{2,3,1,0:T(8,128)(2,1)}, bf16[2,2,512,512]{2,3,1,0:T(8,128)(2,1)}, u32[]{:S(2)}, u32[]{:S(2)}) collective-permute-start(bf16[2,2,512,512]{2,3,1,0:T(8,128)(2,1)} %pad_maximum_fusion), channel_id=1, source_target_pairs={{0,2},{2,0},{1,3},{3,1},{4,6},{6,4},{5,7},{7,5},{8,10},{10,8},{9,1... | collective-permute-start | bytes 6291464 | tf_op jit(solution)/shard_map/ppermute | solution.py:15
  68.5 194.2 %all-reduce.8.cloned.1.call-start = ((), (), s32[]{:S(2)}) async-start(), calls=%async_computation.10 | async-start | bytes 4194304 | tf_op jit(solution)/shard_map/psum | solution.py:119
  89.6 72.1 %copy-start.7 = (bf16[2,512,512]{1,2,0:T(8,128)(2,1)}, bf16[2,512,512]{1,2,0:T(8,128)(2,1)S(1)}, u32[]{:S(2)}) copy-start(bf16[2,512,512]{1,2,0:T(8,128)(2,1)S(1)} %multiply_convert_fusion.4) | copy-start | bytes 3145732
  165.0 22.7 %copy-start = (f32[2,8,512,512]{2,3,1,0:T(8,128)}, f32[2,8,512,512]{2,3,1,0:T(8,128)S(1)}, u32[]{:S(2)}) copy-start(f32[2,8,512,512]{2,3,1,0:T(8,128)S(1)} %get-tuple-element.104) | copy-start | bytes 50331652
  165.1 15.1 %copy-start.19 = (bf16[2,512,512]{1,2,0:T(8,128)(2,1)S(1)}, bf16[2,512,512]{1,2,0:T(8,128)(2,1)}, u32[]{:S(2)}) copy-start(bf16[2,512,512]{1,2,0:T(8,128)(2,1)} %copy-done.18) | copy-start | bytes 3145732
  195.0 67.7 %copy-start.30 = (f32[1024]{0:T(1024)S(1)}, f32[1024]{0:T(1024)}, u32[]{:S(2)}) copy-start(f32[1024]{0:T(1024)} %param.29) | copy-start | bytes 12292
  199.2 103.0 %all-gather.15.cloned.1.call-start = ((), (), s32[]{:S(2)}) async-start(), calls=%async_computation.11 | async-start | bytes 4718592 | tf_op jit(solution)/shard_map/all_gather | solution.py:59
  199.8 141.7 %all-gather.17.cloned.1.call-start = ((), (), s32[]{:S(2)}) async-start(), calls=%async_computation.12 | async-start | bytes 4718592 | tf_op jit(solution)/shard_map/all_gather | solution.py:60
  200.5 101.7 %copy-start.31 = (f32[1024]{0:T(1024)S(1)}, f32[1024]{0:T(1024)}, u32[]{:S(2)}) copy-start(f32[1024]{0:T(1024)} %param.32) | copy-start | bytes 12292
  200.6 101.7 %copy-start.33 = (f32[2048]{0:T(1024)S(1)}, f32[2048]{0:T(1024)}, u32[]{:S(2)}) copy-start(f32[2048]{0:T(1024)} %param.30) | copy-start | bytes 24580
  200.6 101.7 %copy-start.36 = (f32[1024]{0:T(1024)S(1)}, f32[1024]{0:T(1024)}, u32[]{:S(2)}) copy-start(f32[1024]{0:T(1024)} %param.33) | copy-start | bytes 12292
  200.6 212.8 %all-reduce.10.cloned.1.call-start = ((), (), s32[]{:S(2)}) async-start(), calls=%async_computation.13 | async-start | bytes 4194304 | tf_op jit(solution)/shard_map/psum | solution.py:128
  341.5 71.9 %copy-start.35 = (f32[1024]{0:T(1024)S(1)}, f32[1024]{0:T(1024)}, u32[]{:S(2)}) copy-start(f32[1024]{0:T(1024)} %param.31) | copy-start | bytes 12292
  350.8 161.4 %all-reduce.12.cloned.1.call-start = ((), (), s32[]{:S(2)}) async-start(), calls=%async_computation.14 | async-start | bytes 4194304 | tf_op jit(solution)/shard_map/psum | solution.py:201
  448.5 371.9 %reduce-scatter.25.cloned.1.call-start = ((), (), s32[]{:S(2)}) async-start(), calls=%async_computation.20 | async-start | bytes 1179648
  550.6 271.5 %reduce-scatter.19.cloned.1.call-start = ((), (), s32[]{:S(2)}) async-start(), calls=%async_computation.17 | async-start | bytes 1179648
  564.6 259.1 %reduce-scatter.27.cloned.1.call-start = ((), (), s32[]{:S(2)}) async-start(), calls=%async_computation.21 | async-start | bytes 4718592
  580.6 256.1 %reduce-scatter.23.cloned.1.call-start = ((), (), s32[]{:S(2)}) async-start(), calls=%async_computation.19 | async-start | bytes 1179648
  606.3 92.5 %collective-permute-start.1 = (bf16[2,2,512,512]{3,2,1,0:T(8,128)(2,1)}, bf16[2,2,512,512]{3,2,1,0:T(8,128)(2,1)}, u32[]{:S(2)}, u32[]{:S(2)}) collective-permute-start(bf16[2,2,512,512]{3,2,1,0:T(8,128)(2,1)} %pad_maximum_fusion.1), channel_id=1, source_target_pairs={{0,2},{2,0},{1,3},{3,1},{4,6},{6,4},{5,7},{7,5},{8,10},{10,8},{9,1... | collective-permute-start | bytes 6291464 | tf_op jit(solution)/shard_map/ppermute | solution.py:15
  702.4 92.2 %collective-permute-start.2 = (bf16[2,2,512,512]{3,2,1,0:T(8,128)(2,1)S(1)}, bf16[2,2,512,512]{3,2,1,0:T(8,128)(2,1)S(1)}, u32[]{:S(2)}, u32[]{:S(2)}) collective-permute-start(bf16[2,2,512,512]{3,2,1,0:T(8,128)(2,1)S(1)} %fusion.32), channel_id=1, source_target_pairs={{0,2},{2,0},{1,3},{3,1},{4,6},{6,4},{5,7},{7,5},{8,10},{10,8},{9,1... | collective-permute-start | bytes 6291464 | tf_op jit(solution)/shard_map/ppermute | solution.py:15
  798.6 77.7 %reduce-scatter.21.cloned.1.call-start = ((), (), s32[]{:S(2)}) async-start(), calls=%async_computation.18 | async-start | bytes 1179648
  802.5 128.7 %reduce-scatter.17.cloned.1.call-start = ((), (), s32[]{:S(2)}) async-start(), calls=%async_computation.16 | async-start | bytes 4718592 | tf_op jit(solution)/shard_map/reduce_scatter | solution.py:271
  812.6 185.2 %all-reduce.14.cloned.1.call-start = ((), (), s32[]{:S(2)}) async-start(), calls=%async_computation.15 | async-start | bytes 4194304 | tf_op jit(solution)/shard_map/psum | solution.py:257
  820.3 265.4 %all-reduce.16.cloned.1.call-start = ((), (), s32[]{:S(2)}) async-start(), calls=%async_computation.22 | async-start | bytes 3145728 | tf_op jit(solution)/shard_map/psum | solution.py:279
  (33 other events, 140.8 us)
Sparse Core Ops, SparseCore 0:
  10.5 24.6 all-gather.8
  37.6 23.4 all-gather.10
  63.6 23.5 all-gather.6
  88.8 23.4 all-gather.12
  199.3 63.3 all-reduce.7
  264.5 37.7 all-gather.14
  304.1 37.3 all-gather.16
  350.9 62.3 all-reduce.9
  448.6 63.5 all-reduce.11
  550.8 37.1 reduce-scatter.24
  591.1 35.9 reduce-scatter.18
  630.3 51.1 reduce-scatter.26
  798.7 37.9 reduce-scatter.22
  840.3 35.9 reduce-scatter.20
  880.1 51.1 reduce-scatter.16
  933.4 64.3 all-reduce.13
  1001.0 84.6 all-reduce.15
where the time goes:
time: 1110 us; the launch traced here: 1100 us
  waiting for transfers between devices  701 us (63%)
  matrix products  177 us (16%)
  other arithmetic  78.4 us (7%)
  blocking collectives  62.6 us (6%)
  local copies, waits for them, and re-layouts  59.8 us (5%)
  between operations  14.8 us (1%)
    ppermute x3, waiting for transfers between devices, from_behind(): lax.ppermute(value, axis, [(i, (i + by) % count) for i in range(count)])  218 us
    psum x1, waiting for transfers between devices, per_device(): lax.psum(owned[0].astype(jnp.bfloat16), 'ctx').astype(jnp.float32)  82.5 us
    psum x1, waiting for transfers between devices, per_device(): lax.psum(product_back(d_upper, full_up).astype(jnp.bfloat16), 'tp')  63.6 us
    psum x1, blocking collectives, per_device(): lax.psum((query_bias_grad, value_bias_grad, out_bias_grad, up_bias_grad,...  62.6 us
    psum x1, waiting for transfers between devices, forward(): lax.psum(product(activated, down_weight).astype(jnp.bfloat16), 'tp')  62.5 us
    psum x1, waiting for transfers between devices, forward(): lax.psum(product(merged, out_weight).astype(jnp.bfloat16), 'tp')  61.9 us
    reduce_scatter x1, waiting for transfers between devices, per_device(): lax.psum_scatter(up_weight_grad.astype(jnp.bfloat16), 'fsdp', scatter_dim...  53.3 us
    unnamed x22, waiting for transfers between devices  50.3 us
  transfers between devices with their start and end apart: 20, of which 16 were waited for; matrix products, arithmetic and copies ran while one was open for 19% of the time, Pallas kernels for 0%

commit v1 on v0

v1 whole, which is shorter than its diff:
```python
import functools

import jax
import jax.numpy as jnp
from jax import lax
from jax.experimental import pallas as pl
from jax.experimental.pallas import tpu as pltpu
from jax.sharding import PartitionSpec as P

DH = 64
PAIR = 2 * DH
ROWS = 256

norm_eps = 1e-05
masked_score = -1e30
BF16 = jnp.bfloat16
F32 = jnp.float32
AXES = ("fsdp", "ctx", "tp")


def send(value, target):
    fsdp, ctx, tp = (lax.axis_size(axis) for axis in AXES)
    pairs = []
    for f in range(fsdp):
        for h in range(ctx):
            for t in range(tp):
                plane, core, high, low = target(f // 2, f % 2, h, t)
                pairs.append(((f * ctx + h) * tp + t, ((2 * plane + core) * ctx + high) * tp + low))
    return lax.ppermute(value, AXES, pairs)


def to_core(value):
    return send(value, lambda p, c, h, t: (p, 1 - c, h, t))


def to_x(value):
    return send(value, lambda p, c, h, t: (p ^ 1, c, h, t))


def to_y(value):
    return send(value, lambda p, c, h, t: (p ^ 2, c, h, t))


def to_high(value):
    return send(value, lambda p, c, h, t: (p, c, 1 - h, t))


def to_low(value):
    return send(value, lambda p, c, h, t: (p, c, h, 1 - t))


def to_turned(value):
    return send(value, lambda p, c, h, t: (p, h, c, t))


def to_first(value):
    return send(value, lambda p, c, h, t: (p, t, h, c))


def to_second(value):
    return send(value, lambda p, c, h, t: (p, t, h, 1 - c))


def from_second(value):
    return send(value, lambda p, c, h, t: (p, 1 - t, h, c))


def plane_groups():
    fsdp = lax.axis_size("fsdp")
    return [[2 * p + c for p in range(fsdp // 2)] for c in range(2)]


def gather_rows(shard):
    first = to_first(shard)
    second = to_second(shard)
    unit = jnp.concatenate([first, second], axis=0)
    planes = lax.axis_size("fsdp") // 2
    if planes != 4:
        return lax.all_gather(unit, "fsdp", axis=0, tiled=True, axis_index_groups=plane_groups())
    half = shard.shape[0]
    over_x = to_x(unit)
    over_y = to_y(unit)
    far_first = to_y(over_x[:half])
    far_second = to_x(over_y[half:])
    return jnp.concatenate([unit, over_x, over_y, far_first, far_second], axis=0)


def scatter_rows(rows_of, half):
    planes = lax.axis_size("fsdp") // 2
    if planes != 4:
        whole = rows_of(0, 2 * planes * half)
        mine = lax.psum_scatter(
            whole, "fsdp", scatter_dimension=0, tiled=True, axis_index_groups=plane_groups()
        )
    else:
        far_first = to_y(rows_of(6 * half, 7 * half))
        far_second = to_x(rows_of(7 * half, 8 * half))
        over_x = rows_of(2 * half, 4 * half)
        over_y = rows_of(4 * half, 6 * half)
        over_x = jnp.concatenate([added(over_x[:half], far_first), over_x[half:]], axis=0)
        over_y = jnp.concatenate([over_y[:half], added(over_y[half:], far_second)], axis=0)
        over_x = to_x(over_x)
        over_y = to_y(over_y)
        mine = rows_of(0, 2 * half).astype(F32) + over_x.astype(F32) + over_y.astype(F32)
        mine = mine.astype(BF16)
    first = to_first(mine[:half])
    second = from_second(mine[half:])
    return added(first, second)


def added(one, other):
    return (one.astype(F32) + other.astype(F32)).astype(BF16)


def summed_high(part):
    return part.astype(F32) + to_high(part).astype(F32)


def summed_all(vector):
    fsdp = lax.axis_size("fsdp")
    if fsdp != 8:
        return lax.psum(vector, AXES)
    for step in (to_core, to_x, to_y, to_low, to_high):
        vector = vector + step(vector)
    return vector


def turned_columns(value, key, width):
    lead = value.shape[:-1]
    blocks = value.shape[-1] // width
    value = value.reshape(lead + (blocks, width))
    bit = 1
    while bit < blocks:
        swapped = value.reshape(lead + (blocks // (2 * bit), 2, bit, width))
        swapped = swapped[..., ::-1, :, :].reshape(value.shape)
        value = jnp.where((key & bit) != 0, swapped, value)
        bit *= 2
    return value.reshape(lead + (blocks * width,))


def product(left, right, out=F32):
    return jnp.dot(left, right, preferred_element_type=F32).astype(out)


def product_back(left, right, out=F32):
    return lax.dot_general(
        left, right, (((1,), (1,)), ((), ())), preferred_element_type=F32
    ).astype(out)


def row_product(left, right, out=BF16):
    return lax.dot_general(
        left, right, (((0,), (0,)), ((), ())), preferred_element_type=F32
    ).astype(out)


def attend_kernel(qkv_ref, bias_ref, out_ref, log_ref):
    rows = qkv_ref.shape[0]
    low = lax.broadcasted_iota(jnp.int32, (1, PAIR), 1) < DH
    keys = qkv_ref[:, PAIR : 2 * PAIR]
    values = qkv_ref[:, 2 * PAIR :]
    bias = bias_ref[...]
    zero = jnp.zeros((), BF16)
    picks = (low, jnp.logical_not(low))
    head_values = [jnp.where(pick, values, zero) for pick in picks]
    for tile in range(rows // ROWS):
        at = slice(tile * ROWS, (tile + 1) * ROWS)
        query = qkv_ref[at, :PAIR]
        out = jnp.zeros((ROWS, PAIR), F32)
        logs = jnp.zeros((ROWS, PAIR), F32)
        for head in range(2):
            mine = jnp.where(picks[head], query, zero)
            scores = product_back(mine, keys) + bias
            top = jnp.max(scores, axis=1, keepdims=True)
            weights = jnp.exp(scores - top)
            total = jnp.sum(weights, axis=1, keepdims=True)
            out = out + product(weights.astype(BF16), head_values[head]) / total
            logs = jnp.where(picks[head], top + jnp.log(total), logs)
        out_ref[at, :] = out.astype(BF16)
        log_ref[at, :] = logs


def attend(qkv, bias):
    rows = qkv.shape[0]
    pairs = qkv.shape[1] // (3 * PAIR)
    flops = 2 * 2 * 2 * pairs * rows * rows * DH
    return pl.pallas_call(
        attend_kernel,
        grid=(pairs,),
        in_specs=[
            pl.BlockSpec((rows, 3 * PAIR), lambda i: (0, i)),
            pl.BlockSpec((1, rows), lambda i: (0, 0)),
        ],
        out_specs=[
            pl.BlockSpec((rows, PAIR), lambda i: (0, i)),
            pl.BlockSpec((rows, PAIR), lambda i: (0, i)),
        ],
        out_shape=[
            jax.ShapeDtypeStruct((rows, pairs * PAIR), BF16),
            jax.ShapeDtypeStruct((rows, pairs * PAIR), F32),
        ],
        cost_estimate=pl.CostEstimate(
            flops=4 * flops, bytes_accessed=8 * rows * pairs * PAIR * 2,
            transcendentals=2 * pairs * rows * rows,
        ),
        name="attend",
    )(qkv, bias)


def attend_back_kernel(qkv_ref, bias_ref, out_ref, log_ref, grad_ref, result_ref, key_acc, value_acc):
    rows = qkv_ref.shape[0]
    low = lax.broadcasted_iota(jnp.int32, (1, PAIR), 1) < DH
    keys = qkv_ref[:, PAIR : 2 * PAIR]
    values = qkv_ref[:, 2 * PAIR :]
    bias = bias_ref[...]
    zero = jnp.zeros((), BF16)
    picks = (low, jnp.logical_not(low))
    head_keys = [jnp.where(pick, keys, zero) for pick in picks]
    for tile in range(rows // ROWS):
        at = slice(tile * ROWS, (tile + 1) * ROWS)
        query = qkv_ref[at, :PAIR]
        grad = grad_ref[at, :]
        both = grad.astype(F32) * out_ref[at, :].astype(F32)
        query_grad = jnp.zeros((ROWS, PAIR), F32)
        key_grad = jnp.zeros((rows, PAIR), F32)
        value_grad = jnp.zeros((rows, PAIR), F32)
        for head in range(2):
            pick = picks[head]
            mine = jnp.where(pick, query, zero)
            mine_grad = jnp.where(pick, grad, zero)
            delta = jnp.sum(jnp.where(pick, both, 0.0), axis=1, keepdims=True)
            logs = log_ref[at, head * DH : head * DH + 1]
            prob = jnp.exp(product_back(mine, keys) + bias - logs)
            d_prob = product_back(mine_grad, values)
            d_scores = (prob * (d_prob - delta)).astype(BF16)
            query_grad = query_grad + product(d_scores, head_keys[head])
            key_grad = key_grad + row_product(d_scores, mine, F32)
            value_grad = value_grad + row_product(prob.astype(BF16), mine_grad, F32)
        result_ref[at, :PAIR] = (query_grad * DH**-0.5).astype(BF16)
        if tile == 0:
            key_acc[...] = key_grad
            value_acc[...] = value_grad
        else:
            key_acc[...] += key_grad
            value_acc[...] += value_grad
    result_ref[:, PAIR : 2 * PAIR] = key_acc[...].astype(BF16)
    result_ref[:, 2 * PAIR :] = value_acc[...].astype(BF16)


def attend_back(qkv, bias, out, logs, grad):
    rows = qkv.shape[0]
    pairs = qkv.shape[1] // (3 * PAIR)
    flops = 2 * 5 * 2 * pairs * rows * rows * DH
    wide = pl.BlockSpec((rows, 3 * PAIR), lambda i: (0, i))
    narrow = pl.BlockSpec((rows, PAIR), lambda i: (0, i))
    return pl.pallas_call(
        attend_back_kernel,
        grid=(pairs,),
        in_specs=[wide, pl.BlockSpec((1, rows), lambda i: (0, 0)), narrow, narrow, narrow],
        out_specs=wide,
        out_shape=jax.ShapeDtypeStruct(qkv.shape, BF16),
        scratch_shapes=[pltpu.VMEM((rows, PAIR), F32)] * 2,
        cost_estimate=pl.CostEstimate(
            flops=4 * flops, bytes_accessed=12 * rows * pairs * PAIR * 2,
            transcendentals=2 * pairs * rows * rows,
        ),
        name="attend_back",
    )(qkv, bias, out, logs, grad)


def normed_of(hidden):
    centred = hidden - jnp.mean(hidden, axis=-1, keepdims=True)
    spread = jnp.mean(centred * centred, axis=-1, keepdims=True)
    scale = lax.rsqrt(spread + norm_eps)
    return centred * scale, scale


def norm_back(grad, gain, unit, scale):
    inner = grad * gain
    return scale * (
        inner
        - jnp.mean(inner, axis=-1, keepdims=True)
        - unit * jnp.mean(inner * unit, axis=-1, keepdims=True)
    )


def weave(parts):
    lead = parts[0].shape[0]
    parts = [part.reshape(lead, -1, PAIR) for part in parts]
    return jnp.stack(parts, axis=2).reshape(lead, -1)


def unweave(woven):
    lead = woven.shape[0]
    woven = woven.reshape(lead, -1, 3, PAIR)
    return [woven[:, :, part].reshape(lead, -1) for part in range(3)]


def per_device(
    layer_in,
    lengths,
    out_grad,
    query_weight,
    key_weight,
    value_weight,
    out_weight,
    up_weight,
    down_weight,
    query_bias,
    value_bias,
    out_bias,
    up_bias,
    down_bias,
    norm_gain,
    norm_bias,
    final_gain,
    final_bias,
):
    fsdp = lax.axis_index("fsdp")
    plane, core = fsdp // 2, fsdp % 2
    high, low = lax.axis_index("ctx"), lax.axis_index("tp")
    planes = lax.axis_size("fsdp") // 2
    half = query_weight.shape[0]
    rows = layer_in.shape[1]
    width = layer_in.shape[2]
    heads_width = query_weight.shape[1]
    hidden = up_weight.shape[1]
    key = 2 * plane + low if planes == 4 else low
    order = functools.partial(turned_columns, key=key, width=half)

    qkv_shard = weave([query_weight, key_weight, value_weight])
    qkv_weight = gather_rows(qkv_shard)
    mine_in = order(lax.dynamic_index_in_dim(layer_in, low, 0, keepdims=False))
    own = to_turned(mine_in)
    other = to_core(own)
    x = jnp.concatenate([own, other], axis=0)
    vectors = to_first(jnp.concatenate([query_bias, value_bias, up_bias]))
    lengths_other = to_core(lengths)
    length = jnp.where(core == high, lengths, lengths_other)
    length = lax.dynamic_index_in_dim(length, low, 0, keepdims=False)
    out_up = gather_rows(jnp.concatenate([out_weight.T, up_weight], axis=1))
    out_t = out_up[:, :heads_width]
    up = out_up[:, heads_width:]
    down_t = gather_rows(down_weight.T)
    mine_grad = order(lax.dynamic_index_in_dim(out_grad, low, 0, keepdims=False))
    own_grad = to_turned(mine_grad)

    out_b, down_b, gain1, bias1, gain2, bias2 = order(
        jnp.stack([out_bias, down_bias, norm_gain, norm_bias, final_gain, final_bias])
    )
    query_b = vectors[:heads_width]
    value_b = vectors[heads_width : 2 * heads_width]
    up_b = vectors[2 * heads_width :]
    qkv_b = weave([query_b[None], jnp.zeros_like(query_b)[None], value_b[None]])
    scales = weave(
        [
            jnp.full((1, heads_width), DH**-0.5, F32),
            jnp.ones((1, heads_width), F32),
            jnp.ones((1, heads_width), F32),
        ]
    )
    places = lax.iota(jnp.int32, rows)
    own_places = core * rows + places
    other_places = (1 - core) * rows + places
    valid = jnp.concatenate([own_places, other_places]) < length
    bias = jnp.where(valid, 0.0, masked_score).astype(F32)[None, :]
    row_valid = (own_places < length).astype(F32)[:, None]

    qkv = ((product(x, qkv_weight) + qkv_b) * scales).astype(BF16)
    merged, logs = attend(qkv, bias)
    attn = product_back(merged, out_t)
    first = own.astype(F32) + attn[:rows] + to_core(attn[rows:].astype(BF16)).astype(F32) + out_b
    unit1, scale1 = normed_of(first)
    normed = unit1 * gain1 + bias1
    normed_own = normed.astype(BF16)
    normed_low = jnp.concatenate([normed_own, to_core(normed_own)], axis=0)
    upper = product(normed_low, up) + up_b
    cdf = 0.5 * lax.erfc(upper * -(0.5**0.5))
    activated = (upper * cdf).astype(BF16)
    slope = (cdf + upper * jnp.exp(-0.5 * upper * upper) * (2 * jnp.pi) ** -0.5).astype(BF16)
    ffn = product_back(activated, down_t)
    second = normed + ffn[:rows] + to_core(ffn[rows:].astype(BF16)).astype(F32) + down_b
    unit2, scale2 = normed_of(second)
    result = order((unit2 * gain2 + bias2).astype(BF16))
    result = to_turned(result)
    result_pair = to_low(result)
    layer_out = jnp.where(
        low == 0, jnp.stack([result, result_pair]), jnp.stack([result_pair, result])
    )

    cot = own_grad.astype(F32) * row_valid
    final_gain_grad = jnp.sum(cot * unit2, axis=0)
    final_bias_grad = jnp.sum(cot, axis=0)
    d_second = norm_back(cot, gain2, unit2, scale2)
    d_ffn_own = d_second.astype(BF16)
    down_bias_grad = jnp.sum(d_ffn_own.astype(F32), axis=0)
    d_ffn = jnp.concatenate([d_ffn_own, to_core(d_ffn_own)], axis=0)
    down_part = scatter_rows(lambda a, b: row_product(d_ffn[:, a:b], activated), half)
    d_upper = (product(d_ffn, down_t) * slope.astype(F32)).astype(BF16)
    up_bias_grad = jnp.sum(d_upper.astype(F32), axis=0)
    up_part = scatter_rows(lambda a, b: row_product(normed_low[:, a:b], d_upper), half)
    back = product_back(d_upper, up)
    d_normed = d_second + back[:rows] + to_core(back[rows:].astype(BF16)).astype(F32)
    norm_gain_grad = jnp.sum(d_normed * unit1, axis=0)
    norm_bias_grad = jnp.sum(d_normed, axis=0)
    d_first = norm_back(d_normed, gain1, unit1, scale1)
    d_attn_own = d_first.astype(BF16)
    out_bias_grad = jnp.sum(d_attn_own.astype(F32), axis=0)
    d_attn = jnp.concatenate([d_attn_own, to_core(d_attn_own)], axis=0)
    d_merged = product(d_attn, out_t, BF16)
    out_part = scatter_rows(lambda a, b: row_product(d_attn[:, a:b], merged), half)
    d_qkv = attend_back(qkv, bias, merged, logs, d_merged)
    qkv_bias_grad = jnp.sum(d_qkv.astype(F32), axis=0, keepdims=True)
    query_bias_grad, _, value_bias_grad = (part[0] for part in unweave(qkv_bias_grad))
    qkv_part = scatter_rows(lambda a, b: row_product(x[:, a:b], d_qkv), half)
    back = product_back(d_qkv, qkv_weight)
    total = d_first + back[:rows] + to_core(back[rows:].astype(BF16)).astype(F32)
    total = to_turned(order(total.astype(BF16)))
    total_pair = to_low(total)
    input_grad = jnp.where(
        low == 0, jnp.stack([total, total_pair]), jnp.stack([total_pair, total])
    ).astype(F32)

    down_grad = summed_high(down_part).T
    up_grad = summed_high(up_part)
    out_weight_grad = summed_high(out_part).T
    query_grad, key_grad, value_grad = unweave(summed_high(qkv_part))

    def spread(vector):
        empty = jnp.zeros_like(vector)
        return jnp.where(
            core == 0, jnp.concatenate([vector, empty]), jnp.concatenate([empty, vector])
        )

    features = order(
        jnp.stack(
            [
                out_bias_grad,
                down_bias_grad,
                norm_gain_grad,
                norm_bias_grad,
                final_gain_grad,
                final_bias_grad,
            ]
        )
    ).reshape(-1)
    small = summed_all(
        jnp.concatenate(
            [features, spread(query_bias_grad), spread(value_bias_grad), spread(up_bias_grad)]
        )
    )
    features = small[: 6 * width].reshape(6, width)
    at = 6 * width

    def mine(start, size):
        return lax.dynamic_slice(small, (start + low * size,), (size,))

    query_bias_grad = mine(at, heads_width)
    value_bias_grad = mine(at + 2 * heads_width, heads_width)
    up_bias_grad = mine(at + 4 * heads_width, hidden)
    return (
        layer_out,
        input_grad,
        query_grad,
        key_grad,
        value_grad,
        out_weight_grad,
        up_grad,
        down_grad,
        query_bias_grad,
        value_bias_grad,
        features[0],
        up_bias_grad,
        features[1],
        features[2],
        features[3],
        features[4],
        features[5],
    )


def solution(mesh):
    in_specs = (
        P("fsdp", "ctx", None),
        P("fsdp"),
        P("fsdp", "ctx", None),
        P("fsdp", "tp"),
        P("fsdp", "tp"),
        P("fsdp", "tp"),
        P("tp", "fsdp"),
        P("fsdp", "tp"),
        P("tp", "fsdp"),
        P("tp"),
        P("tp"),
        P(),
        P("tp"),
        P(),
        P(),
        P(),
        P(),
        P(),
    )
    out_specs = (
        P("fsdp", "ctx", None),
        P("fsdp", "ctx", None),
        P("fsdp", "tp"),
        P("fsdp", "tp"),
        P("fsdp", "tp"),
        P("tp", "fsdp"),
        P("fsdp", "tp"),
        P("tp", "fsdp"),
        P("tp"),
        P("tp"),
        P(),
        P("tp"),
        P(),
        P(),
        P(),
        P(),
        P(),
    )
    return jax.shard_map(
        per_device, mesh=mesh, in_specs=in_specs, out_specs=out_specs, check_vma=False
    )
```

time: 1110 us -> 625 us (0.56)
  waiting for transfers between devices: 701 us -> 152 us
  starting transfers between devices: 10.4 us -> 128 us
  matrix products: 177 us -> 105 us
  blocking collectives: 62.6 us -> 0 us
  local copies, waits for them, and re-layouts: 59.8 us -> 110 us
  Pallas kernels: 0 us -> 45.1 us
  between operations: 14.8 us -> 2.75 us
    psum x5 -> x0, waiting for transfers between devices: 274 us -> none  [the longest x1 82.5 us: per_device(): lax.psum(owned[0].astype(jnp.bfloat16), 'ctx').astype(jnp.float32)]
    ppermute x3 -> x67, starting transfers between devices: 8.51 us -> 128 us  [send(): return lax.ppermute(value, AXES, pairs)]
    all_gather x6 -> x0, waiting for transfers between devices: 105 us -> none  [the longest x1 35.9 us: collect(): lax.all_gather(shards[4], 'fsdp', axis=0, tiled=True)]
    dot_general x30 -> x28, matrix products: 177 us -> 105 us  [the longest x4 45.9 us: product(): return jnp.dot(left, right, preferred_element_type=F32).astype(out)]
    ppermute x3 -> x67, waiting for transfers between devices: 218 us -> 152 us  [send(): return lax.ppermute(value, AXES, pairs)]
    psum x1 -> x0, blocking collectives: 62.6 us -> none  [per_device(): lax.psum((query_bias_grad, value_bias_grad, out_bias_grad, up_bias_grad,...]
    reduce_scatter x1 -> x0, waiting for transfers between devices: 53.3 us -> none  [per_device(): lax.psum_scatter(up_weight_grad.astype(jnp.bfloat16), 'fsdp', scatter_dim...]
    unnamed x22 -> x0, waiting for transfers between devices: 50.3 us -> none
  transfers between devices with their start and end apart: 20 -> 67, of which waited for: 16 -> 21; matrix products, arithmetic and copies ran while one was open for 19% -> 35% of each run, Pallas kernels for 0% -> 7%
where the time goes in v1:
time: 625 us; the launch traced here: 615 us
  waiting for transfers between devices  152 us (24%)
  starting transfers between devices  128 us (20%)
  local copies, waits for them, and re-layouts  110 us (18%)
  matrix products  105 us (17%)
  other arithmetic  72.7 us (12%)
  Pallas kernels  45.1 us (7%)
    ppermute x67, waiting for transfers between devices, send(): return lax.ppermute(value, AXES, pairs)  152 us
    ppermute x67, starting transfers between devices, send(): return lax.ppermute(value, AXES, pairs)  128 us
    unnamed x182, local copies, waits for them, and re-layouts  54.6 us
    dot_general x4, matrix products, product(): return jnp.dot(left, right, preferred_element_type=F32).astype(out)  45.9 us
    dot_general x20, matrix products, row_product(): lax.dot_general(left, right, (((0,), (0,)), ((), ())), preferred_element_...  38.2 us
    pallas_call x1, Pallas kernels, attend_back(): pl.pallas_call(attend_back_kernel, grid=(pairs,), in_specs=[wide, pl.Bloc...  26.4 us
    select_n x18, other arithmetic, turned_columns(): value = jnp.where(key & bit != 0, swapped, value)  25 us
    rev x18, local copies, waits for them, and re-layouts, turned_columns(): swapped = swapped[..., ::-1, :, :].reshape(value.shape)  23.8 us
  transfers between devices with their start and end apart: 67, of which 21 were waited for; matrix products, arithmetic and copies ran while one was open for 35% of the time, Pallas kernels for 7%

profile of v1, /device:TPU:8, one launch (start us, length us, event | category | flops | bytes accessed | tf_op | source)
XLA Modules:
  0.0 615.4 jit_solution(7775328854724378828)
XLA Ops:
  8.7 3.6 collective-permute-start.10
  12.4 4.7 collective-permute-start.11
  64.4 17.0 %collective-permute-start.18 = (bf16[128,2048]{0,1:T(8,128)(2,1)}, bf16[128,2048]{0,1:T(8,128)(2,1)}, u32[]{:S(2)}, u32[]{:S(2)}) collective-permute-start(bf16[128,2048]{0,1:T(8,128)(2,1)} %bitcast.53), channel_id=1, source_target_pairs={{0,0},{1,4},{2,2},{3,6},{4,1},{5,5},{6,3},{7,7},{8,8},{9,12},{10,1... | collective-permute-start | bytes 1572872 | tf_op jit(solution)/shard_map/ppermute | solution.py:29
  87.1 25.8 %collective-permute-done.6 = bf16[128,1536]{0,1:T(8,128)(2,1)S(1)} collective-permute-done((bf16[128,1536]{0,1:T(8,128)(2,1)S(1)}, bf16[128,1536]{0,1:T(8,128)(2,1)S(1)}, u32[]{:S(2)}, u32[]{:S(2)}) %collective-permute-start.6) | collective-permute-done | bytes 393248 | tf_op jit(solution)/shard_map/ppermute | solution.py:29
  125.0 5.0 multiply_convert_fusion.2.qkv_ref
  130.0 18.6 %attend.1 = (bf16[1024,512]{1,0:T(8,128)(2,1)}, f32[1024,512]{1,0:T(8,128)}) custom-call(bf16[1024,1536]{1,0:T(8,128)(2,1)} %multiply_convert_fusion.2.qkv_ref, f32[1,1024]{1,0:T(1,128)} %compare_select_fusion.bias_ref), custom_call_target="tpu_custom_call" | custom-call | flops 8589934592 | bytes 8388608 | tf_op jit(solution)/shard_map/attend/pallas_call | solution.py:187
  167.4 19.6 %collective-permute-done.20 = bf16[256,2048]{0,1:T(8,128)(2,1)S(1)} collective-permute-done((bf16[256,2048]{0,1:T(8,128)(2,1)}, bf16[256,2048]{0,1:T(8,128)(2,1)S(1)}, u32[]{:S(2)}, u32[]{:S(2)}) %collective-permute-start.20) | collective-permute-done | bytes 1048608 | tf_op jit(solution)/shard_map/ppermute | solution.py:29
  204.7 3.6 collective-permute-done.23
  209.2 26.2 %multiply_convert_fusion.1 = (bf16[1024,2048]{1,0:T(8,128)(2,1)S(1)}, f32[1024,2048]{1,0:T(8,128)}, f32[1024,2048]{1,0:T(8,128)}) fusion(f32[2048]{0:T(1024)S(1)} %slice.351, bf16[1024,2560]{1,0:T(8,128)(2,1)} %constant_dynamic-update-slice_fusion.12, bf16[512,1024]{0,1:T(8,128)(2,1)} %collective-permute-done.17, bf16[512,1024]{0,1:T(8,128)(2,1)S(1)} %fusion.41), kind=kOutput, calls=%fused_computation.11 | convolution fusion | flops 4435476480 | bytes 27271168 | tf_op jit(solution)/shard_map/dot_general | solution.py:142
  235.5 4.6 fusion.133
  260.1 22.7 %collective-permute-start.28 = (bf16[512,1024]{0,1:T(8,128)(2,1)}, bf16[512,1024]{0,1:T(8,128)(2,1)}, u32[]{:S(2)}, u32[]{:S(2)}) collective-permute-start(bf16[512,1024]{0,1:T(8,128)(2,1)} %get-tuple-element.64), channel_id=1, source_target_pairs={{0,4},{1,5},{2,6},{3,7},{4,0},{5,1},{6,2},{7,3},{8,12},{9,13},{10,... | collective-permute-start | bytes 3145736 | tf_op jit(solution)/shard_map/ppermute | solution.py:29
  285.5 10.9 %convert_reduce_fusion = (f32[2048]{0:T(1024)S(1)}, bf16[1024,2048]{1,0:T(8,128)(2,1)S(1)}) fusion(f32[1024,2048]{1,0:T(8,128)} %get-tuple-element.71, f32[1024,2048]{1,0:T(8,128)} %get-tuple-element.116, f32[2048]{0:T(1024)S(1)} %slice.351, bf16[1024,2048]{0,1:T(8,128)(2,1)} %constant_dynamic-update-slice_fusion.44, ...), kind=kOutput, calls=%fused_computation.9 | convolution fusion | flops 4324325376 | bytes 27279360 | tf_op jit(solution)/shard_map/dot_general | solution.py:142
  296.4 8.1 %fusion.13 = f32[1024,1024]{0,1:T(8,128)S(1)} fusion(bf16[1024,2048]{1,0:T(8,128)(2,1)S(1)} %get-tuple-element.118, bf16[1024,2560]{1,0:T(8,128)(2,1)} %constant_dynamic-update-slice_fusion.12), kind=kOutput, calls=%fused_computation.27 | convolution fusion | flops 4294967296 | bytes 12582912 | tf_op jit(solution)/shard_map/dot_general | solution.py:146
  361.4 10.1 %collective-permute-start.25 = (bf16[512,1024]{0,1:T(8,128)(2,1)}, bf16[512,1024]{0,1:T(8,128)(2,1)}, u32[]{:S(2)}, u32[]{:S(2)}) collective-permute-start(bf16[512,1024]{0,1:T(8,128)(2,1)} %fusion.52), channel_id=1, source_target_pairs={{0,0},{1,1},{2,4},{3,5},{4,2},{5,3},{6,6},{7,7},{8,8},{9,9},{10,12... | collective-permute-start | bytes 3145736 | tf_op jit(solution)/shard_map/ppermute | solution.py:29
  377.7 4.8 collective-permute-done.49
  382.5 3.4 collective-permute-start.60
  391.9 3.4 collective-permute-start.53
  395.4 3.8 fusion.42.grad_ref
  399.2 26.4 %attend_back.1 = bf16[1024,1536]{1,0:T(8,128)(2,1)} custom-call(bf16[1024,1536]{1,0:T(8,128)(2,1)} %multiply_convert_fusion.2.qkv_ref, f32[1,1024]{1,0:T(1,128)} %compare_select_fusion.bias_ref, bf16[1024,512]{1,0:T(8,128)(2,1)} %get-tuple-element.19.out_ref, f32[1024,512]{1,0:T(8,128)} %get-tuple-element.20.log_ref, bf16[1024,512]{1,0:T(8,128)(2,1)} %fusion.42.grad_ref), custom_call_target="tpu_custom_call" | custom-call | flops 21474836480 | bytes 12582912 | tf_op jit(solution)/shard_map/attend_back/pallas_call | solution.py:256
  434.0 5.2 fusion.134
  463.3 4.0 collective-permute-done.64
  468.6 4.0 collective-permute-done.65
  473.0 4.7 collective-permute-done.66
  480.4 3.6 collective-permute-done.44
  490.6 31.6 %collective-permute-done.45 = bf16[128,512]{1,0:T(8,128)(2,1)S(1)} collective-permute-done((bf16[128,512]{1,0:T(8,128)(2,1)S(1)}, bf16[128,512]{1,0:T(8,128)(2,1)S(1)}, u32[]{:S(2)}, u32[]{:S(2)}) %collective-permute-start.45) | collective-permute-done | bytes 131104 | tf_op jit(solution)/shard_map/ppermute | solution.py:29
  546.5 5.1 collective-permute-start.38
  554.0 9.8 %collective-permute-done.38 = bf16[128,1536]{1,0:T(8,128)(2,1)S(1)} collective-permute-done((bf16[128,1536]{1,0:T(8,128)(2,1)S(1)}, bf16[128,1536]{1,0:T(8,128)(2,1)S(1)}, u32[]{:S(2)}, u32[]{:S(2)}) %collective-permute-start.38) | collective-permute-done | bytes 393248 | tf_op jit(solution)/shard_map/ppermute | solution.py:29
  563.8 6.9 %collective-permute-done.39 = bf16[128,1536]{1,0:T(8,128)(2,1)S(1)} collective-permute-done((bf16[128,1536]{1,0:T(8,128)(2,1)S(1)}, bf16[128,1536]{1,0:T(8,128)(2,1)S(1)}, u32[]{:S(2)}, u32[]{:S(2)}) %collective-permute-start.39) | collective-permute-done | bytes 393248 | tf_op jit(solution)/shard_map/ppermute | solution.py:29
  580.2 6.6 %collective-permute-done.40 = bf16[128,1536]{1,0:T(8,128)(2,1)} collective-permute-done((bf16[128,1536]{1,0:T(8,128)(2,1)S(1)}, bf16[128,1536]{1,0:T(8,128)(2,1)}, u32[]{:S(2)}, u32[]{:S(2)}) %collective-permute-start.40) | collective-permute-done | bytes 393248 | tf_op jit(solution)/shard_map/ppermute | solution.py:29
  590.7 15.0 %collective-permute-done.33 = bf16[512,1024]{0,1:T(8,128)(2,1)} collective-permute-done((bf16[512,1024]{0,1:T(8,128)(2,1)S(1)}, bf16[512,1024]{0,1:T(8,128)(2,1)}, u32[]{:S(2)}, u32[]{:S(2)}) %collective-permute-start.33) | collective-permute-done | bytes 1048608 | tf_op jit(solution)/shard_map/ppermute | solution.py:29
  605.7 3.9 fusion.37
  609.6 5.3 copy.50
  (466 shorter events, 284.5 us)
Async XLA Ops:
  3.8 48.0 %collective-permute-start.2 = (bf16[128,1536]{0,1:T(8,128)(2,1)S(1)}, bf16[128,1536]{0,1:T(8,128)(2,1)}, u32[]{:S(2)}, u32[]{:S(2)}) collective-permute-start(bf16[128,1536]{0,1:T(8,128)(2,1)S(1)} %bitcast.254), channel_id=1, source_target_pairs={{0,0},{1,4},{2,2},{3,6},{4,1},{5,5},{6,3},{7,7},{8,8},{9,12},{10,1... | collective-permute-start | bytes 1179656 | tf_op jit(solution)/shard_map/ppermute | solution.py:29
  5.7 48.1 %collective-permute-start.3 = (bf16[128,1536]{0,1:T(8,128)(2,1)S(1)}, bf16[128,1536]{0,1:T(8,128)(2,1)}, u32[]{:S(2)}, u32[]{:S(2)}) collective-permute-start(bf16[128,1536]{0,1:T(8,128)(2,1)S(1)} %bitcast.255), channel_id=1, source_target_pairs={{0,1},{1,5},{2,3},{3,7},{4,0},{5,4},{6,2},{7,6},{8,9},{9,13},{10,1... | collective-permute-start | bytes 1179656 | tf_op jit(solution)/shard_map/ppermute | solution.py:29
  8.7 50.0 %collective-permute-start.10 = (bf16[128,2560]{1,0:T(8,128)(2,1)}, bf16[128,2560]{1,0:T(8,128)(2,1)}, u32[]{:S(2)}, u32[]{:S(2)}) collective-permute-start(bf16[128,2560]{1,0:T(8,128)(2,1)} %pad_maximum_fusion.14), channel_id=1, source_target_pairs={{0,0},{1,4},{2,2},{3,6},{4,1},{5,5},{6,3},{7,7},{8,8},{9,12},{10,1... | collective-permute-start | bytes 1966088 | tf_op jit(solution)/shard_map/ppermute | solution.py:29
  12.4 48.6 %collective-permute-start.11 = (bf16[128,2560]{1,0:T(8,128)(2,1)}, bf16[128,2560]{1,0:T(8,128)(2,1)}, u32[]{:S(2)}, u32[]{:S(2)}) collective-permute-start(bf16[128,2560]{1,0:T(8,128)(2,1)} %pad_maximum_fusion.14), channel_id=1, source_target_pairs={{0,1},{1,5},{2,3},{3,7},{4,0},{5,4},{6,2},{7,6},{8,9},{9,13},{10,1... | collective-permute-start | bytes 1966088 | tf_op jit(solution)/shard_map/ppermute | solution.py:29
  63.3 51.5 %collective-permute-start.12 = (bf16[256,2560]{1,0:T(8,128)(2,1)}, bf16[256,2560]{1,0:T(8,128)(2,1)S(1)}, u32[]{:S(2)}, u32[]{:S(2)}) collective-permute-start(bf16[256,2560]{1,0:T(8,128)(2,1)} %get-tuple-element.84), channel_id=1, source_target_pairs={{0,8},{1,9},{2,10},{3,11},{4,12},{5,13},{6,14},{7,15},{8,0},{9,1},... | collective-permute-start | bytes 3932168 | tf_op jit(solution)/shard_map/ppermute | solution.py:29
  63.8 53.5 %collective-permute-start.13 = (bf16[256,2560]{1,0:T(8,128)(2,1)}, bf16[256,2560]{1,0:T(8,128)(2,1)}, u32[]{:S(2)}, u32[]{:S(2)}) collective-permute-start(bf16[256,2560]{1,0:T(8,128)(2,1)} %get-tuple-element.84), channel_id=1, source_target_pairs={{0,16},{1,17},{2,18},{3,19},{4,20},{5,21},{6,22},{7,23},{8,24},{9,... | collective-permute-start | bytes 3932168 | tf_op jit(solution)/shard_map/ppermute | solution.py:29
  64.4 92.4 %collective-permute-start.18 = (bf16[128,2048]{0,1:T(8,128)(2,1)}, bf16[128,2048]{0,1:T(8,128)(2,1)}, u32[]{:S(2)}, u32[]{:S(2)}) collective-permute-start(bf16[128,2048]{0,1:T(8,128)(2,1)} %bitcast.53), channel_id=1, source_target_pairs={{0,0},{1,4},{2,2},{3,6},{4,1},{5,5},{6,3},{7,7},{8,8},{9,12},{10,1... | collective-permute-start | bytes 1572872 | tf_op jit(solution)/shard_map/ppermute | solution.py:29
  81.6 31.3 %collective-permute-start.6 = (bf16[128,1536]{0,1:T(8,128)(2,1)S(1)}, bf16[128,1536]{0,1:T(8,128)(2,1)S(1)}, u32[]{:S(2)}, u32[]{:S(2)}) collective-permute-start(bf16[128,1536]{0,1:T(8,128)(2,1)S(1)} %slice.341), channel_id=1, source_target_pairs={{0,16},{1,17},{2,18},{3,19},{4,20},{5,21},{6,22},{7,23},{8,24},{9,... | collective-permute-start | bytes 1179656 | tf_op jit(solution)/shard_map/ppermute | solution.py:29
  114.4 44.7 %collective-permute-start.19 = (bf16[128,2048]{0,1:T(8,128)(2,1)}, bf16[128,2048]{0,1:T(8,128)(2,1)}, u32[]{:S(2)}, u32[]{:S(2)}) collective-permute-start(bf16[128,2048]{0,1:T(8,128)(2,1)} %bitcast.53), channel_id=1, source_target_pairs={{0,1},{1,5},{2,3},{3,7},{4,0},{5,4},{6,2},{7,6},{8,9},{9,13},{10,1... | collective-permute-start | bytes 1572872 | tf_op jit(solution)/shard_map/ppermute | solution.py:29
  115.8 32.9 %collective-permute-start.14 = (bf16[128,2560]{1,0:T(8,128)(2,1)}, bf16[128,2560]{1,0:T(8,128)(2,1)S(1)}, u32[]{:S(2)}, u32[]{:S(2)}) collective-permute-start(bf16[128,2560]{1,0:T(8,128)(2,1)} %slice.345), channel_id=1, source_target_pairs={{0,16},{1,17},{2,18},{3,19},{4,20},{5,21},{6,22},{7,23},{8,24},{9,... | collective-permute-start | bytes 1966088 | tf_op jit(solution)/shard_map/ppermute | solution.py:29
  119.3 30.2 %collective-permute-start.15 = (bf16[128,2560]{1,0:T(8,128)(2,1)}, bf16[128,2560]{1,0:T(8,128)(2,1)}, u32[]{:S(2)}, u32[]{:S(2)}) collective-permute-start(bf16[128,2560]{1,0:T(8,128)(2,1)} %slice.346), channel_id=1, source_target_pairs={{0,8},{1,9},{2,10},{3,11},{4,12},{5,13},{6,14},{7,15},{8,0},{9,1},... | collective-permute-start | bytes 1966088 | tf_op jit(solution)/shard_map/ppermute | solution.py:29
  162.8 31.1 %collective-permute-start.21 = (bf16[256,2048]{0,1:T(8,128)(2,1)}, bf16[256,2048]{0,1:T(8,128)(2,1)}, u32[]{:S(2)}, u32[]{:S(2)}) collective-permute-start(bf16[256,2048]{0,1:T(8,128)(2,1)} %get-tuple-element.88), channel_id=1, source_target_pairs={{0,16},{1,17},{2,18},{3,19},{4,20},{5,21},{6,22},{7,23},{8,24},{9,... | collective-permute-start | bytes 3145736 | tf_op jit(solution)/shard_map/ppermute | solution.py:29
  167.3 41.9 %collective-permute-start.17 = (bf16[512,1024]{0,1:T(8,128)(2,1)S(1)}, bf16[512,1024]{0,1:T(8,128)(2,1)}, u32[]{:S(2)}, u32[]{:S(2)}) collective-permute-start(bf16[512,1024]{0,1:T(8,128)(2,1)S(1)} %fusion.41), channel_id=1, source_target_pairs={{0,4},{1,5},{2,6},{3,7},{4,0},{5,1},{6,2},{7,3},{8,12},{9,13},{10,... | collective-permute-start | bytes 3145736 | tf_op jit(solution)/shard_map/ppermute | solution.py:29
  304.6 35.7 %collective-permute-start.29 = (bf16[512,1024]{0,1:T(8,128)(2,1)S(1)}, bf16[512,1024]{0,1:T(8,128)(2,1)S(1)}, u32[]{:S(2)}, u32[]{:S(2)}) collective-permute-start(bf16[512,1024]{0,1:T(8,128)(2,1)S(1)} %slice.599), channel_id=1, source_target_pairs={{0,4},{1,5},{2,6},{3,7},{4,0},{5,1},{6,2},{7,3},{8,12},{9,13},{10,... | collective-permute-start | bytes 3145736 | tf_op jit(solution)/shard_map/ppermute | solution.py:29
  327.3 34.1 %collective-permute-start.56 = (bf16[256,2048]{1,0:T(8,128)(2,1)}, bf16[256,2048]{1,0:T(8,128)(2,1)}, u32[]{:S(2)}, u32[]{:S(2)}) collective-permute-start(bf16[256,2048]{1,0:T(8,128)(2,1)} %pad_maximum_fusion.10), channel_id=1, source_target_pairs={{0,8},{1,9},{2,10},{3,11},{4,12},{5,13},{6,14},{7,15},{8,0},{9,1},... | collective-permute-start | bytes 3145736 | tf_op jit(solution)/shard_map/ppermute | solution.py:29
  330.4 41.2 %collective-permute-start.58 = (bf16[256,2048]{1,0:T(8,128)(2,1)}, bf16[256,2048]{1,0:T(8,128)(2,1)}, u32[]{:S(2)}, u32[]{:S(2)}) collective-permute-start(bf16[256,2048]{1,0:T(8,128)(2,1)} %pad_maximum_fusion.11), channel_id=1, source_target_pairs={{0,16},{1,17},{2,18},{3,19},{4,20},{5,21},{6,22},{7,23},{8,24},{9,... | collective-permute-start | bytes 3145736 | tf_op jit(solution)/shard_map/ppermute | solution.py:29
  333.4 49.1 %collective-permute-start.49 = (bf16[256,2048]{1,0:T(8,128)(2,1)}, bf16[256,2048]{1,0:T(8,128)(2,1)}, u32[]{:S(2)}, u32[]{:S(2)}) collective-permute-start(bf16[256,2048]{1,0:T(8,128)(2,1)} %pad_maximum_fusion.8), channel_id=1, source_target_pairs={{0,8},{1,9},{2,10},{3,11},{4,12},{5,13},{6,14},{7,15},{8,0},{9,1},... | collective-permute-start | bytes 3145736 | tf_op jit(solution)/shard_map/ppermute | solution.py:29
  339.7 46.2 %collective-permute-start.51 = (bf16[256,2048]{1,0:T(8,128)(2,1)}, bf16[256,2048]{1,0:T(8,128)(2,1)}, u32[]{:S(2)}, u32[]{:S(2)}) collective-permute-start(bf16[256,2048]{1,0:T(8,128)(2,1)} %pad_maximum_fusion.9), channel_id=1, source_target_pairs={{0,16},{1,17},{2,18},{3,19},{4,20},{5,21},{6,22},{7,23},{8,24},{9,... | collective-permute-start | bytes 3145736 | tf_op jit(solution)/shard_map/ppermute | solution.py:29
  346.1 45.8 %collective-permute-start.30 = (bf16[512,1024]{0,1:T(8,128)(2,1)S(1)}, bf16[512,1024]{0,1:T(8,128)(2,1)}, u32[]{:S(2)}, u32[]{:S(2)}) collective-permute-start(bf16[512,1024]{0,1:T(8,128)(2,1)S(1)} %get-tuple-element.66), channel_id=1, source_target_pairs={{0,4},{1,5},{2,6},{3,7},{4,0},{5,1},{6,2},{7,3},{8,12},{9,13},{10,... | collective-permute-start | bytes 3145736 | tf_op jit(solution)/shard_map/ppermute | solution.py:29
  361.4 118.8 %collective-permute-start.25 = (bf16[512,1024]{0,1:T(8,128)(2,1)}, bf16[512,1024]{0,1:T(8,128)(2,1)}, u32[]{:S(2)}, u32[]{:S(2)}) collective-permute-start(bf16[512,1024]{0,1:T(8,128)(2,1)} %fusion.52), channel_id=1, source_target_pairs={{0,0},{1,1},{2,4},{3,5},{4,2},{5,3},{6,6},{7,7},{8,8},{9,9},{10,12... | collective-permute-start | bytes 3145736 | tf_op jit(solution)/shard_map/ppermute | solution.py:29
  375.8 75.4 %collective-permute-start.59 = (bf16[128,2048]{1,0:T(8,128)(2,1)}, bf16[128,2048]{1,0:T(8,128)(2,1)}, u32[]{:S(2)}, u32[]{:S(2)}) collective-permute-start(bf16[128,2048]{1,0:T(8,128)(2,1)} %get-tuple-element.75), channel_id=1, source_target_pairs={{0,0},{1,4},{2,2},{3,6},{4,1},{5,5},{6,3},{7,7},{8,8},{9,12},{10,1... | collective-permute-start | bytes 1572872 | tf_op jit(solution)/shard_map/ppermute | solution.py:29
  382.5 68.8 %collective-permute-start.60 = (bf16[128,2048]{1,0:T(8,128)(2,1)}, bf16[128,2048]{1,0:T(8,128)(2,1)}, u32[]{:S(2)}, u32[]{:S(2)}) collective-permute-start(bf16[128,2048]{1,0:T(8,128)(2,1)} %get-tuple-element.76), channel_id=1, source_target_pairs={{0,4},{1,0},{2,6},{3,2},{4,5},{5,1},{6,7},{7,3},{8,12},{9,8},{10,1... | collective-permute-start | bytes 1572872 | tf_op jit(solution)/shard_map/ppermute | solution.py:29
  390.0 65.3 %collective-permute-start.52 = (bf16[128,2048]{1,0:T(8,128)(2,1)}, bf16[128,2048]{1,0:T(8,128)(2,1)}, u32[]{:S(2)}, u32[]{:S(2)}) collective-permute-start(bf16[128,2048]{1,0:T(8,128)(2,1)} %get-tuple-element.77), channel_id=1, source_target_pairs={{0,0},{1,4},{2,2},{3,6},{4,1},{5,5},{6,3},{7,7},{8,8},{9,12},{10,1... | collective-permute-start | bytes 1572872 | tf_op jit(solution)/shard_map/ppermute | solution.py:29
  391.9 64.7 %collective-permute-start.53 = (bf16[128,2048]{1,0:T(8,128)(2,1)}, bf16[128,2048]{1,0:T(8,128)(2,1)}, u32[]{:S(2)}, u32[]{:S(2)}) collective-permute-start(bf16[128,2048]{1,0:T(8,128)(2,1)} %get-tuple-element.78), channel_id=1, source_target_pairs={{0,4},{1,0},{2,6},{3,2},{4,5},{5,1},{6,7},{7,3},{8,12},{9,8},{10,1... | collective-permute-start | bytes 1572872 | tf_op jit(solution)/shard_map/ppermute | solution.py:29
  455.3 30.5 %collective-permute-start.34 = (bf16[128,1536]{1,0:T(8,128)(2,1)S(1)}, bf16[128,1536]{1,0:T(8,128)(2,1)S(1)}, u32[]{:S(2)}, u32[]{:S(2)}) collective-permute-start(bf16[128,1536]{1,0:T(8,128)(2,1)S(1)} %convolution_convert_fusion.14), channel_id=1, source_target_pairs={{0,16},{1,17},{2,18},{3,19},{4,20},{5,21},{6,22},{7,23},{8,24},{9,... | collective-permute-start | bytes 1179656 | tf_op jit(solution)/shard_map/ppermute | solution.py:29
  480.3 48.6 %collective-permute-start.31 = (bf16[512,1024]{0,1:T(8,128)(2,1)}, bf16[512,1024]{0,1:T(8,128)(2,1)}, u32[]{:S(2)}, u32[]{:S(2)}) collective-permute-start(bf16[512,1024]{0,1:T(8,128)(2,1)} %slice.598), channel_id=1, source_target_pairs={{0,4},{1,5},{2,6},{3,7},{4,0},{5,1},{6,2},{7,3},{8,12},{9,13},{10,... | collective-permute-start | bytes 3145736 | tf_op jit(solution)/shard_map/ppermute | solution.py:29
  480.4 94.9 %collective-permute-start.26 = (bf16[512,1024]{0,1:T(8,128)(2,1)}, bf16[512,1024]{0,1:T(8,128)(2,1)}, u32[]{:S(2)}, u32[]{:S(2)}) collective-permute-start(bf16[512,1024]{0,1:T(8,128)(2,1)} %collective-permute-done.25), channel_id=1, source_target_pairs={{0,1},{1,0},{2,3},{3,2},{4,5},{5,4},{6,7},{7,6},{8,9},{9,8},{10,11... | collective-permute-start | bytes 3145736 | tf_op jit(solution)/shard_map/ppermute | solution.py:29
  484.0 42.8 %collective-permute-start.61 = (bf16[128,2048]{1,0:T(8,128)(2,1)S(1)}, bf16[128,2048]{1,0:T(8,128)(2,1)S(1)}, u32[]{:S(2)}, u32[]{:S(2)}) collective-permute-start(bf16[128,2048]{1,0:T(8,128)(2,1)S(1)} %add_convert_fusion.1), channel_id=1, source_target_pairs={{0,2},{1,3},{2,0},{3,1},{4,6},{5,7},{6,4},{7,5},{8,10},{9,11},{10,... | collective-permute-start | bytes 1572872 | tf_op jit(solution)/shard_map/ppermute | solution.py:29
  485.8 36.4 %collective-permute-start.45 = (bf16[128,512]{1,0:T(8,128)(2,1)S(1)}, bf16[128,512]{1,0:T(8,128)(2,1)S(1)}, u32[]{:S(2)}, u32[]{:S(2)}) collective-permute-start(bf16[128,512]{1,0:T(8,128)(2,1)S(1)} %get-tuple-element.96), channel_id=1, source_target_pairs={{0,0},{1,4},{2,2},{3,6},{4,1},{5,5},{6,3},{7,7},{8,8},{9,12},{10,1... | collective-permute-start | bytes 393224 | tf_op jit(solution)/shard_map/ppermute | solution.py:29
  488.0 36.6 %collective-permute-start.46 = (bf16[128,512]{1,0:T(8,128)(2,1)S(1)}, bf16[128,512]{1,0:T(8,128)(2,1)S(1)}, u32[]{:S(2)}, u32[]{:S(2)}) collective-permute-start(bf16[128,512]{1,0:T(8,128)(2,1)S(1)} %get-tuple-element.97), channel_id=1, source_target_pairs={{0,4},{1,0},{2,6},{3,2},{4,5},{5,1},{6,7},{7,3},{8,12},{9,8},{10,1... | collective-permute-start | bytes 393224 | tf_op jit(solution)/shard_map/ppermute | solution.py:29
  528.9 44.5 %collective-permute-start.47 = (bf16[128,512]{1,0:T(8,128)(2,1)}, bf16[128,512]{1,0:T(8,128)(2,1)}, u32[]{:S(2)}, u32[]{:S(2)}) collective-permute-start(bf16[128,512]{1,0:T(8,128)(2,1)} %add_convert_fusion.10), channel_id=1, source_target_pairs={{0,2},{1,3},{2,0},{3,1},{4,6},{5,7},{6,4},{7,5},{8,10},{9,11},{10,... | collective-permute-start | bytes 393224 | tf_op jit(solution)/shard_map/ppermute | solution.py:29
  570.8 34.9 %collective-permute-start.33 = (bf16[512,1024]{0,1:T(8,128)(2,1)S(1)}, bf16[512,1024]{0,1:T(8,128)(2,1)}, u32[]{:S(2)}, u32[]{:S(2)}) collective-permute-start(bf16[512,1024]{0,1:T(8,128)(2,1)S(1)} %collective-permute-done.32), channel_id=1, source_target_pairs={{0,1},{1,0},{2,3},{3,2},{4,5},{5,4},{6,7},{7,6},{8,9},{9,8},{10,11... | collective-permute-start | bytes 3145736 | tf_op jit(solution)/shard_map/ppermute | solution.py:29
  (95 other events, 1243.1 us)

commit v2 on v1

--- a/solution.py
+++ b/solution.py
@@ -21,12 +21,25 @@
 def send(value, target):
     fsdp, ctx, tp = (lax.axis_size(axis) for axis in AXES)
     pairs = []
+    kept = 0
     for f in range(fsdp):
         for h in range(ctx):
             for t in range(tp):
                 plane, core, high, low = target(f // 2, f % 2, h, t)
-                pairs.append(((f * ctx + h) * tp + t, ((2 * plane + core) * ctx + high) * tp + low))
-    return lax.ppermute(value, AXES, pairs)
+                source = (f * ctx + h) * tp + t
+                place_of = ((2 * plane + core) * ctx + high) * tp + low
+                if source == place_of:
+                    kept += 1
+                else:
+                    pairs.append((source, place_of))
+    moved = lax.ppermute(value, AXES, pairs)
+    if not kept:
+        return moved
+    plane, core = lax.axis_index("fsdp") // 2, lax.axis_index("fsdp") % 2
+    high, low = lax.axis_index("ctx"), lax.axis_index("tp")
+    _, at_core, at_high, at_low = target(plane, core, high, low)
+    stays = (at_core == core) & (at_high == high) & (at_low == low)
+    return jnp.where(stays, value, moved)
 
 
 def to_core(value):
@@ -70,42 +83,208 @@
     return [[2 * p + c for p in range(fsdp // 2)] for c in range(2)]
 
 
-def gather_rows(shard):
-    first = to_first(shard)
-    second = to_second(shard)
-    unit = jnp.concatenate([first, second], axis=0)
-    planes = lax.axis_size("fsdp") // 2
-    if planes != 4:
-        return lax.all_gather(unit, "fsdp", axis=0, tiled=True, axis_index_groups=plane_groups())
-    half = shard.shape[0]
-    over_x = to_x(unit)
-    over_y = to_y(unit)
-    far_first = to_y(over_x[:half])
-    far_second = to_x(over_y[half:])
-    return jnp.concatenate([unit, over_x, over_y, far_first, far_second], axis=0)
-
-
-def scatter_rows(rows_of, half):
-    planes = lax.axis_size("fsdp") // 2
-    if planes != 4:
-        whole = rows_of(0, 2 * planes * half)
-        mine = lax.psum_scatter(
-            whole, "fsdp", scatter_dimension=0, tiled=True, axis_index_groups=plane_groups()
+def sorted_pair(first, second):
+    low = lax.axis_index("tp")
+    ahead = jnp.where(low == 0, first, second)
+    behind = jnp.where(low == 0, second, first)
+    return ahead, behind
+
+
+def after(value, *others):
+    return lax.optimization_barrier((value,) + others)[0]
+
+
+def place_kernel(key_ref, *refs, homes, half, spans, outs):
+    pieces = refs[: len(homes)]
+    wholes, marks = refs[-1 - outs : -1], refs[-1]
+    key = key_ref[0]
+    copies = []
+    for piece, blocks in zip(pieces, homes):
+        for at, block in enumerate(blocks):
+            start = pl.multiple_of((key ^ block) * half, half)
+            for whole, (column, width) in zip(wholes, spans):
+                copies.append(
+                    pltpu.make_async_copy(
+                        piece.at[pl.ds(at * half, half), pl.ds(column, width)],
+                        whole.at[pl.ds(start, half), :],
+                        marks.at[len(copies)],
+                    )
+                )
+    for copy in copies:
+        copy.start()
+    for copy in copies:
+        copy.wait()
+
+
+def place(key, pieces, homes, half, spans, wholes=()):
+    anywhere = pl.BlockSpec(memory_space=pl.ANY)
+    near = pl.BlockSpec(memory_space=pltpu.VMEM)
+    count = len(spans) * sum(len(home) for home in homes)
+    first = 1 + len(pieces)
+    return pl.pallas_call(
+        functools.partial(place_kernel, homes=homes, half=half, spans=spans, outs=len(spans)),
+        in_specs=[pl.BlockSpec(memory_space=pltpu.SMEM)]
+        + [near] * len(pieces)
+        + [anywhere] * len(wholes),
+        out_specs=[anywhere] * len(spans),
+        out_shape=[jax.ShapeDtypeStruct((8 * half, width), BF16) for _, width in spans],
+        scratch_shapes=[pltpu.SemaphoreType.DMA((count,))],
+        input_output_aliases={first + i: i for i in range(len(wholes))},
+        name="place",
+    )(key, *pieces, *wholes)
+
+
+class Gather:
+    def __init__(self, shard):
+        self.half = shard.shape[0]
+        self.width = shard.shape[1]
+        self.first = to_first(shard)
+        self.second = to_second(shard)
+        self.planes = lax.axis_size("fsdp") // 2
+        self.arrived = (self.first, self.second)
+
+    def near(self, *others):
+        if self.planes != 4:
+            unit = jnp.concatenate(sorted_pair(self.first, self.second), axis=0)
+            self.whole = lax.all_gather(
+                unit, "fsdp", axis=0, tiled=True, axis_index_groups=plane_groups()
+            )
+            return
+        first, second = after(self.first, *others), after(self.second, *others)
+        self.over_x = (to_x(first), to_x(second))
+        self.over_y = (to_y(first), to_y(second))
+
+    def far(self, key, spans):
+        if self.planes != 4:
+            return [[self.whole[:, a : a + n] for a, n in group] for group in spans]
+        half = self.half
+        sent = []
+        for group in spans:
+            start, stop = group[0][0], group[-1][0] + group[-1][1]
+            first = to_y(self.over_x[0][:, start:stop])
+            second = to_x(self.over_y[1][:, start:stop])
+            sent.append((start, first, second))
+        result = []
+        pieces = (self.first, self.second) + self.over_x + self.over_y
+        homes = tuple((block,) for block in range(6))
+        for group, (start, first, second) in zip(spans, sent):
+            wholes = place(key, pieces, homes, half, group)
+            moved = [(a - start, n) for a, n in group]
+            result.append(place(key, (first, second), ((6,), (7,)), half, moved, wholes))
+        return result
+
+
+def feature_rows(lefts, right):
+    half = right.shape[0] // 2
+    total = row_product(lefts[0][...], right[:half, :], F32)
+    return total + row_product(lefts[1][...], right[half:, :], F32)
+
+
+def far_kernel(at_ref, own_ref, other_ref, right_ref, first_ref, second_ref):
+    half = first_ref.shape[0]
+    total = feature_rows((own_ref, other_ref), right_ref).astype(BF16)
+    first_ref[...] = total[:half]
+    second_ref[...] = total[half:]
+
+
+def near_kernel(
+    at_ref, x_own, x_other, y_own, y_other, right_ref, first_ref, second_ref, x_ref, y_ref
+):
+    half = first_ref.shape[0]
+    over_x = feature_rows((x_own, x_other), right_ref)
+    x_ref[:half, :] = (over_x[:half] + first_ref[...].astype(F32)).astype(BF16)
+    x_ref[half:, :] = over_x[half:].astype(BF16)
+    over_y = feature_rows((y_own, y_other), right_ref)
+    y_ref[:half, :] = over_y[:half].astype(BF16)
+    y_ref[half:, :] = (over_y[half:] + second_ref[...].astype(F32)).astype(BF16)
+
+
+def own_kernel(at_ref, own_ref, other_ref, right_ref, x_ref, y_ref, first_ref, second_ref):
+    half = first_ref.shape[0]
+    low = at_ref[1]
+    total = feature_rows((own_ref, other_ref), right_ref)
+    total = total + x_ref[...].astype(F32) + y_ref[...].astype(F32)
+    total = total.astype(BF16)
+    first_ref[...] = jnp.where(low == 0, total[:half], total[half:])
+    second_ref[...] = jnp.where(low == 0, total[half:], total[:half])
+
+
+def feature_call(kernel, name, at, lefts, right, extras, steps, outs):
+    tokens, width = right.shape
+    tile = min(width, 512)
+    size = 2 * (lefts[0].shape[1] // 8)
+
+    def left_spec(step):
+        return pl.BlockSpec((tokens // 2, size), lambda i, at: (0, at[0] ^ step))
+
+    def column_spec(rows):
+        return pl.BlockSpec((rows, tile), lambda i, at: (0, i))
+
+    operands, specs = [], []
+    for step in steps:
+        for left in lefts:
+            operands.append(left)
+            specs.append(left_spec(step))
+    return pl.pallas_call(
+        kernel,
+        grid_spec=pltpu.PrefetchScalarGridSpec(
+            num_scalar_prefetch=1,
+            grid=(width // tile,),
+            in_specs=specs + [column_spec(tokens)] + [column_spec(e.shape[0]) for e in extras],
+            out_specs=[column_spec(rows) for rows in outs],
+        ),
+        out_shape=[jax.ShapeDtypeStruct((rows, width), BF16) for rows in outs],
+        cost_estimate=pl.CostEstimate(
+            flops=tokens * width, bytes_accessed=tokens * width, transcendentals=0
+        ),
+        name=name,
+    )(at, *operands, right, *extras)
+
+
+class Scatter:
+    def __init__(self, lefts, right, half):
+        self.half = half
+        self.lefts = lefts
+        self.right = right
+        self.planes = lax.axis_size("fsdp") // 2
+        plane, low = lax.axis_index("fsdp") // 2, lax.axis_index("tp")
+        self.at = jnp.stack([plane, low]).astype(jnp.int32)
+        if self.planes == 4:
+            first, second = feature_call(
+                far_kernel, "far_rows", self.at, lefts, right, (), (3,), (half, half)
+            )
+            self.far_first = to_y(first)
+            self.far_second = to_x(second)
+
+    def near(self, *others):
+        if self.planes != 4:
+            return
+        half = self.half
+        over_x, over_y = feature_call(
+            near_kernel, "near_rows", self.at, self.lefts, after(self.right, *others),
+            (self.far_first, self.far_second), (1, 2), (2 * half, 2 * half),
         )
-    else:
-        far_first = to_y(rows_of(6 * half, 7 * half))
-        far_second = to_x(rows_of(7 * half, 8 * half))
-        over_x = rows_of(2 * half, 4 * half)
-        over_y = rows_of(4 * half, 6 * half)
-        over_x = jnp.concatenate([added(over_x[:half], far_first), over_x[half:]], axis=0)
-        over_y = jnp.concatenate([over_y[:half], added(over_y[half:], far_second)], axis=0)
-        over_x = to_x(over_x)
-        over_y = to_y(over_y)
-        mine = rows_of(0, 2 * half).astype(F32) + over_x.astype(F32) + over_y.astype(F32)
-        mine = mine.astype(BF16)
-    first = to_first(mine[:half])
-    second = from_second(mine[half:])
-    return added(first, second)
+        self.over_x = to_x(over_x)
+        self.over_y = to_y(over_y)
+
+    def own(self, *others):
+        half = self.half
+        right = after(self.right, *others)
+        if self.planes != 4:
+            mine = lax.psum_scatter(
+                row_product(jnp.concatenate(self.lefts, axis=0), right), "fsdp",
+                scatter_dimension=0, tiled=True, axis_index_groups=plane_groups(),
+            )
+            self.pair = sorted_pair(mine[:half], mine[half:])
+        else:
+            self.pair = feature_call(
+                own_kernel, "own_rows", self.at, self.lefts, right,
+                (self.over_x, self.over_y), (0,), (half, half),
+            )
+        self.landed = (to_first(self.pair[0]), from_second(self.pair[1]))
+
+    def part(self):
+        return added(*self.landed)
 
 
 def added(one, other):
@@ -123,19 +302,6 @@
     for step in (to_core, to_x, to_y, to_low, to_high):
         vector = vector + step(vector)
     return vector
-
-
-def turned_columns(value, key, width):
-    lead = value.shape[:-1]
-    blocks = value.shape[-1] // width
-    value = value.reshape(lead + (blocks, width))
-    bit = 1
-    while bit < blocks:
-        swapped = value.reshape(lead + (blocks // (2 * bit), 2, bit, width))
-        swapped = swapped[..., ::-1, :, :].reshape(value.shape)
-        value = jnp.where((key & bit) != 0, swapped, value)
-        bit *= 2
-    return value.reshape(lead + (blocks * width,))
 
 
 def product(left, right, out=F32):
@@ -200,8 +366,7 @@
             jax.ShapeDtypeStruct((rows, pairs * PAIR), F32),
         ],
         cost_estimate=pl.CostEstimate(
-            flops=4 * flops, bytes_accessed=8 * rows * pairs * PAIR * 2,
-            transcendentals=2 * pairs * rows * rows,
+            flops=flops // 64, bytes_accessed=rows * pairs * PAIR, transcendentals=0,
         ),
         name="attend",
     )(qkv, bias)
@@ -261,8 +426,7 @@
         out_shape=jax.ShapeDtypeStruct(qkv.shape, BF16),
         scratch_shapes=[pltpu.VMEM((rows, PAIR), F32)] * 2,
         cost_estimate=pl.CostEstimate(
-            flops=4 * flops, bytes_accessed=12 * rows * pairs * PAIR * 2,
-            transcendentals=2 * pairs * rows * rows,
+            flops=flops // 64, bytes_accessed=rows * pairs * PAIR, transcendentals=0,
         ),
         name="attend_back",
     )(qkv, bias, out, logs, grad)
@@ -325,28 +489,35 @@
     width = layer_in.shape[2]
     heads_width = query_weight.shape[1]
     hidden = up_weight.shape[1]
-    key = 2 * plane + low if planes == 4 else low
-    order = functools.partial(turned_columns, key=key, width=half)
-
-    qkv_shard = weave([query_weight, key_weight, value_weight])
-    qkv_weight = gather_rows(qkv_shard)
-    mine_in = order(lax.dynamic_index_in_dim(layer_in, low, 0, keepdims=False))
+    key = (2 * plane + low).astype(jnp.int32)[None]
+    qkv_width = 3 * heads_width
+    inner_gather = Gather(
+        jnp.concatenate([weave([query_weight, key_weight, value_weight]), out_weight.T], axis=1)
+    )
+    mine_in = lax.dynamic_index_in_dim(layer_in, low, 0, keepdims=False)
     own = to_turned(mine_in)
+    inner_gather.near()
+    outer_shard = jnp.concatenate([up_weight, down_weight.T], axis=1)
+    outer_gather = Gather(after(outer_shard, inner_gather.first, inner_gather.second))
     other = to_core(own)
     x = jnp.concatenate([own, other], axis=0)
     vectors = to_first(jnp.concatenate([query_bias, value_bias, up_bias]))
     lengths_other = to_core(lengths)
     length = jnp.where(core == high, lengths, lengths_other)
     length = lax.dynamic_index_in_dim(length, low, 0, keepdims=False)
-    out_up = gather_rows(jnp.concatenate([out_weight.T, up_weight], axis=1))
-    out_t = out_up[:, :heads_width]
-    up = out_up[:, heads_width:]
-    down_t = gather_rows(down_weight.T)
-    mine_grad = order(lax.dynamic_index_in_dim(out_grad, low, 0, keepdims=False))
-    own_grad = to_turned(mine_grad)
-
-    out_b, down_b, gain1, bias1, gain2, bias2 = order(
-        jnp.stack([out_bias, down_bias, norm_gain, norm_bias, final_gain, final_bias])
+    ((qkv_weight, out_t),) = inner_gather.far(
+        key, (((0, qkv_width), (qkv_width, heads_width)),)
+    )
+    if planes == 4:
+        outer_gather.near(*inner_gather.over_x, *inner_gather.over_y)
+    else:
+        outer_gather.near()
+    mine_grad = lax.dynamic_index_in_dim(out_grad, low, 0, keepdims=False)
+    own_grad = to_turned(after(mine_grad, own))
+    x = after(x, *outer_gather.arrived)
+
+    out_b, down_b, gain1, bias1, gain2, bias2 = (
+        out_bias, down_bias, norm_gain, norm_bias, final_gain, final_bias
     )
     query_b = vectors[:heads_width]
     value_b = vectors[heads_width : 2 * heads_width]
@@ -368,20 +539,27 @@
 
     qkv = ((product(x, qkv_weight) + qkv_b) * scales).astype(BF16)
     merged, logs = attend(qkv, bias)
-    attn = product_back(merged, out_t)
-    first = own.astype(F32) + attn[:rows] + to_core(attn[rows:].astype(BF16)).astype(F32) + out_b
+    if planes == 4:
+        merged = after(merged, own_grad, *outer_gather.over_x, *outer_gather.over_y)
+    (up,), (down_t,) = outer_gather.far(key, (((0, hidden),), ((hidden, hidden),)))
+    attn_other = to_core(product_back(merged[rows:], out_t, BF16))
+    attn = product_back(merged[:rows], out_t)
+    first = own.astype(F32) + attn + attn_other.astype(F32) + out_b
     unit1, scale1 = normed_of(first)
     normed = unit1 * gain1 + bias1
     normed_own = normed.astype(BF16)
-    normed_low = jnp.concatenate([normed_own, to_core(normed_own)], axis=0)
+    normed_other = to_core(normed_own)
+    normed_low = jnp.concatenate([normed_own, normed_other], axis=0)
     upper = product(normed_low, up) + up_b
-    cdf = 0.5 * lax.erfc(upper * -(0.5**0.5))
+    cdf = 0.5 + 0.5 * lax.erf(upper * 0.5**0.5)
     activated = (upper * cdf).astype(BF16)
     slope = (cdf + upper * jnp.exp(-0.5 * upper * upper) * (2 * jnp.pi) ** -0.5).astype(BF16)
-    ffn = product_back(activated, down_t)
-    second = normed + ffn[:rows] + to_core(ffn[rows:].astype(BF16)).astype(F32) + down_b
+    activated, slope = lax.optimization_barrier((activated, slope))
+    ffn_other = to_core(product_back(activated[rows:], down_t, BF16))
+    ffn = product_back(activated[:rows], down_t)
+    second = normed + ffn + ffn_other.astype(F32) + down_b
     unit2, scale2 = normed_of(second)
-    result = order((unit2 * gain2 + bias2).astype(BF16))
+    result = (unit2 * gain2 + bias2).astype(BF16)
     result = to_turned(result)
     result_pair = to_low(result)
     layer_out = jnp.where(
@@ -394,32 +572,50 @@
     d_second = norm_back(cot, gain2, unit2, scale2)
     d_ffn_own = d_second.astype(BF16)
     down_bias_grad = jnp.sum(d_ffn_own.astype(F32), axis=0)
-    d_ffn = jnp.concatenate([d_ffn_own, to_core(d_ffn_own)], axis=0)
-    down_part = scatter_rows(lambda a, b: row_product(d_ffn[:, a:b], activated), half)
+    d_ffn_other = to_core(d_ffn_own)
+    d_ffn = jnp.concatenate([d_ffn_own, d_ffn_other], axis=0)
+    down_scatter = Scatter((d_ffn_own, d_ffn_other), activated, half)
     d_upper = (product(d_ffn, down_t) * slope.astype(F32)).astype(BF16)
+    down_scatter.near()
     up_bias_grad = jnp.sum(d_upper.astype(F32), axis=0)
-    up_part = scatter_rows(lambda a, b: row_product(normed_low[:, a:b], d_upper), half)
-    back = product_back(d_upper, up)
-    d_normed = d_second + back[:rows] + to_core(back[rows:].astype(BF16)).astype(F32)
+    back_other = to_core(product_back(d_upper[rows:], up, BF16))
+    back = product_back(d_upper[:rows], up)
+    d_normed = d_second + back + back_other.astype(F32)
+    up_scatter = Scatter((normed_own, normed_other), d_upper, half)
     norm_gain_grad = jnp.sum(d_normed * unit1, axis=0)
     norm_bias_grad = jnp.sum(d_normed, axis=0)
     d_first = norm_back(d_normed, gain1, unit1, scale1)
     d_attn_own = d_first.astype(BF16)
     out_bias_grad = jnp.sum(d_attn_own.astype(F32), axis=0)
-    d_attn = jnp.concatenate([d_attn_own, to_core(d_attn_own)], axis=0)
+    d_attn_other = to_core(d_attn_own)
+    d_attn = jnp.concatenate([d_attn_own, d_attn_other], axis=0)
+    up_scatter.near()
+    down_scatter.own()
     d_merged = product(d_attn, out_t, BF16)
-    out_part = scatter_rows(lambda a, b: row_product(d_attn[:, a:b], merged), half)
+    out_scatter = Scatter((d_attn_own, d_attn_other), merged, half)
+    if planes == 4:
+        d_merged = after(d_merged, *down_scatter.pair, out_scatter.far_first)
     d_qkv = attend_back(qkv, bias, merged, logs, d_merged)
+    out_scatter.near()
+    back_other = to_core(product_back(d_qkv[rows:], qkv_weight, BF16))
+    back = product_back(d_qkv[:rows], qkv_weight)
+    total = d_first + back + back_other.astype(F32)
+    total = to_turned(total.astype(BF16))
+    qkv_scatter = Scatter((own, other), d_qkv, half)
+    up_scatter.own()
+    out_scatter.own()
+    qkv_scatter.near()
     qkv_bias_grad = jnp.sum(d_qkv.astype(F32), axis=0, keepdims=True)
     query_bias_grad, _, value_bias_grad = (part[0] for part in unweave(qkv_bias_grad))
-    qkv_part = scatter_rows(lambda a, b: row_product(x[:, a:b], d_qkv), half)
-    back = product_back(d_qkv, qkv_weight)
-    total = d_first + back[:rows] + to_core(back[rows:].astype(BF16)).astype(F32)
-    total = to_turned(order(total.astype(BF16)))
+    down_part = down_scatter.part()
+    up_part = up_scatter.part()
+    out_part = out_scatter.part()
     total_pair = to_low(total)
     input_grad = jnp.where(
         low == 0, jnp.stack([total, total_pair]), jnp.stack([total_pair, total])
     ).astype(F32)
+    qkv_scatter.own()
+    qkv_part = qkv_scatter.part()
 
     down_grad = summed_high(down_part).T
     up_grad = summed_high(up_part)
@@ -432,7 +628,7 @@
             core == 0, jnp.concatenate([vector, empty]), jnp.concatenate([empty, vector])
         )
 
-    features = order(
+    features = (
         jnp.stack(
             [
                 out_bias_grad,

time: 625 us -> 515 us (0.82)
  Pallas kernels: 45.1 us -> 129 us
  local copies, waits for them, and re-layouts: 110 us -> 31.9 us
  matrix products: 105 us -> 49.3 us
  starting transfers between devices: 128 us -> 94.8 us
  other arithmetic: 72.7 us -> 49.7 us
    pallas_call x0 -> x18, Pallas kernels: none -> 84.1 us  [the longest x12 64.9 us: feature_call(): pl.pallas_call(kernel, grid_spec=pltpu.PrefetchScalarGridSpec(num_scalar_...]
    dot_general x20 -> x0, matrix products: 38.2 us -> none  [row_product(): lax.dot_general(left, right, (((0,), (0,)), ((), ())), preferred_element_...]
    unnamed x182 -> x120, local copies, waits for them, and re-layouts: 54.6 us -> 18.7 us
    ppermute x67, starting transfers between devices: 128 us -> 94.8 us  [send(): moved = lax.ppermute(value, AXES, pairs)]
    rev x18 -> x0, local copies, waits for them, and re-layouts: 23.8 us -> none  [turned_columns(): swapped = swapped[..., ::-1, :, :].reshape(value.shape)]
    dot_general x4, matrix products: 45.9 us -> 24.8 us  [product(): return jnp.dot(left, right, preferred_element_type=F32).astype(out)]
    select_n x18 -> x7, other arithmetic: 25 us -> 9.14 us  [send(): return jnp.where(stays, value, moved)]
    concatenate x7 -> x1, local copies, waits for them, and re-layouts: 9.62 us -> 0.01 us  [per_device(): vectors = to_first(jnp.concatenate([query_bias, value_bias, up_bias]))]
  transfers between devices with their start and end apart: 67 -> 67, of which waited for: 21 -> 24; matrix products, arithmetic and copies ran while one was open for 35% -> 17% of each run, Pallas kernels for 7% -> 25%
where the time goes in v2:
time: 515 us; the launch traced here: 507 us
  waiting for transfers between devices  150 us (29%)
  Pallas kernels  129 us (25%)
  starting transfers between devices  94.8 us (18%)
  other arithmetic  49.7 us (10%)
  matrix products  49.3 us (10%)
  local copies, waits for them, and re-layouts  31.9 us (6%)
    ppermute x67, waiting for transfers between devices, send(): moved = lax.ppermute(value, AXES, pairs)  150 us
    ppermute x67, starting transfers between devices, send(): moved = lax.ppermute(value, AXES, pairs)  94.8 us
    pallas_call x12, Pallas kernels, feature_call(): pl.pallas_call(kernel, grid_spec=pltpu.PrefetchScalarGridSpec(num_scalar_...  64.9 us
    pallas_call x1, Pallas kernels, attend_back(): pl.pallas_call(attend_back_kernel, grid=(pairs,), in_specs=[wide, pl.Bloc...  26.4 us
    dot_general x4, matrix products, product(): return jnp.dot(left, right, preferred_element_type=F32).astype(out)  24.8 us
    dot_general x8, matrix products, product_back(): lax.dot_general(left, right, (((1,), (1,)), ((), ())), preferred_element_...  24.4 us
    pallas_call x6, Pallas kernels, place(): pl.pallas_call(functools.partial(place_kernel, homes=homes, half=half, sp...  19.3 us
    unnamed x120, local copies, waits for them, and re-layouts  18.7 us
  transfers between devices with their start and end apart: 67, of which 24 were waited for; matrix products, arithmetic and copies ran while one was open for 17% of the time, Pallas kernels for 25%

profile of v2, /device:TPU:8, one launch (start us, length us, event | category | flops | bytes accessed | tf_op | source)
XLA Modules:
  0.0 506.8 jit_solution(14130851527760396811)
XLA Ops:
  11.2 6.5 %collective-permute-start.12 = (f32[3072]{0:T(1024)S(1)}, f32[3072]{0:T(1024)S(1)}, u32[]{:S(2)}, u32[]{:S(2)}) collective-permute-start(f32[3072]{0:T(1024)S(1)} %constant_dynamic-update-slice_fusion), channel_id=1, source_target_pairs={{1,4},{3,6},{4,1},{6,3},{9,12},{11,14},{12,9},{14,11},{17,20},{19,... | collective-permute-start | bytes 36872 | tf_op jit(solution)/shard_map/ppermute | solution.py:35
  37.3 8.9 %collective-permute-done.6.refs_2_ = bf16[128,2048]{1,0:T(8,128)(2,1)} collective-permute-done((bf16[128,2048]{1,0:T(8,128)(2,1)S(1)}, bf16[128,2048]{1,0:T(8,128)(2,1)}, u32[]{:S(2)}, u32[]{:S(2)}) %collective-permute-start.6) | collective-permute-done | bytes 524320 | tf_op jit(solution)/shard_map/ppermute | solution.py:35
  47.8 7.8 %collective-permute-done.8.refs_5_ = bf16[128,2048]{1,0:T(8,128)(2,1)S(1)} collective-permute-done((bf16[128,2048]{1,0:T(8,128)(2,1)}, bf16[128,2048]{1,0:T(8,128)(2,1)S(1)}, u32[]{:S(2)}, u32[]{:S(2)}) %collective-permute-start.8) | collective-permute-done | bytes 524320 | tf_op jit(solution)/shard_map/ppermute | solution.py:35
  71.1 6.5 %collective-permute-done.9.refs_1_ = bf16[128,2048]{1,0:T(8,128)(2,1)} collective-permute-done((bf16[128,2048]{1,0:T(8,128)(2,1)}, bf16[128,2048]{1,0:T(8,128)(2,1)}, u32[]{:S(2)}, u32[]{:S(2)}) %collective-permute-start.9) | collective-permute-done | bytes 524320 | tf_op jit(solution)/shard_map/ppermute | solution.py:35
  82.6 5.0 multiply_convert_fusion.2.qkv_ref
  87.7 18.6 %attend.1 = (bf16[1024,512]{1,0:T(8,128)(2,1)}, f32[1024,512]{1,0:T(8,128)}) custom-call(bf16[1024,1536]{1,0:T(8,128)(2,1)} %multiply_convert_fusion.2.qkv_ref, f32[1,1024]{1,0:T(1,128)} %compare_select_fusion.bias_ref), custom_call_target="tpu_custom_call" | custom-call | flops 33554432 | bytes 524288 | tf_op jit(solution)/shard_map/attend/pallas_call | solution.py:353
  108.8 10.3 %collective-permute-done.16.refs_3_ = bf16[128,4096]{1,0:T(8,128)(2,1)} collective-permute-done((bf16[128,4096]{1,0:T(8,128)(2,1)}, bf16[128,4096]{1,0:T(8,128)(2,1)}, u32[]{:S(2)}, u32[]{:S(2)}) %collective-permute-start.16) | collective-permute-done | bytes 1048608 | tf_op jit(solution)/shard_map/ppermute | solution.py:35
  147.1 5.4 %collective-permute-done.21.refs_0_ = bf16[128,2048]{1,0:T(8,128)(2,1)} collective-permute-done((bf16[128,2048]{1,0:T(8,128)(2,1)}, bf16[128,2048]{1,0:T(8,128)(2,1)}, u32[]{:S(2)}, u32[]{:S(2)}) %collective-permute-start.21) | collective-permute-done | bytes 524320 | tf_op jit(solution)/shard_map/ppermute | solution.py:35
  157.3 10.6 %fusion.4 = (bf16[1024,2048]{1,0:T(8,128)(2,1)S(1)}, bf16[1024,2048]{1,0:T(8,128)(2,1)S(1)}) fusion(f32[2048]{0:T(1024)S(1)} %slice-done, bf16[1024,2048]{1,0:T(8,128)(2,1)} %place.9, bf16[512,1024]{1,0:T(8,128)(2,1)} %collective-permute-done.20.other_ref.x_other.y_other, bf16[512,1024]{1,0:T(8,128)(2,1)S(1)} %fusion.28.own_ref.x_own.y_own), kind=kOutput, calls=%fused_computation.5 | convolution fusion | flops 4324327424 | bytes 14688256 | tf_op jit(solution)/shard_map/dot_general | solution.py:308
  181.2 5.8 %convert_reduce_fusion = (f32[2048]{0:T(1024)S(1)}, bf16[1024,2048]{1,0:T(8,128)(2,1)S(1)}) fusion(bf16[1024,2048]{1,0:T(8,128)(2,1)S(1)} %get-tuple-element.68, bf16[1024,2048]{1,0:T(8,128)(2,1)S(1)} %copy-done.15, bf16[512,1024]{1,0:T(8,128)(2,1)S(1)} %collective-permute-done.28.other_ref.x_other.y_other, ...), kind=kOutput, calls=%fused_computation.6 | convolution fusion | flops 4309645312 | bytes 14688256 | tf_op jit(solution)/shard_map/dot_general | solution.py:308
  191.4 5.8 %far_rows.4 = (bf16[128,2048]{1,0:T(8,128)(2,1)}, bf16[128,2048]{1,0:T(8,128)(2,1)}) custom-call(s32[2]{0:T(128)} %pad_add_fusion.at_ref, bf16[512,1024]{1,0:T(8,128)(2,1)} %copy-done.8, bf16[512,1024]{1,0:T(8,128)(2,1)} %copy-done.13, bf16[1024,2048]{1,0:T(8,128)(2,1)} %copy-done.6), custom_call_target="tpu_custom_call" | custom-call | flops 2097152 | bytes 2097152 | tf_op jit(solution)/shard_map/far_rows/pallas_call | solution.py:228
  199.3 6.5 %fusion.7 = f32[512,1024]{1,0:T(8,128)} fusion(bf16[1024,2048]{1,0:T(8,128)(2,1)} %place.9, bf16[1024,2048]{1,0:T(8,128)(2,1)} %copy-done.5), kind=kOutput, calls=%fused_computation.14 | convolution fusion | flops 2147483648 | bytes 8388608 | tf_op jit(solution)/shard_map/dot_general | solution.py:312
  205.9 5.7 %collective-permute-done.31.first_ref = bf16[128,2048]{1,0:T(8,128)(2,1)} collective-permute-done((bf16[128,2048]{1,0:T(8,128)(2,1)}, bf16[128,2048]{1,0:T(8,128)(2,1)}, u32[]{:S(2)}, u32[]{:S(2)}) %collective-permute-start.31) | collective-permute-done | bytes 524320 | tf_op jit(solution)/shard_map/ppermute | solution.py:35
  212.8 6.9 %near_rows.4 = (bf16[256,2048]{1,0:T(8,128)(2,1)}, bf16[256,2048]{1,0:T(8,128)(2,1)}) custom-call(s32[2]{0:T(128)} %pad_add_fusion.at_ref, bf16[512,1024]{1,0:T(8,128)(2,1)} %copy-done.8, bf16[512,1024]{1,0:T(8,128)(2,1)} %copy-done.13, bf16[512,1024]{1,0:T(8,128)(2,1)} %copy-done.8, bf16[512,1024]{1,0:T(8,128)(2,1)} %copy-done.13, ...), custom_call_target="tpu_custom_call" | custom-call | flops 2097152 | bytes 2097152 | tf_op jit(solution)/shard_map/near_rows/pallas_call | solution.py:228
  220.7 4.9 multiply_reduce_fusion.1
  227.6 5.7 %far_rows.7 = (bf16[128,2048]{1,0:T(8,128)(2,1)}, bf16[128,2048]{1,0:T(8,128)(2,1)}) custom-call(s32[2]{0:T(128)} %pad_add_fusion.at_ref, bf16[512,1024]{1,0:T(8,128)(2,1)} %copy-done.7, bf16[512,1024]{1,0:T(8,128)(2,1)} %collective-permute-done.20.other_ref.x_other.y_other, bf16[1024,2048]{1,0:T(8,128)(2,1)} %copy-done.5), custom_call_target="tpu_custom_call" | custom-call | flops 2097152 | bytes 2097152 | tf_op jit(solution)/shard_map/far_rows/pallas_call | solution.py:228
  236.3 19.1 %collective-permute-done.52.first_ref = bf16[128,2048]{1,0:T(8,128)(2,1)S(1)} collective-permute-done((bf16[128,2048]{1,0:T(8,128)(2,1)}, bf16[128,2048]{1,0:T(8,128)(2,1)S(1)}, u32[]{:S(2)}, u32[]{:S(2)}) %collective-permute-start.52) | collective-permute-done | bytes 524320 | tf_op jit(solution)/shard_map/ppermute | solution.py:35
  257.0 6.9 %near_rows.7 = (bf16[256,2048]{1,0:T(8,128)(2,1)}, bf16[256,2048]{1,0:T(8,128)(2,1)}) custom-call(s32[2]{0:T(128)} %pad_add_fusion.at_ref, bf16[512,1024]{1,0:T(8,128)(2,1)} %copy-done.7, bf16[512,1024]{1,0:T(8,128)(2,1)} %collective-permute-done.20.other_ref.x_other.y_other, bf16[512,1024]{1,0:T(8,128)(2,1)} %copy-done.7, ...), custom_call_target="tpu_custom_call" | custom-call | flops 2097152 | bytes 2097152 | tf_op jit(solution)/shard_map/near_rows/pallas_call | solution.py:228
  267.7 6.2 %own_rows.4 = (bf16[128,2048]{1,0:T(8,128)(2,1)}, bf16[128,2048]{1,0:T(8,128)(2,1)}) custom-call(s32[2]{0:T(128)} %pad_add_fusion.at_ref, bf16[512,1024]{1,0:T(8,128)(2,1)} %copy-done.8, bf16[512,1024]{1,0:T(8,128)(2,1)} %copy-done.13, bf16[1024,2048]{1,0:T(8,128)(2,1)} %copy-done.6, bf16[256,2048]{1,0:T(8,128)(2,1)} %collective-permute-done.33.x_ref, ...), custom_call_target="tpu_custom_call" | custom-call | flops 2097152 | bytes 2097152 | tf_op jit(solution)/shard_map/own_rows/pallas_call | solution.py:228
  283.2 7.9 %collective-permute-done.35.first_ref = bf16[128,512]{1,0:T(8,128)(2,1)S(1)} collective-permute-done((bf16[128,512]{1,0:T(8,128)(2,1)}, bf16[128,512]{1,0:T(8,128)(2,1)S(1)}, u32[]{:S(2)}, u32[]{:S(2)}) %collective-permute-start.35) | collective-permute-done | bytes 131104 | tf_op jit(solution)/shard_map/ppermute | solution.py:35
  291.1 26.4 %attend_back.1.right_ref = bf16[1024,1536]{1,0:T(8,128)(2,1)} custom-call(bf16[1024,1536]{1,0:T(8,128)(2,1)} %multiply_convert_fusion.2.qkv_ref, f32[1,1024]{1,0:T(1,128)} %compare_select_fusion.bias_ref, bf16[1024,512]{1,0:T(8,128)(2,1)} %get-tuple-element.65.right_ref.out_ref, f32[1024,512]{1,0:T(8,128)} %get-tuple-element.69.log_ref, ...), custom_call_target="tpu_custom_call" | custom-call | flops 83886080 | bytes 524288 | tf_op jit(solution)/shard_map/attend_back/pallas_call | solution.py:421
  322.2 6.2 %own_rows.7 = (bf16[128,2048]{1,0:T(8,128)(2,1)}, bf16[128,2048]{1,0:T(8,128)(2,1)}) custom-call(s32[2]{0:T(128)} %pad_add_fusion.at_ref, bf16[512,1024]{1,0:T(8,128)(2,1)} %copy-done.7, bf16[512,1024]{1,0:T(8,128)(2,1)} %collective-permute-done.20.other_ref.x_other.y_other, bf16[1024,2048]{1,0:T(8,128)(2,1)} %copy-done.5, ...), custom_call_target="tpu_custom_call" | custom-call | flops 2097152 | bytes 2097152 | tf_op jit(solution)/shard_map/own_rows/pallas_call | solution.py:228
  347.3 6.6 %collective-permute-start.66 = (f32[12288]{0:T(1024)S(1)}, f32[12288]{0:T(1024)S(1)}, u32[]{:S(2)}, u32[]{:S(2)}) collective-permute-start(f32[12288]{0:T(1024)S(1)} %add.259), channel_id=1, source_target_pairs={{0,2},{1,3},{2,0},{3,1},{4,6},{5,7},{6,4},{7,5},{8,10},{9,11},{10,... | collective-permute-start | bytes 147464 | tf_op jit(solution)/shard_map/ppermute | solution.py:35
  362.2 5.2 %far_rows.6 = (bf16[128,1536]{1,0:T(8,128)(2,1)}, bf16[128,1536]{1,0:T(8,128)(2,1)}) custom-call(s32[2]{0:T(128)} %pad_add_fusion.at_ref, bf16[512,1024]{1,0:T(8,128)(2,1)} %copy-done.4, bf16[512,1024]{1,0:T(8,128)(2,1)} %copy-done.11, bf16[1024,1536]{1,0:T(8,128)(2,1)} %attend_back.1.right_ref), custom_call_target="tpu_custom_call" | custom-call | flops 1572864 | bytes 1572864 | tf_op jit(solution)/shard_map/far_rows/pallas_call | solution.py:228
  370.3 5.5 %fusion.31 = f32[512,1024]{1,0:T(8,128)} fusion(bf16[1024,1536]{1,0:T(8,128)(2,1)} %get-tuple-element.60, bf16[1024,1536]{1,0:T(8,128)(2,1)} %attend_back.1.right_ref), kind=kOutput, calls=%fused_computation.61 | convolution fusion | flops 1610612736 | bytes 6815744 | tf_op jit(solution)/shard_map/dot_general | solution.py:312
  387.8 6.0 %near_rows.5 = (bf16[256,1536]{1,0:T(8,128)(2,1)}, bf16[256,1536]{1,0:T(8,128)(2,1)}) custom-call(s32[2]{0:T(128)} %pad_add_fusion.at_ref, bf16[512,1024]{1,0:T(8,128)(2,1)} %copy-done.4, bf16[512,1024]{1,0:T(8,128)(2,1)} %copy-done.11, bf16[512,1024]{1,0:T(8,128)(2,1)} %copy-done.4, bf16[512,1024]{1,0:T(8,128)(2,1)} %copy-done.11, ...), custom_call_target="tpu_custom_call" | custom-call | flops 1572864 | bytes 1572864 | tf_op jit(solution)/shard_map/near_rows/pallas_call | solution.py:228
  402.3 22.4 %collective-permute-done.61 = bf16[128,2048]{1,0:T(8,128)(2,1)} collective-permute-done((bf16[128,2048]{1,0:T(8,128)(2,1)}, bf16[128,2048]{1,0:T(8,128)(2,1)}, u32[]{:S(2)}, u32[]{:S(2)}) %collective-permute-start.61) | collective-permute-done | bytes 524320 | tf_op jit(solution)/shard_map/ppermute | solution.py:35
  428.1 5.6 %own_rows.5 = (bf16[128,1536]{1,0:T(8,128)(2,1)}, bf16[128,1536]{1,0:T(8,128)(2,1)}) custom-call(s32[2]{0:T(128)} %pad_add_fusion.at_ref, bf16[512,1024]{1,0:T(8,128)(2,1)} %copy-done.4, bf16[512,1024]{1,0:T(8,128)(2,1)} %copy-done.11, bf16[1024,1536]{1,0:T(8,128)(2,1)} %attend_back.1.right_ref, bf16[256,1536]{1,0:T(8,128)(2,1)} %collective-permute-done.41.x_ref, ...), custom_call_target="tpu_custom_call" | custom-call | flops 1572864 | bytes 1572864 | tf_op jit(solution)/shard_map/own_rows/pallas_call | solution.py:228
  437.9 15.0 %collective-permute-start.44 = (bf16[128,1536]{1,0:T(8,128)(2,1)}, bf16[128,1536]{1,0:T(8,128)(2,1)}, u32[]{:S(2)}, u32[]{:S(2)}) collective-permute-start(bf16[128,1536]{1,0:T(8,128)(2,1)} %get-tuple-element.83), channel_id=1, source_target_pairs={{0,4},{1,0},{2,6},{3,2},{4,5},{5,1},{6,7},{7,3},{8,12},{9,8},{10,1... | collective-permute-start | bytes 1179656 | tf_op jit(solution)/shard_map/ppermute | solution.py:35
  456.3 11.6 %collective-permute-done.44 = bf16[128,1536]{1,0:T(8,128)(2,1)} collective-permute-done((bf16[128,1536]{1,0:T(8,128)(2,1)}, bf16[128,1536]{1,0:T(8,128)(2,1)}, u32[]{:S(2)}, u32[]{:S(2)}) %collective-permute-start.44) | collective-permute-done | bytes 393248 | tf_op jit(solution)/shard_map/ppermute | solution.py:35
  477.1 10.0 %collective-permute-done.45 = bf16[128,1536]{1,0:T(8,128)(2,1)S(1)} collective-permute-done((bf16[128,1536]{1,0:T(8,128)(2,1)S(1)}, bf16[128,1536]{1,0:T(8,128)(2,1)S(1)}, u32[]{:S(2)}, u32[]{:S(2)}) %collective-permute-start.45) | collective-permute-done | bytes 393248 | tf_op jit(solution)/shard_map/ppermute | solution.py:35
  493.8 8.7 %collective-permute-done.38 = bf16[512,1024]{1,0:T(8,128)(2,1)} collective-permute-done((bf16[512,1024]{1,0:T(8,128)(2,1)S(1)}, bf16[512,1024]{1,0:T(8,128)(2,1)}, u32[]{:S(2)}, u32[]{:S(2)}) %collective-permute-start.38) | collective-permute-done | bytes 1048608 | tf_op jit(solution)/shard_map/ppermute | solution.py:35
  (331 shorter events, 214.6 us)
Async XLA Ops:
  9.5 25.5 %collective-permute-start = (bf16[512,1024]{1,0:T(8,128)(2,1)}, bf16[512,1024]{1,0:T(8,128)(2,1)}, u32[]{:S(2)}, u32[]{:S(2)}) collective-permute-start(bf16[512,1024]{1,0:T(8,128)(2,1)} %dynamic-slice_bitcast_fusion.1), channel_id=1, source_target_pairs={{2,4},{3,5},{4,2},{5,3},{10,12},{11,13},{12,10},{13,11},{18,20},{1... | collective-permute-start | bytes 3145736 | tf_op jit(solution)/shard_map/ppermute | solution.py:35
  11.2 23.2 %collective-permute-start.12 = (f32[3072]{0:T(1024)S(1)}, f32[3072]{0:T(1024)S(1)}, u32[]{:S(2)}, u32[]{:S(2)}) collective-permute-start(f32[3072]{0:T(1024)S(1)} %constant_dynamic-update-slice_fusion), channel_id=1, source_target_pairs={{1,4},{3,6},{4,1},{6,3},{9,12},{11,14},{12,9},{14,11},{17,20},{19,... | collective-permute-start | bytes 36872 | tf_op jit(solution)/shard_map/ppermute | solution.py:35
  26.1 36.3 %collective-permute-start.4 = (bf16[128,4096]{1,0:T(8,128)(2,1)}, bf16[128,4096]{1,0:T(8,128)(2,1)}, u32[]{:S(2)}, u32[]{:S(2)}) collective-permute-start(bf16[128,4096]{1,0:T(8,128)(2,1)} %pad_maximum_fusion.1), channel_id=1, source_target_pairs={{1,4},{3,6},{4,1},{6,3},{9,12},{11,14},{12,9},{14,11},{17,20},{19,... | collective-permute-start | bytes 3145736 | tf_op jit(solution)/shard_map/ppermute | solution.py:35
  35.0 22.4 %collective-permute-start.10 = (bf16[128,2048]{1,0:T(8,128)(2,1)}, bf16[128,2048]{1,0:T(8,128)(2,1)}, u32[]{:S(2)}, u32[]{:S(2)}) collective-permute-start(bf16[128,2048]{1,0:T(8,128)(2,1)} %collective-permute-done.3.refs_1_), channel_id=1, source_target_pairs={{0,8},{1,9},{2,10},{3,11},{4,12},{5,13},{6,14},{7,15},{8,0},{9,1},... | collective-permute-start | bytes 1572872 | tf_op jit(solution)/shard_map/ppermute | solution.py:35
  47.8 32.6 %collective-permute-start.1 = (bf16[512,1024]{1,0:T(8,128)(2,1)S(1)}, bf16[512,1024]{1,0:T(8,128)(2,1)S(1)}, u32[]{:S(2)}, u32[]{:S(2)}) collective-permute-start(bf16[512,1024]{1,0:T(8,128)(2,1)S(1)} %broadcast_select_fusion.4.own_ref.x_own.y_own), channel_id=1, source_target_pairs={{0,4},{1,5},{2,6},{3,7},{4,0},{5,1},{6,2},{7,3},{8,12},{9,13},{10,... | collective-permute-start | bytes 3145736 | tf_op jit(solution)/shard_map/ppermute | solution.py:35
  55.7 50.6 %collective-permute-start.14 = (bf16[512,1024]{1,0:T(8,128)(2,1)}, bf16[512,1024]{1,0:T(8,128)(2,1)}, u32[]{:S(2)}, u32[]{:S(2)}) collective-permute-start(bf16[512,1024]{1,0:T(8,128)(2,1)} %dynamic-slice_bitcast_fusion), channel_id=1, source_target_pairs={{2,4},{3,5},{4,2},{5,3},{10,12},{11,13},{12,10},{13,11},{18,20},{1... | collective-permute-start | bytes 3145736 | tf_op jit(solution)/shard_map/ppermute | solution.py:35
  64.4 44.4 %collective-permute-start.15 = (bf16[128,4096]{1,0:T(8,128)(2,1)S(1)}, bf16[128,4096]{1,0:T(8,128)(2,1)}, u32[]{:S(2)}, u32[]{:S(2)}) collective-permute-start(bf16[128,4096]{1,0:T(8,128)(2,1)S(1)} %broadcast_select_fusion.refs_0_), channel_id=1, source_target_pairs={{0,8},{1,9},{2,10},{3,11},{4,12},{5,13},{6,14},{7,15},{8,0},{9,1},... | collective-permute-start | bytes 3145736 | tf_op jit(solution)/shard_map/ppermute | solution.py:35
  69.6 39.1 %collective-permute-start.17 = (bf16[128,4096]{1,0:T(8,128)(2,1)S(1)}, bf16[128,4096]{1,0:T(8,128)(2,1)}, u32[]{:S(2)}, u32[]{:S(2)}) collective-permute-start(bf16[128,4096]{1,0:T(8,128)(2,1)S(1)} %broadcast_select_fusion.refs_0_), channel_id=1, source_target_pairs={{0,16},{1,17},{2,18},{3,19},{4,20},{5,21},{6,22},{7,23},{8,24},{9,... | collective-permute-start | bytes 3145736 | tf_op jit(solution)/shard_map/ppermute | solution.py:35
  77.6 41.4 %collective-permute-start.16 = (bf16[128,4096]{1,0:T(8,128)(2,1)}, bf16[128,4096]{1,0:T(8,128)(2,1)}, u32[]{:S(2)}, u32[]{:S(2)}) collective-permute-start(bf16[128,4096]{1,0:T(8,128)(2,1)} %collective-permute-done.5.refs_1_), channel_id=1, source_target_pairs={{0,8},{1,9},{2,10},{3,11},{4,12},{5,13},{6,14},{7,15},{8,0},{9,1},... | collective-permute-start | bytes 3145736 | tf_op jit(solution)/shard_map/ppermute | solution.py:35
  80.4 38.6 %collective-permute-start.18 = (bf16[128,4096]{1,0:T(8,128)(2,1)}, bf16[128,4096]{1,0:T(8,128)(2,1)}, u32[]{:S(2)}, u32[]{:S(2)}) collective-permute-start(bf16[128,4096]{1,0:T(8,128)(2,1)} %collective-permute-done.5.refs_1_), channel_id=1, source_target_pairs={{0,16},{1,17},{2,18},{3,19},{4,20},{5,21},{6,22},{7,23},{8,24},{9,... | collective-permute-start | bytes 3145736 | tf_op jit(solution)/shard_map/ppermute | solution.py:35
  124.2 33.0 %collective-permute-start.20 = (bf16[512,1024]{1,0:T(8,128)(2,1)S(1)}, bf16[512,1024]{1,0:T(8,128)(2,1)}, u32[]{:S(2)}, u32[]{:S(2)}) collective-permute-start(bf16[512,1024]{1,0:T(8,128)(2,1)S(1)} %fusion.28.own_ref.x_own.y_own), channel_id=1, source_target_pairs={{0,4},{1,5},{2,6},{3,7},{4,0},{5,1},{6,2},{7,3},{8,12},{9,13},{10,... | collective-permute-start | bytes 3145736 | tf_op jit(solution)/shard_map/ppermute | solution.py:35
  130.3 22.2 %collective-permute-start.21 = (bf16[128,2048]{1,0:T(8,128)(2,1)}, bf16[128,2048]{1,0:T(8,128)(2,1)}, u32[]{:S(2)}, u32[]{:S(2)}) collective-permute-start(bf16[128,2048]{1,0:T(8,128)(2,1)} %get-tuple-element.152), channel_id=1, source_target_pairs={{0,16},{1,17},{2,18},{3,19},{4,20},{5,21},{6,22},{7,23},{8,24},{9,... | collective-permute-start | bytes 1572872 | tf_op jit(solution)/shard_map/ppermute | solution.py:35
  131.8 23.2 %collective-permute-start.22 = (bf16[128,2048]{1,0:T(8,128)(2,1)}, bf16[128,2048]{1,0:T(8,128)(2,1)}, u32[]{:S(2)}, u32[]{:S(2)}) collective-permute-start(bf16[128,2048]{1,0:T(8,128)(2,1)} %get-tuple-element.150), channel_id=1, source_target_pairs={{0,8},{1,9},{2,10},{3,11},{4,12},{5,13},{6,14},{7,15},{8,0},{9,1},... | collective-permute-start | bytes 1572872 | tf_op jit(solution)/shard_map/ppermute | solution.py:35
  190.4 30.3 %collective-permute-start.29 = (bf16[512,1024]{1,0:T(8,128)(2,1)}, bf16[512,1024]{1,0:T(8,128)(2,1)}, u32[]{:S(2)}, u32[]{:S(2)}) collective-permute-start(bf16[512,1024]{1,0:T(8,128)(2,1)} %fusion.42), channel_id=1, source_target_pairs={{0,4},{1,5},{2,6},{3,7},{4,0},{5,1},{6,2},{7,3},{8,12},{9,13},{10,... | collective-permute-start | bytes 3145736 | tf_op jit(solution)/shard_map/ppermute | solution.py:35
  219.6 46.4 %collective-permute-start.33 = (bf16[256,2048]{1,0:T(8,128)(2,1)}, bf16[256,2048]{1,0:T(8,128)(2,1)}, u32[]{:S(2)}, u32[]{:S(2)}) collective-permute-start(bf16[256,2048]{1,0:T(8,128)(2,1)} %get-tuple-element.72), channel_id=1, source_target_pairs={{0,8},{1,9},{2,10},{3,11},{4,12},{5,13},{6,14},{7,15},{8,0},{9,1},... | collective-permute-start | bytes 3145736 | tf_op jit(solution)/shard_map/ppermute | solution.py:35
  220.2 47.5 %collective-permute-start.34 = (bf16[256,2048]{1,0:T(8,128)(2,1)}, bf16[256,2048]{1,0:T(8,128)(2,1)}, u32[]{:S(2)}, u32[]{:S(2)}) collective-permute-start(bf16[256,2048]{1,0:T(8,128)(2,1)} %get-tuple-element.73), channel_id=1, source_target_pairs={{0,16},{1,17},{2,18},{3,19},{4,20},{5,21},{6,22},{7,23},{8,24},{9,... | collective-permute-start | bytes 3145736 | tf_op jit(solution)/shard_map/ppermute | solution.py:35
  227.6 46.3 %collective-permute-start.30 = (bf16[512,1024]{1,0:T(8,128)(2,1)S(1)}, bf16[512,1024]{1,0:T(8,128)(2,1)S(1)}, u32[]{:S(2)}, u32[]{:S(2)}) collective-permute-start(bf16[512,1024]{1,0:T(8,128)(2,1)S(1)} %get-tuple-element.140.own_ref.x_own.y_own), channel_id=1, source_target_pairs={{0,4},{1,5},{2,6},{3,7},{4,0},{5,1},{6,2},{7,3},{8,12},{9,13},{10,... | collective-permute-start | bytes 3145736 | tf_op jit(solution)/shard_map/ppermute | solution.py:35
  263.9 58.1 %collective-permute-start.54 = (bf16[256,2048]{1,0:T(8,128)(2,1)}, bf16[256,2048]{1,0:T(8,128)(2,1)}, u32[]{:S(2)}, u32[]{:S(2)}) collective-permute-start(bf16[256,2048]{1,0:T(8,128)(2,1)} %get-tuple-element.91), channel_id=1, source_target_pairs={{0,8},{1,9},{2,10},{3,11},{4,12},{5,13},{6,14},{7,15},{8,0},{9,1},... | collective-permute-start | bytes 3145736 | tf_op jit(solution)/shard_map/ppermute | solution.py:35
  265.4 56.7 %collective-permute-start.55 = (bf16[256,2048]{1,0:T(8,128)(2,1)}, bf16[256,2048]{1,0:T(8,128)(2,1)}, u32[]{:S(2)}, u32[]{:S(2)}) collective-permute-start(bf16[256,2048]{1,0:T(8,128)(2,1)} %get-tuple-element.92), channel_id=1, source_target_pairs={{0,16},{1,17},{2,18},{3,19},{4,20},{5,21},{6,22},{7,23},{8,24},{9,... | collective-permute-start | bytes 3145736 | tf_op jit(solution)/shard_map/ppermute | solution.py:35
  266.1 66.2 %collective-permute-start.26 = (bf16[512,1024]{1,0:T(8,128)(2,1)}, bf16[512,1024]{1,0:T(8,128)(2,1)}, u32[]{:S(2)}, u32[]{:S(2)}) collective-permute-start(bf16[512,1024]{1,0:T(8,128)(2,1)} %get-tuple-element.149), channel_id=1, source_target_pairs={{2,4},{3,5},{4,2},{5,3},{10,12},{11,13},{12,10},{13,11},{18,20},{1... | collective-permute-start | bytes 3145736 | tf_op jit(solution)/shard_map/ppermute | solution.py:35
  347.3 23.0 %collective-permute-start.66 = (f32[12288]{0:T(1024)S(1)}, f32[12288]{0:T(1024)S(1)}, u32[]{:S(2)}, u32[]{:S(2)}) collective-permute-start(f32[12288]{0:T(1024)S(1)} %add.259), channel_id=1, source_target_pairs={{0,2},{1,3},{2,0},{3,1},{4,6},{5,7},{6,4},{7,5},{8,10},{9,11},{10,... | collective-permute-start | bytes 147464 | tf_op jit(solution)/shard_map/ppermute | solution.py:35
  370.3 27.7 %collective-permute-start.36 = (bf16[512,1024]{1,0:T(8,128)(2,1)}, bf16[512,1024]{1,0:T(8,128)(2,1)}, u32[]{:S(2)}, u32[]{:S(2)}) collective-permute-start(bf16[512,1024]{1,0:T(8,128)(2,1)} %fusion.33), channel_id=1, source_target_pairs={{0,4},{1,5},{2,6},{3,7},{4,0},{5,1},{6,2},{7,3},{8,12},{9,13},{10,... | collective-permute-start | bytes 3145736 | tf_op jit(solution)/shard_map/ppermute | solution.py:35
  387.0 87.0 %collective-permute-start.27 = (bf16[512,1024]{1,0:T(8,128)(2,1)S(1)}, bf16[512,1024]{1,0:T(8,128)(2,1)}, u32[]{:S(2)}, u32[]{:S(2)}) collective-permute-start(bf16[512,1024]{1,0:T(8,128)(2,1)S(1)} %broadcast_select_fusion.2), channel_id=1, source_target_pairs={{0,1},{1,0},{2,3},{3,2},{4,5},{5,4},{6,7},{7,6},{8,9},{9,8},{10,11... | collective-permute-start | bytes 3145736 | tf_op jit(solution)/shard_map/ppermute | solution.py:35
  387.4 37.2 %collective-permute-start.61 = (bf16[128,2048]{1,0:T(8,128)(2,1)}, bf16[128,2048]{1,0:T(8,128)(2,1)}, u32[]{:S(2)}, u32[]{:S(2)}) collective-permute-start(bf16[128,2048]{1,0:T(8,128)(2,1)} %add_convert_fusion.2), channel_id=1, source_target_pairs={{0,2},{1,3},{2,0},{3,1},{4,6},{5,7},{6,4},{7,5},{8,10},{9,11},{10,... | collective-permute-start | bytes 1572872 | tf_op jit(solution)/shard_map/ppermute | solution.py:35
  393.8 44.1 %collective-permute-start.58 = (bf16[128,2048]{1,0:T(8,128)(2,1)}, bf16[128,2048]{1,0:T(8,128)(2,1)}, u32[]{:S(2)}, u32[]{:S(2)}) collective-permute-start(bf16[128,2048]{1,0:T(8,128)(2,1)} %add_convert_fusion.3), channel_id=1, source_target_pairs={{0,2},{1,3},{2,0},{3,1},{4,6},{5,7},{6,4},{7,5},{8,10},{9,11},{10,... | collective-permute-start | bytes 1572872 | tf_op jit(solution)/shard_map/ppermute | solution.py:35
  396.5 31.1 %collective-permute-start.41 = (bf16[256,1536]{1,0:T(8,128)(2,1)}, bf16[256,1536]{1,0:T(8,128)(2,1)}, u32[]{:S(2)}, u32[]{:S(2)}) collective-permute-start(bf16[256,1536]{1,0:T(8,128)(2,1)} %get-tuple-element.80), channel_id=1, source_target_pairs={{0,8},{1,9},{2,10},{3,11},{4,12},{5,13},{6,14},{7,15},{8,0},{9,1},... | collective-permute-start | bytes 2359304 | tf_op jit(solution)/shard_map/ppermute | solution.py:35
  398.0 30.1 %collective-permute-start.42 = (bf16[256,1536]{1,0:T(8,128)(2,1)}, bf16[256,1536]{1,0:T(8,128)(2,1)}, u32[]{:S(2)}, u32[]{:S(2)}) collective-permute-start(bf16[256,1536]{1,0:T(8,128)(2,1)} %get-tuple-element.81), channel_id=1, source_target_pairs={{0,16},{1,17},{2,18},{3,19},{4,20},{5,21},{6,22},{7,23},{8,24},{9,... | collective-permute-start | bytes 2359304 | tf_op jit(solution)/shard_map/ppermute | solution.py:35
  424.7 44.6 %collective-permute-start.37 = (bf16[512,1024]{1,0:T(8,128)(2,1)}, bf16[512,1024]{1,0:T(8,128)(2,1)}, u32[]{:S(2)}, u32[]{:S(2)}) collective-permute-start(bf16[512,1024]{1,0:T(8,128)(2,1)} %add_convert_fusion), channel_id=1, source_target_pairs={{2,4},{3,5},{4,2},{5,3},{10,12},{11,13},{12,10},{13,11},{18,20},{1... | collective-permute-start | bytes 3145736 | tf_op jit(solution)/shard_map/ppermute | solution.py:35
  427.6 45.5 %collective-permute-start.51 = (bf16[128,512]{1,0:T(8,128)(2,1)S(1)}, bf16[128,512]{1,0:T(8,128)(2,1)S(1)}, u32[]{:S(2)}, u32[]{:S(2)}) collective-permute-start(bf16[128,512]{1,0:T(8,128)(2,1)S(1)} %add_convert_fusion.5), channel_id=1, source_target_pairs={{0,2},{1,3},{2,0},{3,1},{4,6},{5,7},{6,4},{7,5},{8,10},{9,11},{10,... | collective-permute-start | bytes 393224 | tf_op jit(solution)/shard_map/ppermute | solution.py:35
  433.7 22.7 %collective-permute-start.43 = (bf16[128,1536]{1,0:T(8,128)(2,1)}, bf16[128,1536]{1,0:T(8,128)(2,1)}, u32[]{:S(2)}, u32[]{:S(2)}) collective-permute-start(bf16[128,1536]{1,0:T(8,128)(2,1)} %get-tuple-element.82), channel_id=1, source_target_pairs={{1,4},{3,6},{4,1},{6,3},{9,12},{11,14},{12,9},{14,11},{17,20},{19,... | collective-permute-start | bytes 1179656 | tf_op jit(solution)/shard_map/ppermute | solution.py:35
  437.9 30.0 %collective-permute-start.44 = (bf16[128,1536]{1,0:T(8,128)(2,1)}, bf16[128,1536]{1,0:T(8,128)(2,1)}, u32[]{:S(2)}, u32[]{:S(2)}) collective-permute-start(bf16[128,1536]{1,0:T(8,128)(2,1)} %get-tuple-element.83), channel_id=1, source_target_pairs={{0,4},{1,0},{2,6},{3,2},{4,5},{5,1},{6,7},{7,3},{8,12},{9,8},{10,1... | collective-permute-start | bytes 1179656 | tf_op jit(solution)/shard_map/ppermute | solution.py:35
  470.6 31.8 %collective-permute-start.38 = (bf16[512,1024]{1,0:T(8,128)(2,1)S(1)}, bf16[512,1024]{1,0:T(8,128)(2,1)}, u32[]{:S(2)}, u32[]{:S(2)}) collective-permute-start(bf16[512,1024]{1,0:T(8,128)(2,1)S(1)} %broadcast_select_fusion.1), channel_id=1, source_target_pairs={{0,1},{1,0},{2,3},{3,2},{4,5},{5,4},{6,7},{7,6},{8,9},{9,8},{10,11... | collective-permute-start | bytes 3145736 | tf_op jit(solution)/shard_map/ppermute | solution.py:35
  (90 other events, 1148.7 us)

commit v3 on v2

--- a/solution.py
+++ b/solution.py
@@ -154,154 +154,214 @@
         self.over_x = (to_x(first), to_x(second))
         self.over_y = (to_y(first), to_y(second))
 
-    def far(self, key, spans):
+    def far(self, spans):
+        self.spans = spans
+        self.sent = []
+        for group in spans if self.planes == 4 else ():
+            start, stop = group[0][0], group[-1][0] + group[-1][1]
+            first, second = self.over_x[0], self.over_y[1]
+            if stop - start != self.width:
+                first, second = first[:, start:stop], second[:, start:stop]
+            first, second = to_y(first), to_x(second)
+            self.sent.append((start, first, second))
+
+    def last(self):
+        return self.sent[-1][1:] if self.planes == 4 else ()
+
+    def placed(self, key, index):
+        group = self.spans[index]
         if self.planes != 4:
-            return [[self.whole[:, a : a + n] for a, n in group] for group in spans]
+            return [self.whole[:, a : a + n] for a, n in group]
         half = self.half
-        sent = []
-        for group in spans:
-            start, stop = group[0][0], group[-1][0] + group[-1][1]
-            first = to_y(self.over_x[0][:, start:stop])
-            second = to_x(self.over_y[1][:, start:stop])
-            sent.append((start, first, second))
-        result = []
         pieces = (self.first, self.second) + self.over_x + self.over_y
         homes = tuple((block,) for block in range(6))
-        for group, (start, first, second) in zip(spans, sent):
-            wholes = place(key, pieces, homes, half, group)
-            moved = [(a - start, n) for a, n in group]
-            result.append(place(key, (first, second), ((6,), (7,)), half, moved, wholes))
-        return result
-
-
-def feature_rows(lefts, right):
-    half = right.shape[0] // 2
-    total = row_product(lefts[0][...], right[:half, :], F32)
-    return total + row_product(lefts[1][...], right[half:, :], F32)
-
-
-def far_kernel(at_ref, own_ref, other_ref, right_ref, first_ref, second_ref):
-    half = first_ref.shape[0]
-    total = feature_rows((own_ref, other_ref), right_ref).astype(BF16)
-    first_ref[...] = total[:half]
-    second_ref[...] = total[half:]
-
-
-def near_kernel(
-    at_ref, x_own, x_other, y_own, y_other, right_ref, first_ref, second_ref, x_ref, y_ref
-):
-    half = first_ref.shape[0]
-    over_x = feature_rows((x_own, x_other), right_ref)
-    x_ref[:half, :] = (over_x[:half] + first_ref[...].astype(F32)).astype(BF16)
-    x_ref[half:, :] = over_x[half:].astype(BF16)
-    over_y = feature_rows((y_own, y_other), right_ref)
-    y_ref[:half, :] = over_y[:half].astype(BF16)
-    y_ref[half:, :] = (over_y[half:] + second_ref[...].astype(F32)).astype(BF16)
-
-
-def own_kernel(at_ref, own_ref, other_ref, right_ref, x_ref, y_ref, first_ref, second_ref):
-    half = first_ref.shape[0]
-    low = at_ref[1]
-    total = feature_rows((own_ref, other_ref), right_ref)
-    total = total + x_ref[...].astype(F32) + y_ref[...].astype(F32)
-    total = total.astype(BF16)
-    first_ref[...] = jnp.where(low == 0, total[:half], total[half:])
-    second_ref[...] = jnp.where(low == 0, total[half:], total[:half])
-
-
-def feature_call(kernel, name, at, lefts, right, extras, steps, outs):
-    tokens, width = right.shape
-    tile = min(width, 512)
-    size = 2 * (lefts[0].shape[1] // 8)
-
-    def left_spec(step):
-        return pl.BlockSpec((tokens // 2, size), lambda i, at: (0, at[0] ^ step))
-
-    def column_spec(rows):
-        return pl.BlockSpec((rows, tile), lambda i, at: (0, i))
+        start, first, second = self.sent[index]
+        wholes = place(key, pieces, homes, half, group)
+        moved = [(a - start, n) for a, n in group]
+        return place(key, (first, second), ((6,), (7,)), half, moved, wholes)
+
+
+TAIL = 16
+
+
+def rows_kernel(at_ref, *refs, starts, half, tail, extra):
+    count = len(starts) - 1
+    lefts, rights = refs[: 2 * count], refs[2 * count : 3 * count]
+    outs, turned = refs[3 * count + extra : -1], refs[-1]
+    place_of = pl.program_id(0)
+    tokens = turned.shape[1] // 2
+    blocks = len(outs)
+    plane, low = at_ref[0], at_ref[1]
+    if tail:
+
+        @pl.when(place_of == 0)
+        def _():
+            row = lax.broadcasted_iota(jnp.int32, (tail, 2 * tokens), 0)
+            turned[blocks * half :, :] = (row == 0).astype(F32).astype(BF16)
+
+    for source in range(count):
+
+        @pl.when(place_of == starts[source])
+        def _(source=source):
+            for block in range(blocks):
+                step, side = block // 2, block % 2
+                start = (2 * (plane ^ step) + (side ^ low)) * half
+                start = pl.multiple_of(start, half)
+                for part in range(2):
+                    left = lefts[2 * source + part][:, pl.ds(start, half)]
+                    turned[
+                        block * half : (block + 1) * half, part * tokens : (part + 1) * tokens
+                    ] = left.T
+
+        @pl.when((place_of >= starts[source]) & (place_of < starts[source + 1]))
+        def _(source=source):
+            total = product(turned[...], rights[source][...])
+            last = total[blocks * half :]
+            if extra:
+                last = last + refs[3 * count][...]
+            total, last = total.astype(BF16), last.astype(BF16)
+            for block, out in enumerate(outs):
+                out[:half, :] = total[block * half : (block + 1) * half]
+                if tail:
+                    out[half:, :] = last
+
+
+def row_blocks(at, sources, half, tail, extra):
+    tile = 512
+    starts = [0]
+    for _, _, right in sources:
+        starts.append(starts[-1] + right.shape[1] // tile)
+    width = starts[-1] * tile
+    tokens = sources[0][2].shape[0]
+    features = sources[0][0].shape[1]
+    blocks = features // half
+
+    def right_spec(start, stop):
+        return pl.BlockSpec(
+            (tokens, tile), lambda i, at: (0, jnp.clip(i - start, 0, stop - start - 1))
+        )
 
     operands, specs = [], []
-    for step in steps:
-        for left in lefts:
-            operands.append(left)
-            specs.append(left_spec(step))
+    for own, other, _ in sources:
+        operands += [own, other]
+        specs += [pl.BlockSpec((tokens // 2, features), lambda i, at: (0, 0))] * 2
+    for source, (_, _, right) in enumerate(sources):
+        operands.append(right)
+        specs.append(right_spec(starts[source], starts[source + 1]))
+    if extra is not None:
+        operands.append(extra)
+        specs.append(pl.BlockSpec((tail, tile), lambda i, at: (0, i)))
     return pl.pallas_call(
-        kernel,
+        functools.partial(
+            rows_kernel, starts=tuple(starts), half=half, tail=tail, extra=int(extra is not None)
+        ),
         grid_spec=pltpu.PrefetchScalarGridSpec(
             num_scalar_prefetch=1,
-            grid=(width // tile,),
-            in_specs=specs + [column_spec(tokens)] + [column_spec(e.shape[0]) for e in extras],
-            out_specs=[column_spec(rows) for rows in outs],
+            grid=(starts[-1],),
+            in_specs=specs,
+            out_specs=[pl.BlockSpec((half + tail, tile), lambda i, at: (0, i))] * blocks,
+            scratch_shapes=[pltpu.VMEM((features + tail, tokens), BF16)],
         ),
-        out_shape=[jax.ShapeDtypeStruct((rows, width), BF16) for rows in outs],
-        cost_estimate=pl.CostEstimate(
-            flops=tokens * width, bytes_accessed=tokens * width, transcendentals=0
-        ),
-        name=name,
-    )(at, *operands, right, *extras)
+        out_shape=[jax.ShapeDtypeStruct((half + tail, width), BF16)] * blocks,
+        cost_estimate=cheap(tokens * width),
+        name="row_blocks",
+    )(at, *operands)
+
+
+def cheap(size):
+    return pl.CostEstimate(flops=size, bytes_accessed=size // 4, transcendentals=0)
 
 
 class Scatter:
-    def __init__(self, lefts, right, half):
-        self.half = half
-        self.lefts = lefts
-        self.right = right
+    def __init__(self, sources, half, tail=0, extra=None):
         self.planes = lax.axis_size("fsdp") // 2
         plane, low = lax.axis_index("fsdp") // 2, lax.axis_index("tp")
-        self.at = jnp.stack([plane, low]).astype(jnp.int32)
         if self.planes == 4:
-            first, second = feature_call(
-                far_kernel, "far_rows", self.at, lefts, right, (), (3,), (half, half)
+            at = jnp.stack([plane, low]).astype(jnp.int32)
+            self.blocks = row_blocks(at, sources, half, tail, extra)
+            self.far_first = to_y(self.blocks[6])
+            self.far_second = to_x(self.blocks[7])
+            self.x_second = to_x(self.blocks[3])
+            self.y_first = to_y(self.blocks[4])
+        else:
+            whole = jnp.concatenate(
+                [
+                    row_product(jnp.concatenate([own, other], axis=0), right)
+                    for own, other, right in sources
+                ],
+                axis=1,
             )
-            self.far_first = to_y(first)
-            self.far_second = to_x(second)
+            mine = lax.psum_scatter(
+                whole, "fsdp", scatter_dimension=0, tiled=True, axis_index_groups=plane_groups()
+            )
+            self.blocks = sorted_pair(mine[:half], mine[half:])
 
     def near(self, *others):
         if self.planes != 4:
-            return
-        half = self.half
-        over_x, over_y = feature_call(
-            near_kernel, "near_rows", self.at, self.lefts, after(self.right, *others),
-            (self.far_first, self.far_second), (1, 2), (2 * half, 2 * half),
-        )
-        self.over_x = to_x(over_x)
-        self.over_y = to_y(over_y)
+            return ()
+        blocks = self.blocks
+        if others:
+            blocks = lax.optimization_barrier(tuple(blocks) + others)[: len(blocks)]
+        sent = (added(blocks[2], self.far_first), added(blocks[5], self.far_second))
+        sent = lax.optimization_barrier(sent)
+        self.x_first = to_x(sent[0])
+        self.y_second = to_y(sent[1])
+        return sent
+
+    def early(self):
+        return (self.x_second, self.y_first) if self.planes == 4 else ()
 
     def own(self, *others):
-        half = self.half
-        right = after(self.right, *others)
-        if self.planes != 4:
-            mine = lax.psum_scatter(
-                row_product(jnp.concatenate(self.lefts, axis=0), right), "fsdp",
-                scatter_dimension=0, tiled=True, axis_index_groups=plane_groups(),
-            )
-            self.pair = sorted_pair(mine[:half], mine[half:])
-        else:
-            self.pair = feature_call(
-                own_kernel, "own_rows", self.at, self.lefts, right,
-                (self.over_x, self.over_y), (0,), (half, half),
-            )
-        self.landed = (to_first(self.pair[0]), from_second(self.pair[1]))
-
-    def part(self):
-        return added(*self.landed)
+        blocks = self.blocks
+        if others:
+            blocks = lax.optimization_barrier(tuple(blocks) + others)[: len(blocks)]
+        first, second = blocks[0].astype(F32), blocks[1].astype(F32)
+        if self.planes == 4:
+            first = first + self.x_first.astype(F32) + self.y_first.astype(F32)
+            second = second + self.x_second.astype(F32) + self.y_second.astype(F32)
+        pair = lax.optimization_barrier((first.astype(BF16), second.astype(BF16)))
+        self.landed = (to_first(pair[0]), from_second(pair[1]))
+        return pair
+
+    def part(self, *others):
+        return added(after(self.landed[0], *others), self.landed[1])
+
+
+def column_call(body, name, operands, weight, extras, outs, tile):
+    width = weight.shape[1]
+
+    def column_spec(rows):
+        return pl.BlockSpec((rows, tile), lambda i: (0, i))
+
+    return pl.pallas_call(
+        body,
+        grid=(width // tile,),
+        in_specs=[pl.BlockSpec(left.shape, lambda i: (0, 0)) for left in operands]
+        + [column_spec(array.shape[0]) for array in (weight,) + extras],
+        out_specs=[column_spec(rows) for rows, _ in outs],
+        out_shape=[jax.ShapeDtypeStruct((rows, width), kind) for rows, kind in outs],
+        cost_estimate=cheap(weight.size),
+        name=name,
+    )(*operands, weight, *extras)
+
+
+def up_kernel(own_ref, other_ref, weight_ref, bias_ref, active_ref, slope_ref):
+    rows = own_ref.shape[0]
+    for side, left in enumerate((own_ref, other_ref)):
+        at = slice(side * rows, (side + 1) * rows)
+        upper = product(left[...], weight_ref[...]) + bias_ref[...]
+        cdf = 0.5 + 0.5 * lax.erf(upper * 0.5**0.5)
+        active_ref[at, :] = (upper * cdf).astype(BF16)
+        density = jnp.exp(upper * upper * -0.5) * (2 * jnp.pi) ** -0.5
+        slope_ref[at, :] = (cdf + upper * density).astype(BF16)
 
 
 def added(one, other):
     return (one.astype(F32) + other.astype(F32)).astype(BF16)
 
 
-def summed_high(part):
-    return part.astype(F32) + to_high(part).astype(F32)
-
-
-def summed_all(vector):
-    fsdp = lax.axis_size("fsdp")
-    if fsdp != 8:
-        return lax.psum(vector, AXES)
-    for step in (to_core, to_x, to_y, to_low, to_high):
-        vector = vector + step(vector)
-    return vector
+def summed(part, other):
+    return part.astype(F32) + other.astype(F32)
 
 
 def product(left, right, out=F32):
@@ -372,7 +432,9 @@
     )(qkv, bias)
 
 
-def attend_back_kernel(qkv_ref, bias_ref, out_ref, log_ref, grad_ref, result_ref, key_acc, value_acc):
+def attend_back_kernel(
+    qkv_ref, bias_ref, out_ref, log_ref, grad_ref, result_ref, key_acc, value_acc
+):
     rows = qkv_ref.shape[0]
     low = lax.broadcasted_iota(jnp.int32, (1, PAIR), 1) < DH
     keys = qkv_ref[:, PAIR : 2 * PAIR]
@@ -401,7 +463,8 @@
             query_grad = query_grad + product(d_scores, head_keys[head])
             key_grad = key_grad + row_product(d_scores, mine, F32)
             value_grad = value_grad + row_product(prob.astype(BF16), mine_grad, F32)
-        result_ref[at, :PAIR] = (query_grad * DH**-0.5).astype(BF16)
+        query_grad = query_grad * DH**-0.5
+        result_ref[at, :PAIR] = query_grad.astype(BF16)
         if tile == 0:
             key_acc[...] = key_grad
             value_acc[...] = value_grad
@@ -412,24 +475,26 @@
     result_ref[:, 2 * PAIR :] = value_acc[...].astype(BF16)
 
 
-def attend_back(qkv, bias, out, logs, grad):
+def attend_back(qkv, bias, out, logs, grad, pairs, begin, into=()):
     rows = qkv.shape[0]
-    pairs = qkv.shape[1] // (3 * PAIR)
-    flops = 2 * 5 * 2 * pairs * rows * rows * DH
-    wide = pl.BlockSpec((rows, 3 * PAIR), lambda i: (0, i))
-    narrow = pl.BlockSpec((rows, PAIR), lambda i: (0, i))
+    wide = pl.BlockSpec((rows, 3 * PAIR), lambda i: (0, i + begin))
+    narrow = pl.BlockSpec((rows, PAIR), lambda i: (0, i + begin))
+
+    def kernel(*refs):
+        attend_back_kernel(*refs[:5], *refs[5 + len(into) :])
+
     return pl.pallas_call(
-        attend_back_kernel,
+        kernel,
         grid=(pairs,),
-        in_specs=[wide, pl.BlockSpec((1, rows), lambda i: (0, 0)), narrow, narrow, narrow],
+        in_specs=[wide, pl.BlockSpec((1, rows), lambda i: (0, 0)), narrow, narrow, narrow]
+        + [pl.BlockSpec(memory_space=pl.ANY)] * len(into),
         out_specs=wide,
         out_shape=jax.ShapeDtypeStruct(qkv.shape, BF16),
         scratch_shapes=[pltpu.VMEM((rows, PAIR), F32)] * 2,
-        cost_estimate=pl.CostEstimate(
-            flops=flops // 64, bytes_accessed=rows * pairs * PAIR, transcendentals=0,
-        ),
+        input_output_aliases={5: 0} if into else {},
+        cost_estimate=cheap(rows * rows),
         name="attend_back",
-    )(qkv, bias, out, logs, grad)
+    )(qkv, bias, out, logs, grad, *into)
 
 
 def normed_of(hidden):
@@ -496,25 +561,22 @@
     )
     mine_in = lax.dynamic_index_in_dim(layer_in, low, 0, keepdims=False)
     own = to_turned(mine_in)
+    length = lax.dynamic_index_in_dim(to_turned(lengths), low, 0, keepdims=False)
     inner_gather.near()
     outer_shard = jnp.concatenate([up_weight, down_weight.T], axis=1)
     outer_gather = Gather(after(outer_shard, inner_gather.first, inner_gather.second))
-    other = to_core(own)
-    x = jnp.concatenate([own, other], axis=0)
-    vectors = to_first(jnp.concatenate([query_bias, value_bias, up_bias]))
-    lengths_other = to_core(lengths)
-    length = jnp.where(core == high, lengths, lengths_other)
-    length = lax.dynamic_index_in_dim(length, low, 0, keepdims=False)
-    ((qkv_weight, out_t),) = inner_gather.far(
-        key, (((0, qkv_width), (qkv_width, heads_width)),)
-    )
+    inner_gather.far((((0, qkv_width), (qkv_width, heads_width)),))
+    arrived = inner_gather.last()
+    other = to_core(after(own, *arrived))
+    vectors = to_first(after(jnp.concatenate([query_bias, value_bias, up_bias]), own, *arrived))
     if planes == 4:
         outer_gather.near(*inner_gather.over_x, *inner_gather.over_y)
     else:
         outer_gather.near()
     mine_grad = lax.dynamic_index_in_dim(out_grad, low, 0, keepdims=False)
     own_grad = to_turned(after(mine_grad, own))
-    x = after(x, *outer_gather.arrived)
+    qkv_weight, out_t = inner_gather.placed(key, 0)
+    own = after(own, *outer_gather.arrived)
 
     out_b, down_b, gain1, bias1, gain2, bias2 = (
         out_bias, down_bias, norm_gain, norm_bias, final_gain, final_bias
@@ -537,11 +599,12 @@
     bias = jnp.where(valid, 0.0, masked_score).astype(F32)[None, :]
     row_valid = (own_places < length).astype(F32)[:, None]
 
+    x = jnp.concatenate([own, other], axis=0)
     qkv = ((product(x, qkv_weight) + qkv_b) * scales).astype(BF16)
     merged, logs = attend(qkv, bias)
     if planes == 4:
         merged = after(merged, own_grad, *outer_gather.over_x, *outer_gather.over_y)
-    (up,), (down_t,) = outer_gather.far(key, (((0, hidden),), ((hidden, hidden),)))
+    outer_gather.far((((0, hidden), (hidden, hidden)),))
     attn_other = to_core(product_back(merged[rows:], out_t, BF16))
     attn = product_back(merged[:rows], out_t)
     first = own.astype(F32) + attn + attn_other.astype(F32) + out_b
@@ -549,12 +612,11 @@
     normed = unit1 * gain1 + bias1
     normed_own = normed.astype(BF16)
     normed_other = to_core(normed_own)
-    normed_low = jnp.concatenate([normed_own, normed_other], axis=0)
-    upper = product(normed_low, up) + up_b
-    cdf = 0.5 + 0.5 * lax.erf(upper * 0.5**0.5)
-    activated = (upper * cdf).astype(BF16)
-    slope = (cdf + upper * jnp.exp(-0.5 * upper * upper) * (2 * jnp.pi) ** -0.5).astype(BF16)
-    activated, slope = lax.optimization_barrier((activated, slope))
+    up, down_t = outer_gather.placed(key, 0)
+    activated, slope = column_call(
+        up_kernel, "up", (normed_own, normed_other), up, (up_b[None],),
+        ((2 * rows, BF16), (2 * rows, BF16)), 256,
+    )
     ffn_other = to_core(product_back(activated[rows:], down_t, BF16))
     ffn = product_back(activated[:rows], down_t)
     second = normed + ffn + ffn_other.astype(F32) + down_b
@@ -562,9 +624,6 @@
     result = (unit2 * gain2 + bias2).astype(BF16)
     result = to_turned(result)
     result_pair = to_low(result)
-    layer_out = jnp.where(
-        low == 0, jnp.stack([result, result_pair]), jnp.stack([result_pair, result])
-    )
 
     cot = own_grad.astype(F32) * row_valid
     final_gain_grad = jnp.sum(cot * unit2, axis=0)
@@ -573,87 +632,109 @@
     d_ffn_own = d_second.astype(BF16)
     down_bias_grad = jnp.sum(d_ffn_own.astype(F32), axis=0)
     d_ffn_other = to_core(d_ffn_own)
-    d_ffn = jnp.concatenate([d_ffn_own, d_ffn_other], axis=0)
-    down_scatter = Scatter((d_ffn_own, d_ffn_other), activated, half)
+    down_scatter = Scatter([(d_ffn_own, d_ffn_other, activated)], half)
+    d_ffn = jnp.concatenate([d_ffn_own, after(d_ffn_other, *down_scatter.blocks)], axis=0)
     d_upper = (product(d_ffn, down_t) * slope.astype(F32)).astype(BF16)
-    down_scatter.near()
-    up_bias_grad = jnp.sum(d_upper.astype(F32), axis=0)
+    up_scatter = Scatter([(normed_own, normed_other, d_upper)], half, TAIL)
+    d_upper = after(d_upper, *up_scatter.blocks)
     back_other = to_core(product_back(d_upper[rows:], up, BF16))
-    back = product_back(d_upper[:rows], up)
-    d_normed = d_second + back + back_other.astype(F32)
-    up_scatter = Scatter((normed_own, normed_other), d_upper, half)
+    sent = down_scatter.near(d_upper)
+    back = product_back(after(d_upper, *sent)[:rows], up)
+    d_normed = d_second + after(back, result, *down_scatter.early()) + back_other.astype(F32)
     norm_gain_grad = jnp.sum(d_normed * unit1, axis=0)
     norm_bias_grad = jnp.sum(d_normed, axis=0)
     d_first = norm_back(d_normed, gain1, unit1, scale1)
     d_attn_own = d_first.astype(BF16)
     out_bias_grad = jnp.sum(d_attn_own.astype(F32), axis=0)
     d_attn_other = to_core(d_attn_own)
+    features = jnp.stack(
+        [
+            out_bias_grad,
+            down_bias_grad,
+            norm_gain_grad,
+            norm_bias_grad,
+            final_gain_grad,
+            final_bias_grad,
+        ]
+    )
+    extra = None
+    if planes == 4:
+        features = (features + to_core(features)).reshape(3, -1)
+        extra = jnp.pad(features, ((1, TAIL - 4), (0, 4 * heads_width - features.shape[1])))
     d_attn = jnp.concatenate([d_attn_own, d_attn_other], axis=0)
-    up_scatter.near()
-    down_scatter.own()
     d_merged = product(d_attn, out_t, BF16)
-    out_scatter = Scatter((d_attn_own, d_attn_other), merged, half)
-    if planes == 4:
-        d_merged = after(d_merged, *down_scatter.pair, out_scatter.far_first)
-    d_qkv = attend_back(qkv, bias, merged, logs, d_merged)
-    out_scatter.near()
-    back_other = to_core(product_back(d_qkv[rows:], qkv_weight, BF16))
-    back = product_back(d_qkv[:rows], qkv_weight)
+    pairs = heads_width // PAIR
+    part = pairs // 2
+    back_args = (qkv, bias, merged, logs)
+    d_qkv = attend_back(*back_args, d_merged, part, 0)
+    down_pair = down_scatter.own(d_qkv)
+    sent = up_scatter.near(*down_pair)
+    d_merged = after(d_merged, d_qkv, result_pair, *sent)
+    d_qkv = attend_back(*back_args, d_merged, pairs - part, part, (d_qkv,))
+    down_part = down_scatter.part(d_qkv)
+    down_high = to_high(down_part)
+    inner_scatter = Scatter(
+        [(own, other, after(d_qkv, down_part)), (d_attn_own, d_attn_other, merged)], half, TAIL, extra
+    )
+    pair = up_scatter.own(*inner_scatter.blocks)
+    d_qkv = after(d_qkv, *pair)
+    d_back = after(d_qkv, down_high, *inner_scatter.blocks)
+    back_other = to_core(product_back(d_back[rows:], qkv_weight, BF16))
+    back = product_back(d_back[:rows], qkv_weight)
     total = d_first + back + back_other.astype(F32)
-    total = to_turned(total.astype(BF16))
-    qkv_scatter = Scatter((own, other), d_qkv, half)
-    up_scatter.own()
-    out_scatter.own()
-    qkv_scatter.near()
-    qkv_bias_grad = jnp.sum(d_qkv.astype(F32), axis=0, keepdims=True)
-    query_bias_grad, _, value_bias_grad = (part[0] for part in unweave(qkv_bias_grad))
-    down_part = down_scatter.part()
-    up_part = up_scatter.part()
-    out_part = out_scatter.part()
+    total = total.astype(BF16)
+    up_part = up_scatter.part(back)
+    up_high = to_high(up_part)
+    inner_scatter.near(total, up_part)
+    total = to_turned(total)
+    pair = inner_scatter.own()
     total_pair = to_low(total)
+    inner_part = inner_scatter.part(total_pair)
+    result_pair = after(result_pair, *pair)
+    layer_out = jnp.where(
+        low == 0, jnp.stack([result, result_pair]), jnp.stack([result_pair, result])
+    )
     input_grad = jnp.where(
         low == 0, jnp.stack([total, total_pair]), jnp.stack([total_pair, total])
     ).astype(F32)
-    qkv_scatter.own()
-    qkv_part = qkv_scatter.part()
-
-    down_grad = summed_high(down_part).T
-    up_grad = summed_high(up_part)
-    out_weight_grad = summed_high(out_part).T
-    query_grad, key_grad, value_grad = unweave(summed_high(qkv_part))
-
-    def spread(vector):
-        empty = jnp.zeros_like(vector)
-        return jnp.where(
-            core == 0, jnp.concatenate([vector, empty]), jnp.concatenate([empty, vector])
+    inner_high = to_high(inner_part)
+
+    down_grad = summed(down_part, down_high).T
+    up_sums = summed(up_part, up_high)
+    up_grad = up_sums[:half]
+    inner_sums = summed(inner_part, inner_high)
+    query_grad, key_grad, value_grad = unweave(inner_sums[:half, :qkv_width])
+    out_weight_grad = inner_sums[:half, qkv_width:].T
+    if planes == 4:
+        features = inner_sums[half + 1 : half + 4, : 2 * width].reshape(6, width)
+        up_bias_grad = up_sums[half]
+        query_bias_grad, _, value_bias_grad = (
+            row[0] for row in unweave(inner_sums[half : half + 1, :qkv_width])
         )
-
-    features = (
-        jnp.stack(
-            [
-                out_bias_grad,
-                down_bias_grad,
-                norm_gain_grad,
-                norm_bias_grad,
-                final_gain_grad,
-                final_bias_grad,
-            ]
+    else:
+
+        def spread(vector):
+            empty = jnp.zeros_like(vector)
+            return jnp.where(
+                core == 0, jnp.concatenate([vector, empty]), jnp.concatenate([empty, vector])
+            )
+
+        sums = jnp.sum(d_qkv.astype(F32), axis=0, keepdims=True)
+        query_sum, _, value_sum = (row[0] for row in unweave(sums))
+        up_sum = jnp.sum(d_upper.astype(F32), axis=0)
+        small = jnp.concatenate(
+            [features.reshape(-1), spread(query_sum), spread(value_sum), spread(up_sum)]
         )
-    ).reshape(-1)
-    small = summed_all(
-        jnp.concatenate(
-            [features, spread(query_bias_grad), spread(value_bias_grad), spread(up_bias_grad)]
-        )
-    )
-    features = small[: 6 * width].reshape(6, width)
-    at = 6 * width
-
-    def mine(start, size):
-        return lax.dynamic_slice(small, (start + low * size,), (size,))
-
-    query_bias_grad = mine(at, heads_width)
-    value_bias_grad = mine(at + 2 * heads_width, heads_width)
-    up_bias_grad = mine(at + 4 * heads_width, hidden)
+        small = lax.psum(small, AXES)
+        features = small[: 6 * width].reshape(6, width)
+        at = 6 * width
+
+        def mine(start, size):
+            return lax.dynamic_slice(small, (start + low * size,), (size,))
+
+        query_bias_grad = mine(at, heads_width)
+        value_bias_grad = mine(at + 2 * heads_width, heads_width)
+        up_bias_grad = mine(at + 4 * heads_width, hidden)
     return (
         layer_out,
         input_grad,

time: 515 us -> 452 us (0.88)
  Pallas kernels: 129 us -> 106 us
  starting transfers between devices: 94.8 us -> 76.3 us
  waiting for transfers between devices: 150 us -> 139 us
  local copies, waits for them, and re-layouts: 31.9 us -> 22.7 us
  matrix products: 49.3 us -> 44.1 us
    ppermute x67 -> x60, starting transfers between devices: 94.8 us -> 76.3 us  [send(): moved = lax.ppermute(value, AXES, pairs)]
    pallas_call x13 -> x6, Pallas kernels: 91.3 us -> 73 us  [the longest x3 31.3 us: row_blocks(): pl.pallas_call(functools.partial(rows_kernel, starts=tuple(starts), half=...]
    ppermute x67 -> x60, waiting for transfers between devices: 150 us -> 139 us  [send(): moved = lax.ppermute(value, AXES, pairs)]
    convert_element_type x1 -> x7, other arithmetic: 3.58 us -> 9.85 us  [the longest x6 9.2 us: own(): pair = lax.optimization_barrier((first.astype(BF16), second.astype(BF16)))]
    unnamed x120 -> x122, local copies, waits for them, and re-layouts: 18.7 us -> 12.8 us
    dot_general x4 -> x3, matrix products: 24.8 us -> 20.1 us  [product(): return jnp.dot(left, right, preferred_element_type=F32).astype(out)]
    pallas_call x6 -> x4, Pallas kernels: 19.3 us -> 14.8 us  [place(): pl.pallas_call(functools.partial(place_kernel, homes=homes, half=half, sp...]
  transfers between devices with their start and end apart: 67 -> 60, of which waited for: 24 -> 22; matrix products, arithmetic and copies ran while one was open for 17% -> 20% of each run, Pallas kernels for 25% -> 21%
where the time goes in v3:
time: 452 us; the launch traced here: 444 us
  waiting for transfers between devices  139 us (31%)
  Pallas kernels  106 us (23%)
  starting transfers between devices  76.3 us (17%)
  other arithmetic  53.6 us (12%)
  matrix products  44.1 us (10%)
  local copies, waits for them, and re-layouts  22.7 us (5%)
    ppermute x60, waiting for transfers between devices, send(): moved = lax.ppermute(value, AXES, pairs)  139 us
    ppermute x60, starting transfers between devices, send(): moved = lax.ppermute(value, AXES, pairs)  76.3 us
    pallas_call x3, Pallas kernels, row_blocks(): pl.pallas_call(functools.partial(rows_kernel, starts=tuple(starts), half=...  31.3 us
    pallas_call x2, Pallas kernels, attend_back(): pl.pallas_call(kernel, grid=(pairs,), in_specs=[wide, pl.BlockSpec((1, ro...  29 us
    dot_general x8, matrix products, product_back(): lax.dot_general(left, right, (((1,), (1,)), ((), ())), preferred_element_...  24 us
    dot_general x3, matrix products, product(): return jnp.dot(left, right, preferred_element_type=F32).astype(out)  20.1 us
    pallas_call x1, Pallas kernels, attend(): pl.pallas_call(attend_kernel, grid=(pairs,), in_specs=[pl.BlockSpec((rows...  18.6 us
    pallas_call x4, Pallas kernels, place(): pl.pallas_call(functools.partial(place_kernel, homes=homes, half=half, sp...  14.8 us
  transfers between devices with their start and end apart: 60, of which 22 were waited for; matrix products, arithmetic and copies ran while one was open for 20% of the time, Pallas kernels for 21%

profile of v3, /device:TPU:8, one launch (start us, length us, event | category | flops | bytes accessed | tf_op | source)
XLA Modules:
  0.0 444.1 jit_solution(13075849610882639305)
XLA Ops:
  11.0 3.1 collective-permute-start.2
  22.1 4.0 collective-permute-done.2.refs_1_
  29.8 11.8 %collective-permute-start.3 = (bf16[128,4096]{1,0:T(8,128)(2,1)}, bf16[128,4096]{1,0:T(8,128)(2,1)}, u32[]{:S(2)}, u32[]{:S(2)}) collective-permute-start(bf16[128,4096]{1,0:T(8,128)(2,1)} %pad_maximum_fusion), channel_id=1, source_target_pairs={{1,4},{3,6},{4,1},{6,3},{9,12},{11,14},{12,9},{14,11},{17,20},{19,... | collective-permute-start | bytes 3145736 | tf_op jit(solution)/shard_map/ppermute | solution.py:35
  48.9 8.1 %collective-permute-done.10.refs_3_ = bf16[128,2048]{1,0:T(8,128)(2,1)S(1)} collective-permute-done((bf16[128,2048]{1,0:T(8,128)(2,1)}, bf16[128,2048]{1,0:T(8,128)(2,1)S(1)}, u32[]{:S(2)}, u32[]{:S(2)}) %collective-permute-start.10) | collective-permute-done | bytes 524320 | tf_op jit(solution)/shard_map/ppermute | solution.py:35
  58.6 3.7 place.4
  62.3 5.7 %collective-permute-done.4.refs_1_ = bf16[128,4096]{1,0:T(8,128)(2,1)} collective-permute-done((bf16[128,4096]{1,0:T(8,128)(2,1)}, bf16[128,4096]{1,0:T(8,128)(2,1)}, u32[]{:S(2)}, u32[]{:S(2)}) %collective-permute-start.4) | collective-permute-done | bytes 1048608 | tf_op jit(solution)/shard_map/ppermute | solution.py:35
  71.1 5.1 %collective-permute-start.12 = (f32[3072]{0:T(1024)S(1)}, f32[3072]{0:T(1024)S(1)}, u32[]{:S(2)}, u32[]{:S(2)}) collective-permute-start(f32[3072]{0:T(1024)S(1)} %pad_maximum_fusion.3), channel_id=1, source_target_pairs={{1,4},{3,6},{4,1},{6,3},{9,12},{11,14},{12,9},{14,11},{17,20},{19,... | collective-permute-start | bytes 36872 | tf_op jit(solution)/shard_map/ppermute | solution.py:35
  83.3 6.1 %multiply_convert_fusion.1.qkv_ref.refs_0_ = bf16[1024,1536]{1,0:T(8,128)(2,1)} fusion(bf16[1024,1536]{1,0:T(8,128)(2,1)S(1)} %copy-done.19, f32[1536]{0:T(1024)S(1)} %copy-done.55, f32[1536]{0:T(1024)S(1)} %add.216, bf16[512,1024]{1,0:T(8,128)(2,1)} %collective-permute-done.9.refs_1_, bf16[512,1024]{1,0:T(8,128)(2,1)S(1)} %broadcast_select_fusion.4.refs_0_), kind=kOutput, calls=%fused_computation.1 | convolution fusion | flops 3230138368 | bytes 8400896 | tf_op jit(solution)/shard_map/dot_general | solution.py:368
  89.4 18.6 %attend.1 = (bf16[1024,512]{1,0:T(8,128)(2,1)}, f32[1024,512]{1,0:T(8,128)}) custom-call(bf16[1024,1536]{1,0:T(8,128)(2,1)} %multiply_convert_fusion.1.qkv_ref.refs_0_, f32[1,1024]{1,0:T(1,128)} %compare_select_fusion.bias_ref.refs_1_), custom_call_target="tpu_custom_call" | custom-call | flops 33554432 | bytes 524288 | tf_op jit(solution)/shard_map/attend/pallas_call | solution.py:413
  108.0 8.3 %collective-permute-done.15.refs_2_ = bf16[128,4096]{1,0:T(8,128)(2,1)} collective-permute-done((bf16[128,4096]{1,0:T(8,128)(2,1)S(1)}, bf16[128,4096]{1,0:T(8,128)(2,1)}, u32[]{:S(2)}, u32[]{:S(2)}) %collective-permute-start.15) | collective-permute-done | bytes 1048608 | tf_op jit(solution)/shard_map/ppermute | solution.py:35
  126.5 5.6 %place.6 = (bf16[1024,2048]{1,0:T(8,128)(2,1)}, bf16[1024,2048]{1,0:T(8,128)(2,1)}) custom-call(s32[1]{0:T(128)} %bitcast.7.key_ref, bf16[128,4096]{1,0:T(8,128)(2,1)} %copy-done.12, bf16[128,4096]{1,0:T(8,128)(2,1)} %collective-permute-done.4.refs_1_, bf16[128,4096]{1,0:T(8,128)(2,1)} %collective-permute-done.15.refs_2_, ...), custom_call_target="tpu_custom_call" | custom-call | tf_op jit(solution)/shard_map/place/pallas_call | solution.py:124
  132.1 14.1 %collective-permute-done.22.refs_1_ = bf16[128,4096]{1,0:T(8,128)(2,1)} collective-permute-done((bf16[128,4096]{1,0:T(8,128)(2,1)}, bf16[128,4096]{1,0:T(8,128)(2,1)}, u32[]{:S(2)}, u32[]{:S(2)}) %collective-permute-start.22) | collective-permute-done | bytes 1048608 | tf_op jit(solution)/shard_map/ppermute | solution.py:35
  149.4 12.8 %up.1 = (bf16[1024,2048]{1,0:T(8,128)(2,1)}, bf16[1024,2048]{1,0:T(8,128)(2,1)}) custom-call(bf16[512,1024]{1,0:T(8,128)(2,1)} %fusion.22.own_ref.refs_0_, bf16[512,1024]{1,0:T(8,128)(2,1)} %collective-permute-done.20.other_ref.refs_1_, bf16[1024,2048]{1,0:T(8,128)(2,1)} %get-tuple-element.110.weight_ref, f32[1,2048]{1,0:T(1,128)} %bitcast.74), custom_call_target="tpu_custom_call" | custom-call | flops 2097152 | bytes 524288 | tf_op jit(solution)/shard_map/up/pallas_call | solution.py:336
  162.2 5.3 %fusion.33 = bf16[512,1024]{1,0:T(8,128)(2,1)S(1)} fusion(bf16[1024,2048]{1,0:T(8,128)(2,1)} %get-tuple-element.112, bf16[1024,2048]{1,0:T(8,128)(2,1)} %get-tuple-element.111.refs_2_), kind=kOutput, calls=%fused_computation.54 | convolution fusion | flops 2148007936 | bytes 7340032 | tf_op jit(solution)/shard_map/dot_general | solution.py:372
  179.2 10.1 %row_blocks.3 = (bf16[128,2048]{1,0:T(8,128)(2,1)}, bf16[128,2048]{1,0:T(8,128)(2,1)}, bf16[128,2048]{1,0:T(8,128)(2,1)}, bf16[128,2048]{1,0:T(8,128)(2,1)}, bf1...) custom-call(s32[2]{0:T(128)} %pad_add_fusion.at_ref, ...), custom_call_target="tpu_custom_call" | custom-call | flops 2097152 | bytes 524288 | tf_op jit(solution)/shard_map/row_blocks/pallas_call | solution.py:254
  193.4 10.6 %multiply_convert_fusion.refs_2_ = bf16[1024,2048]{1,0:T(8,128)(2,1)} fusion(bf16[1024,2048]{1,0:T(8,128)(2,1)} %get-tuple-element.122, bf16[1024,2048]{1,0:T(8,128)(2,1)} %get-tuple-element.112, bf16[512,1024]{1,0:T(8,128)(2,1)} %collective-permute-done.26.refs_1_, bf16[512,1024]{1,0:T(8,128)(2,1)} %copy-done.17), kind=kOutput, calls=%fused_computation | convolution fusion | flops 4305453056 | bytes 14680064 | tf_op jit(solution)/shard_map/dot_general | solution.py:368
  204.0 9.9 %row_blocks.4 = (bf16[144,2048]{1,0:T(8,128)(2,1)}, bf16[144,2048]{1,0:T(8,128)(2,1)}, bf16[144,2048]{1,0:T(8,128)(2,1)}, bf16[144,2048]{1,0:T(8,128)(2,1)}, bf1...) custom-call(s32[2]{0:T(128)} %pad_add_fusion.at_ref, ...), custom_call_target="tpu_custom_call" | custom-call | flops 2097152 | bytes 524288 | tf_op jit(solution)/shard_map/row_blocks/pallas_call | solution.py:254
  213.8 5.3 %fusion.36 = bf16[512,1024]{1,0:T(8,128)(2,1)S(1)} fusion(bf16[1024,2048]{1,0:T(8,128)(2,1)} %get-tuple-element.110.weight_ref, bf16[1024,2048]{1,0:T(8,128)(2,1)} %multiply_convert_fusion.refs_2_), kind=kOutput, calls=%fused_computation.55 | convolution fusion | flops 2148007936 | bytes 7340032 | tf_op jit(solution)/shard_map/dot_general | solution.py:372
  238.1 3.4 fusion.30.refs_4_
  241.6 14.5 %attend_back.2.refs_5_ = bf16[1024,1536]{1,0:T(8,128)(2,1)} custom-call(bf16[1024,1536]{1,0:T(8,128)(2,1)} %multiply_convert_fusion.1.qkv_ref.refs_0_, f32[1,1024]{1,0:T(1,128)} %compare_select_fusion.bias_ref.refs_1_, bf16[1024,512]{1,0:T(8,128)(2,1)} %get-tuple-element.106.refs_2_.refs_5_, f32[1024,512]{1,0:T(8,128)} %get-tuple-element.138.refs_3_, ...), custom_call_target="tpu_custom_call" | custom-call | flops 1048576 | bytes 262144 | tf_op jit(solution)/shard_map/attend_back/pallas_call | solution.py:486
  270.6 14.5 %attend_back.3.refs_4_ = bf16[1024,1536]{1,0:T(8,128)(2,1)} custom-call(bf16[1024,1536]{1,0:T(8,128)(2,1)} %multiply_convert_fusion.1.qkv_ref.refs_0_, f32[1,1024]{1,0:T(1,128)} %compare_select_fusion.bias_ref.refs_1_, bf16[1024,512]{1,0:T(8,128)(2,1)} %get-tuple-element.106.refs_2_.refs_5_, ...), custom_call_target="tpu_custom_call", output_to_operand_aliasing={{}: (5, {})} | custom-call | flops 1048576 | bytes 262144 | tf_op jit(solution)/shard_map/attend_back/pallas_call | solution.py:486
  292.4 11.3 %row_blocks.5 = (bf16[144,2048]{1,0:T(8,128)(2,1)}, bf16[144,2048]{1,0:T(8,128)(2,1)}, bf16[144,2048]{1,0:T(8,128)(2,1)}, bf16[144,2048]{1,0:T(8,128)(2,1)}, bf1...) custom-call(s32[2]{0:T(128)} %pad_add_fusion.at_ref, ...), custom_call_target="tpu_custom_call" | custom-call | flops 2097152 | bytes 524288 | tf_op jit(solution)/shard_map/row_blocks/pallas_call | solution.py:254
  313.9 3.9 fusion.27
  321.3 4.9 %collective-permute-done.47 = bf16[144,2048]{1,0:T(8,128)(2,1)S(1)} collective-permute-done((bf16[144,2048]{1,0:T(8,128)(2,1)S(1)}, bf16[144,2048]{1,0:T(8,128)(2,1)S(1)}, u32[]{:S(2)}, u32[]{:S(2)}) %collective-permute-start.47) | collective-permute-done | bytes 589856 | tf_op jit(solution)/shard_map/ppermute | solution.py:35
  332.4 3.6 collective-permute-done.52
  336.1 9.3 %collective-permute-done.53 = bf16[144,2048]{1,0:T(8,128)(2,1)S(1)} collective-permute-done((bf16[144,2048]{1,0:T(8,128)(2,1)S(1)}, bf16[144,2048]{1,0:T(8,128)(2,1)S(1)}, u32[]{:S(2)}, u32[]{:S(2)}) %collective-permute-start.53) | collective-permute-done | bytes 589856 | tf_op jit(solution)/shard_map/ppermute | solution.py:35
  346.4 10.6 %collective-permute-done.51 = bf16[144,2048]{1,0:T(8,128)(2,1)S(1)} collective-permute-done((bf16[144,2048]{1,0:T(8,128)(2,1)S(1)}, bf16[144,2048]{1,0:T(8,128)(2,1)S(1)}, u32[]{:S(2)}, u32[]{:S(2)}) %collective-permute-start.51) | collective-permute-done | bytes 589856 | tf_op jit(solution)/shard_map/ppermute | solution.py:35
  366.7 18.8 %collective-permute-done.56 = bf16[144,2048]{1,0:T(8,128)(2,1)} collective-permute-done((bf16[144,2048]{1,0:T(8,128)(2,1)}, bf16[144,2048]{1,0:T(8,128)(2,1)}, u32[]{:S(2)}, u32[]{:S(2)}) %collective-permute-start.56) | collective-permute-done | bytes 589856 | tf_op jit(solution)/shard_map/ppermute | solution.py:35
  386.6 16.1 %collective-permute-done.55 = bf16[512,1024]{1,0:T(8,128)(2,1)} collective-permute-done((bf16[512,1024]{1,0:T(8,128)(2,1)S(1)}, bf16[512,1024]{1,0:T(8,128)(2,1)}, u32[]{:S(2)}, u32[]{:S(2)}) %collective-permute-start.55) | collective-permute-done | bytes 1048608 | tf_op jit(solution)/shard_map/ppermute | solution.py:35
  402.7 6.4 %collective-permute-done.57 = bf16[144,2048]{1,0:T(8,128)(2,1)} collective-permute-done((bf16[144,2048]{1,0:T(8,128)(2,1)}, bf16[144,2048]{1,0:T(8,128)(2,1)}, u32[]{:S(2)}, u32[]{:S(2)}) %collective-permute-start.57) | collective-permute-done | bytes 589856 | tf_op jit(solution)/shard_map/ppermute | solution.py:35
  414.2 4.0 fusion.10
  418.2 18.4 %collective-permute-done.58 = bf16[144,2048]{1,0:T(8,128)(2,1)S(1)} collective-permute-done((bf16[144,2048]{1,0:T(8,128)(2,1)S(1)}, bf16[144,2048]{1,0:T(8,128)(2,1)S(1)}, u32[]{:S(2)}, u32[]{:S(2)}) %collective-permute-start.58) | collective-permute-done | bytes 589856 | tf_op jit(solution)/shard_map/ppermute | solution.py:35
  (314 shorter events, 153.9 us)
Async XLA Ops:
  9.4 32.3 %collective-permute-start = (bf16[512,1024]{1,0:T(8,128)(2,1)}, bf16[512,1024]{1,0:T(8,128)(2,1)}, u32[]{:S(2)}, u32[]{:S(2)}) collective-permute-start(bf16[512,1024]{1,0:T(8,128)(2,1)} %dynamic-slice_bitcast_fusion.1), channel_id=1, source_target_pairs={{2,4},{3,5},{4,2},{5,3},{10,12},{11,13},{12,10},{13,11},{18,20},{1... | collective-permute-start | bytes 3145736 | tf_op jit(solution)/shard_map/ppermute | solution.py:35
  20.6 25.8 %collective-permute-start.11 = (bf16[128,2048]{1,0:T(8,128)(2,1)}, bf16[128,2048]{1,0:T(8,128)(2,1)}, u32[]{:S(2)}, u32[]{:S(2)}) collective-permute-start(bf16[128,2048]{1,0:T(8,128)(2,1)} %broadcast_select_fusion.8.refs_0_), channel_id=1, source_target_pairs={{0,16},{1,17},{2,18},{3,19},{4,20},{5,21},{6,22},{7,23},{8,24},{9,... | collective-permute-start | bytes 1572872 | tf_op jit(solution)/shard_map/ppermute | solution.py:35
  29.8 46.4 %collective-permute-start.3 = (bf16[128,4096]{1,0:T(8,128)(2,1)}, bf16[128,4096]{1,0:T(8,128)(2,1)}, u32[]{:S(2)}, u32[]{:S(2)}) collective-permute-start(bf16[128,4096]{1,0:T(8,128)(2,1)} %pad_maximum_fusion), channel_id=1, source_target_pairs={{1,4},{3,6},{4,1},{6,3},{9,12},{11,14},{12,9},{14,11},{17,20},{19,... | collective-permute-start | bytes 3145736 | tf_op jit(solution)/shard_map/ppermute | solution.py:35
  41.6 26.4 %collective-permute-start.4 = (bf16[128,4096]{1,0:T(8,128)(2,1)}, bf16[128,4096]{1,0:T(8,128)(2,1)}, u32[]{:S(2)}, u32[]{:S(2)}) collective-permute-start(bf16[128,4096]{1,0:T(8,128)(2,1)} %pad_maximum_fusion), channel_id=1, source_target_pairs={{0,1},{1,5},{2,3},{3,7},{4,0},{5,4},{6,2},{7,6},{8,9},{9,13},{10,1... | collective-permute-start | bytes 3145736 | tf_op jit(solution)/shard_map/ppermute | solution.py:35
  44.8 24.7 %collective-permute-start.6 = (bf16[128,2048]{1,0:T(8,128)(2,1)}, bf16[128,2048]{1,0:T(8,128)(2,1)S(1)}, u32[]{:S(2)}, u32[]{:S(2)}) collective-permute-start(bf16[128,2048]{1,0:T(8,128)(2,1)} %collective-permute-done.5.refs_2_), channel_id=1, source_target_pairs={{0,16},{1,17},{2,18},{3,19},{4,20},{5,21},{6,22},{7,23},{8,24},{9,... | collective-permute-start | bytes 1572872 | tf_op jit(solution)/shard_map/ppermute | solution.py:35
  46.4 24.7 %collective-permute-start.8 = (bf16[128,2048]{1,0:T(8,128)(2,1)}, bf16[128,2048]{1,0:T(8,128)(2,1)}, u32[]{:S(2)}, u32[]{:S(2)}) collective-permute-start(bf16[128,2048]{1,0:T(8,128)(2,1)} %collective-permute-done.7.refs_5_), channel_id=1, source_target_pairs={{0,8},{1,9},{2,10},{3,11},{4,12},{5,13},{6,14},{7,15},{8,0},{9,1},... | collective-permute-start | bytes 1572872 | tf_op jit(solution)/shard_map/ppermute | solution.py:35
  68.0 40.0 %collective-permute-start.16 = (bf16[128,4096]{1,0:T(8,128)(2,1)}, bf16[128,4096]{1,0:T(8,128)(2,1)}, u32[]{:S(2)}, u32[]{:S(2)}) collective-permute-start(bf16[128,4096]{1,0:T(8,128)(2,1)} %collective-permute-done.4.refs_1_), channel_id=1, source_target_pairs={{0,8},{1,9},{2,10},{3,11},{4,12},{5,13},{6,14},{7,15},{8,0},{9,1},... | collective-permute-start | bytes 3145736 | tf_op jit(solution)/shard_map/ppermute | solution.py:35
  69.5 38.5 %collective-permute-start.18 = (bf16[128,4096]{1,0:T(8,128)(2,1)}, bf16[128,4096]{1,0:T(8,128)(2,1)}, u32[]{:S(2)}, u32[]{:S(2)}) collective-permute-start(bf16[128,4096]{1,0:T(8,128)(2,1)} %collective-permute-done.4.refs_1_), channel_id=1, source_target_pairs={{0,16},{1,17},{2,18},{3,19},{4,20},{5,21},{6,22},{7,23},{8,24},{9,... | collective-permute-start | bytes 3145736 | tf_op jit(solution)/shard_map/ppermute | solution.py:35
  80.3 36.0 %collective-permute-start.15 = (bf16[128,4096]{1,0:T(8,128)(2,1)S(1)}, bf16[128,4096]{1,0:T(8,128)(2,1)}, u32[]{:S(2)}, u32[]{:S(2)}) collective-permute-start(bf16[128,4096]{1,0:T(8,128)(2,1)S(1)} %broadcast_select_fusion.refs_0_), channel_id=1, source_target_pairs={{0,8},{1,9},{2,10},{3,11},{4,12},{5,13},{6,14},{7,15},{8,0},{9,1},... | collective-permute-start | bytes 3145736 | tf_op jit(solution)/shard_map/ppermute | solution.py:35
  81.0 37.0 %collective-permute-start.17 = (bf16[128,4096]{1,0:T(8,128)(2,1)S(1)}, bf16[128,4096]{1,0:T(8,128)(2,1)}, u32[]{:S(2)}, u32[]{:S(2)}) collective-permute-start(bf16[128,4096]{1,0:T(8,128)(2,1)S(1)} %broadcast_select_fusion.refs_0_), channel_id=1, source_target_pairs={{0,16},{1,17},{2,18},{3,19},{4,20},{5,21},{6,22},{7,23},{8,24},{9,... | collective-permute-start | bytes 3145736 | tf_op jit(solution)/shard_map/ppermute | solution.py:35
  120.4 25.8 %collective-permute-start.22 = (bf16[128,4096]{1,0:T(8,128)(2,1)}, bf16[128,4096]{1,0:T(8,128)(2,1)}, u32[]{:S(2)}, u32[]{:S(2)}) collective-permute-start(bf16[128,4096]{1,0:T(8,128)(2,1)} %collective-permute-done.18.refs_5_), channel_id=1, source_target_pairs={{0,8},{1,9},{2,10},{3,11},{4,12},{5,13},{6,14},{7,15},{8,0},{9,1},... | collective-permute-start | bytes 3145736 | tf_op jit(solution)/shard_map/ppermute | solution.py:35
  120.9 25.5 %collective-permute-start.21 = (bf16[128,4096]{1,0:T(8,128)(2,1)}, bf16[128,4096]{1,0:T(8,128)(2,1)}, u32[]{:S(2)}, u32[]{:S(2)}) collective-permute-start(bf16[128,4096]{1,0:T(8,128)(2,1)} %collective-permute-done.15.refs_2_), channel_id=1, source_target_pairs={{0,16},{1,17},{2,18},{3,19},{4,20},{5,21},{6,22},{7,23},{8,24},{9,... | collective-permute-start | bytes 3145736 | tf_op jit(solution)/shard_map/ppermute | solution.py:35
  177.4 41.8 %collective-permute-start.24 = (bf16[512,1024]{1,0:T(8,128)(2,1)}, bf16[512,1024]{1,0:T(8,128)(2,1)}, u32[]{:S(2)}, u32[]{:S(2)}) collective-permute-start(bf16[512,1024]{1,0:T(8,128)(2,1)} %get-tuple-element.225), channel_id=1, source_target_pairs={{2,4},{3,5},{4,2},{5,3},{10,12},{11,13},{12,10},{13,11},{18,20},{1... | collective-permute-start | bytes 3145736 | tf_op jit(solution)/shard_map/ppermute | solution.py:35
  189.3 32.5 %collective-permute-start.28 = (bf16[128,2048]{1,0:T(8,128)(2,1)}, bf16[128,2048]{1,0:T(8,128)(2,1)}, u32[]{:S(2)}, u32[]{:S(2)}) collective-permute-start(bf16[128,2048]{1,0:T(8,128)(2,1)} %get-tuple-element.120), channel_id=1, source_target_pairs={{0,8},{1,9},{2,10},{3,11},{4,12},{5,13},{6,14},{7,15},{8,0},{9,1},... | collective-permute-start | bytes 1572872 | tf_op jit(solution)/shard_map/ppermute | solution.py:35
  190.8 33.0 %collective-permute-start.27 = (bf16[128,2048]{1,0:T(8,128)(2,1)}, bf16[128,2048]{1,0:T(8,128)(2,1)}, u32[]{:S(2)}, u32[]{:S(2)}) collective-permute-start(bf16[128,2048]{1,0:T(8,128)(2,1)} %get-tuple-element.119), channel_id=1, source_target_pairs={{0,16},{1,17},{2,18},{3,19},{4,20},{5,21},{6,22},{7,23},{8,24},{9,... | collective-permute-start | bytes 1572872 | tf_op jit(solution)/shard_map/ppermute | solution.py:35
  192.3 35.8 %collective-permute-start.29 = (bf16[128,2048]{1,0:T(8,128)(2,1)}, bf16[128,2048]{1,0:T(8,128)(2,1)}, u32[]{:S(2)}, u32[]{:S(2)}) collective-permute-start(bf16[128,2048]{1,0:T(8,128)(2,1)} %get-tuple-element.116), channel_id=1, source_target_pairs={{0,8},{1,9},{2,10},{3,11},{4,12},{5,13},{6,14},{7,15},{8,0},{9,1},... | collective-permute-start | bytes 1572872 | tf_op jit(solution)/shard_map/ppermute | solution.py:35
  192.9 35.3 %collective-permute-start.30 = (bf16[128,2048]{1,0:T(8,128)(2,1)}, bf16[128,2048]{1,0:T(8,128)(2,1)}, u32[]{:S(2)}, u32[]{:S(2)}) collective-permute-start(bf16[128,2048]{1,0:T(8,128)(2,1)} %get-tuple-element.117), channel_id=1, source_target_pairs={{0,16},{1,17},{2,18},{3,19},{4,20},{5,21},{6,22},{7,23},{8,24},{9,... | collective-permute-start | bytes 1572872 | tf_op jit(solution)/shard_map/ppermute | solution.py:35
  234.8 29.8 %collective-permute-start.36 = (bf16[144,2048]{1,0:T(8,128)(2,1)}, bf16[144,2048]{1,0:T(8,128)(2,1)}, u32[]{:S(2)}, u32[]{:S(2)}) collective-permute-start(bf16[144,2048]{1,0:T(8,128)(2,1)} %get-tuple-element.130), channel_id=1, source_target_pairs={{0,8},{1,9},{2,10},{3,11},{4,12},{5,13},{6,14},{7,15},{8,0},{9,1},... | collective-permute-start | bytes 1769480 | tf_op jit(solution)/shard_map/ppermute | solution.py:35
  236.3 31.4 %collective-permute-start.35 = (bf16[144,2048]{1,0:T(8,128)(2,1)}, bf16[144,2048]{1,0:T(8,128)(2,1)}, u32[]{:S(2)}, u32[]{:S(2)}) collective-permute-start(bf16[144,2048]{1,0:T(8,128)(2,1)} %get-tuple-element.129), channel_id=1, source_target_pairs={{0,16},{1,17},{2,18},{3,19},{4,20},{5,21},{6,22},{7,23},{8,24},{9,... | collective-permute-start | bytes 1769480 | tf_op jit(solution)/shard_map/ppermute | solution.py:35
  236.8 32.2 %collective-permute-start.25 = (bf16[512,1024]{1,0:T(8,128)(2,1)}, bf16[512,1024]{1,0:T(8,128)(2,1)S(1)}, u32[]{:S(2)}, u32[]{:S(2)}) collective-permute-start(bf16[512,1024]{1,0:T(8,128)(2,1)} %broadcast_select_fusion.2), channel_id=1, source_target_pairs={{0,1},{1,0},{2,3},{3,2},{4,5},{5,4},{6,7},{7,6},{8,9},{9,8},{10,11... | collective-permute-start | bytes 3145736 | tf_op jit(solution)/shard_map/ppermute | solution.py:35
  237.5 25.1 %collective-permute-start.33 = (bf16[128,2048]{1,0:T(8,128)(2,1)}, bf16[128,2048]{1,0:T(8,128)(2,1)}, u32[]{:S(2)}, u32[]{:S(2)}) collective-permute-start(bf16[128,2048]{1,0:T(8,128)(2,1)} %add_convert_fusion.16), channel_id=1, source_target_pairs={{0,8},{1,9},{2,10},{3,11},{4,12},{5,13},{6,14},{7,15},{8,0},{9,1},... | collective-permute-start | bytes 1572872 | tf_op jit(solution)/shard_map/ppermute | solution.py:35
  256.1 47.6 %collective-permute-start.42 = (bf16[144,2048]{1,0:T(8,128)(2,1)}, bf16[144,2048]{1,0:T(8,128)(2,1)}, u32[]{:S(2)}, u32[]{:S(2)}) collective-permute-start(bf16[144,2048]{1,0:T(8,128)(2,1)} %get-tuple-element.126), channel_id=1, source_target_pairs={{0,8},{1,9},{2,10},{3,11},{4,12},{5,13},{6,14},{7,15},{8,0},{9,1},... | collective-permute-start | bytes 1769480 | tf_op jit(solution)/shard_map/ppermute | solution.py:35
  262.6 44.1 %collective-permute-start.41 = (bf16[144,2048]{1,0:T(8,128)(2,1)}, bf16[144,2048]{1,0:T(8,128)(2,1)}, u32[]{:S(2)}, u32[]{:S(2)}) collective-permute-start(bf16[144,2048]{1,0:T(8,128)(2,1)} %get-tuple-element.127), channel_id=1, source_target_pairs={{0,16},{1,17},{2,18},{3,19},{4,20},{5,21},{6,22},{7,23},{8,24},{9,... | collective-permute-start | bytes 1769480 | tf_op jit(solution)/shard_map/ppermute | solution.py:35
  269.1 35.3 %collective-permute-start.43 = (bf16[144,2048]{1,0:T(8,128)(2,1)S(1)}, bf16[144,2048]{1,0:T(8,128)(2,1)}, u32[]{:S(2)}, u32[]{:S(2)}) collective-permute-start(bf16[144,2048]{1,0:T(8,128)(2,1)S(1)} %add_convert_fusion.10), channel_id=1, source_target_pairs={{0,16},{1,17},{2,18},{3,19},{4,20},{5,21},{6,22},{7,23},{8,24},{9,... | collective-permute-start | bytes 1769480 | tf_op jit(solution)/shard_map/ppermute | solution.py:35
  329.6 27.4 %collective-permute-start.51 = (bf16[144,2048]{1,0:T(8,128)(2,1)S(1)}, bf16[144,2048]{1,0:T(8,128)(2,1)S(1)}, u32[]{:S(2)}, u32[]{:S(2)}) collective-permute-start(bf16[144,2048]{1,0:T(8,128)(2,1)S(1)} %copy-done.53), channel_id=1, source_target_pairs={{0,16},{1,17},{2,18},{3,19},{4,20},{5,21},{6,22},{7,23},{8,24},{9,... | collective-permute-start | bytes 1769480 | tf_op jit(solution)/shard_map/ppermute | solution.py:35
  331.2 25.8 %collective-permute-start.50 = (bf16[144,2048]{1,0:T(8,128)(2,1)S(1)}, bf16[144,2048]{1,0:T(8,128)(2,1)S(1)}, u32[]{:S(2)}, u32[]{:S(2)}) collective-permute-start(bf16[144,2048]{1,0:T(8,128)(2,1)S(1)} %add_convert_fusion.6), channel_id=1, source_target_pairs={{0,8},{1,9},{2,10},{3,11},{4,12},{5,13},{6,14},{7,15},{8,0},{9,1},... | collective-permute-start | bytes 1769480 | tf_op jit(solution)/shard_map/ppermute | solution.py:35
  331.7 28.3 %collective-permute-start.54 = (bf16[512,1024]{1,0:T(8,128)(2,1)S(1)}, bf16[512,1024]{1,0:T(8,128)(2,1)S(1)}, u32[]{:S(2)}, u32[]{:S(2)}) collective-permute-start(bf16[512,1024]{1,0:T(8,128)(2,1)S(1)} %add_convert_fusion), channel_id=1, source_target_pairs={{2,4},{3,5},{4,2},{5,3},{10,12},{11,13},{12,10},{13,11},{18,20},{1... | collective-permute-start | bytes 3145736 | tf_op jit(solution)/shard_map/ppermute | solution.py:35
  358.1 27.4 %collective-permute-start.56 = (bf16[144,2048]{1,0:T(8,128)(2,1)}, bf16[144,2048]{1,0:T(8,128)(2,1)}, u32[]{:S(2)}, u32[]{:S(2)}) collective-permute-start(bf16[144,2048]{1,0:T(8,128)(2,1)} %add_convert_fusion.4), channel_id=1, source_target_pairs={{1,4},{3,6},{4,1},{6,3},{9,12},{11,14},{12,9},{14,11},{17,20},{19,... | collective-permute-start | bytes 1769480 | tf_op jit(solution)/shard_map/ppermute | solution.py:35
  360.2 42.6 %collective-permute-start.55 = (bf16[512,1024]{1,0:T(8,128)(2,1)S(1)}, bf16[512,1024]{1,0:T(8,128)(2,1)}, u32[]{:S(2)}, u32[]{:S(2)}) collective-permute-start(bf16[512,1024]{1,0:T(8,128)(2,1)S(1)} %broadcast_select_fusion.1), channel_id=1, source_target_pairs={{0,1},{1,0},{2,3},{3,2},{4,5},{5,4},{6,7},{7,6},{8,9},{9,8},{10,11... | collective-permute-start | bytes 3145736 | tf_op jit(solution)/shard_map/ppermute | solution.py:35
  360.3 48.9 %collective-permute-start.57 = (bf16[144,2048]{1,0:T(8,128)(2,1)}, bf16[144,2048]{1,0:T(8,128)(2,1)}, u32[]{:S(2)}, u32[]{:S(2)}) collective-permute-start(bf16[144,2048]{1,0:T(8,128)(2,1)} %add_convert_fusion.3), channel_id=1, source_target_pairs={{0,4},{1,0},{2,6},{3,2},{4,5},{5,1},{6,7},{7,3},{8,12},{9,8},{10,1... | collective-permute-start | bytes 1769480 | tf_op jit(solution)/shard_map/ppermute | solution.py:35
  364.9 45.9 %collective-permute-start.59 = (bf16[144,2048]{1,0:T(8,128)(2,1)S(1)}, bf16[144,2048]{1,0:T(8,128)(2,1)S(1)}, u32[]{:S(2)}, u32[]{:S(2)}) collective-permute-start(bf16[144,2048]{1,0:T(8,128)(2,1)S(1)} %copy-done.21), channel_id=1, source_target_pairs={{0,2},{1,3},{2,0},{3,1},{4,6},{5,7},{6,4},{7,5},{8,10},{9,11},{10,... | collective-permute-start | bytes 1769480 | tf_op jit(solution)/shard_map/ppermute | solution.py:35
  410.4 26.2 %collective-permute-start.58 = (bf16[144,2048]{1,0:T(8,128)(2,1)S(1)}, bf16[144,2048]{1,0:T(8,128)(2,1)S(1)}, u32[]{:S(2)}, u32[]{:S(2)}) collective-permute-start(bf16[144,2048]{1,0:T(8,128)(2,1)S(1)} %add_convert_fusion.2), channel_id=1, source_target_pairs={{0,2},{1,3},{2,0},{3,1},{4,6},{5,7},{6,4},{7,5},{8,10},{9,11},{10,... | collective-permute-start | bytes 1769480 | tf_op jit(solution)/shard_map/ppermute | solution.py:35
  (84 other events, 908.3 us)

commit v4 on v3

--- a/solution.py
+++ b/solution.py
@@ -141,7 +141,7 @@
         self.first = to_first(shard)
         self.second = to_second(shard)
         self.planes = lax.axis_size("fsdp") // 2
-        self.arrived = (self.first, self.second)
+        self.unit = jnp.concatenate([self.first, self.second], axis=0)
 
     def near(self, *others):
         if self.planes != 4:
@@ -150,20 +150,21 @@
                 unit, "fsdp", axis=0, tiled=True, axis_index_groups=plane_groups()
             )
             return
-        first, second = after(self.first, *others), after(self.second, *others)
-        self.over_x = (to_x(first), to_x(second))
-        self.over_y = (to_y(first), to_y(second))
+        self.unit = after(self.unit, *others)
+        self.over_x = to_x(self.unit)
+        self.over_y = to_y(self.unit)
 
     def far(self, spans):
         self.spans = spans
         self.sent = []
+        self.cuts = ()
         for group in spans if self.planes == 4 else ():
             start, stop = group[0][0], group[-1][0] + group[-1][1]
-            first, second = self.over_x[0], self.over_y[1]
-            if stop - start != self.width:
-                first, second = first[:, start:stop], second[:, start:stop]
-            first, second = to_y(first), to_x(second)
-            self.sent.append((start, first, second))
+            cut = lax.optimization_barrier(
+                (self.over_x[: self.half, start:stop], self.over_y[self.half :, start:stop])
+            )
+            self.cuts += cut
+            self.sent.append((start, to_y(cut[0]), to_x(cut[1])))
 
     def last(self):
         return self.sent[-1][1:] if self.planes == 4 else ()
@@ -173,8 +174,8 @@
         if self.planes != 4:
             return [self.whole[:, a : a + n] for a, n in group]
         half = self.half
-        pieces = (self.first, self.second) + self.over_x + self.over_y
-        homes = tuple((block,) for block in range(6))
+        pieces = (self.unit, self.over_x, self.over_y)
+        homes = ((0, 1), (2, 3), (4, 5))
         start, first, second = self.sent[index]
         wholes = place(key, pieces, homes, half, group)
         moved = [(a - start, n) for a, n in group]
@@ -190,7 +191,7 @@
     outs, turned = refs[3 * count + extra : -1], refs[-1]
     place_of = pl.program_id(0)
     tokens = turned.shape[1] // 2
-    blocks = len(outs)
+    blocks = 8
     plane, low = at_ref[0], at_ref[1]
     if tail:
 
@@ -220,10 +221,16 @@
             if extra:
                 last = last + refs[3 * count][...]
             total, last = total.astype(BF16), last.astype(BF16)
-            for block, out in enumerate(outs):
-                out[:half, :] = total[block * half : (block + 1) * half]
+            for step, out in enumerate(outs[:3]):
+                at = 2 * step * half
+                out[:half, :] = total[at : at + half]
                 if tail:
-                    out[half:, :] = last
+                    out[half : half + tail, :] = last
+                out[half + tail :, :] = total[at + half : at + 2 * half]
+            outs[3][:half, :] = total[6 * half : 7 * half]
+            if tail:
+                outs[3][half:, :] = last
+            outs[4][...] = total[7 * half : 8 * half]
 
 
 def row_blocks(at, sources, half, tail, extra):
@@ -234,7 +241,7 @@
     width = starts[-1] * tile
     tokens = sources[0][2].shape[0]
     features = sources[0][0].shape[1]
-    blocks = features // half
+    outs = [2 * half + tail] * 3 + [half + tail, half]
 
     def right_spec(start, stop):
         return pl.BlockSpec(
@@ -259,10 +266,10 @@
             num_scalar_prefetch=1,
             grid=(starts[-1],),
             in_specs=specs,
-            out_specs=[pl.BlockSpec((half + tail, tile), lambda i, at: (0, i))] * blocks,
+            out_specs=[pl.BlockSpec((rows, tile), lambda i, at: (0, i)) for rows in outs],
             scratch_shapes=[pltpu.VMEM((features + tail, tokens), BF16)],
         ),
-        out_shape=[jax.ShapeDtypeStruct((half + tail, width), BF16)] * blocks,
+        out_shape=[jax.ShapeDtypeStruct((rows, width), BF16) for rows in outs],
         cost_estimate=cheap(tokens * width),
         name="row_blocks",
     )(at, *operands)
@@ -275,15 +282,15 @@
 class Scatter:
     def __init__(self, sources, half, tail=0, extra=None):
         self.planes = lax.axis_size("fsdp") // 2
+        self.half, self.tail = half, tail
         plane, low = lax.axis_index("fsdp") // 2, lax.axis_index("tp")
         if self.planes == 4:
             at = jnp.stack([plane, low]).astype(jnp.int32)
             self.blocks = row_blocks(at, sources, half, tail, extra)
-            self.far_first = to_y(self.blocks[6])
-            self.far_second = to_x(self.blocks[7])
-            self.x_second = to_x(self.blocks[3])
-            self.y_first = to_y(self.blocks[4])
+            self.far_first = to_y(self.blocks[3])
+            self.far_second = to_x(self.blocks[4])
         else:
+            self.tail = 0
             whole = jnp.concatenate(
                 [
                     row_product(jnp.concatenate([own, other], axis=0), right)
@@ -294,37 +301,44 @@
             mine = lax.psum_scatter(
                 whole, "fsdp", scatter_dimension=0, tiled=True, axis_index_groups=plane_groups()
             )
-            self.blocks = sorted_pair(mine[:half], mine[half:])
+            self.blocks = (jnp.concatenate(sorted_pair(mine[:half], mine[half:]), axis=0),)
+
+    def tied(self, others):
+        if others:
+            return lax.optimization_barrier(tuple(self.blocks) + others)[: len(self.blocks)]
+        return self.blocks
 
     def near(self, *others):
         if self.planes != 4:
             return ()
-        blocks = self.blocks
-        if others:
-            blocks = lax.optimization_barrier(tuple(blocks) + others)[: len(blocks)]
-        sent = (added(blocks[2], self.far_first), added(blocks[5], self.far_second))
-        sent = lax.optimization_barrier(sent)
-        self.x_first = to_x(sent[0])
-        self.y_second = to_y(sent[1])
+        half, tail = self.half, self.tail
+        blocks = self.tied(others)
+        over_x = added(blocks[1], jnp.pad(self.far_first, ((0, half), (0, 0))))
+        over_y = added(blocks[2], jnp.pad(self.far_second, ((half + tail, 0), (0, 0))))
+        sent = lax.optimization_barrier((over_x, over_y))
+        self.over_x = to_x(sent[0])
+        self.over_y = to_y(sent[1])
         return sent
 
-    def early(self):
-        return (self.x_second, self.y_first) if self.planes == 4 else ()
+    def arrivals(self):
+        return (self.over_x, self.over_y) if self.planes == 4 else ()
 
     def own(self, *others):
-        blocks = self.blocks
-        if others:
-            blocks = lax.optimization_barrier(tuple(blocks) + others)[: len(blocks)]
-        first, second = blocks[0].astype(F32), blocks[1].astype(F32)
+        half, tail = self.half, self.tail
+        total = self.tied(others)[0]
         if self.planes == 4:
-            first = first + self.x_first.astype(F32) + self.y_first.astype(F32)
-            second = second + self.x_second.astype(F32) + self.y_second.astype(F32)
-        pair = lax.optimization_barrier((first.astype(BF16), second.astype(BF16)))
+            total = total.astype(F32) + self.over_x.astype(F32) + self.over_y.astype(F32)
+        total = total.astype(BF16)
+        pair = lax.optimization_barrier((total[: half + tail], total[half:]))
         self.landed = (to_first(pair[0]), from_second(pair[1]))
         return pair
 
     def part(self, *others):
-        return added(after(self.landed[0], *others), self.landed[1])
+        half, tail = self.half, self.tail
+        first, second = after(self.landed[0], *others), self.landed[1]
+        if tail:
+            second = jnp.concatenate([second[tail:], second[:tail]], axis=0)
+        return added(first, second)
 
 
 def column_call(body, name, operands, weight, extras, outs, tile):
@@ -513,6 +527,33 @@
     )
 
 
+def finish_kernel(part_ref, high_ref, query_ref, key_ref, value_ref, out_ref, tail_ref, *, half):
+    total = part_ref[...].astype(F32) + high_ref[...].astype(F32)
+    width = query_ref.shape[1]
+    for pair in range(width // PAIR):
+        at = slice(pair * PAIR, (pair + 1) * PAIR)
+        for place_of, ref in enumerate((query_ref, key_ref, value_ref)):
+            start = (3 * pair + place_of) * PAIR
+            ref[:, at] = total[:half, start : start + PAIR]
+    out_ref[...] = total[:half, 3 * width :].T
+    tail_ref[...] = total[half:]
+
+
+def finish(part, high, half, width):
+    columns = part.shape[1]
+    tail = part.shape[0] - half
+    return pl.pallas_call(
+        functools.partial(finish_kernel, half=half),
+        out_shape=[jax.ShapeDtypeStruct((half, width), F32)] * 3
+        + [
+            jax.ShapeDtypeStruct((columns - 3 * width, half), F32),
+            jax.ShapeDtypeStruct((tail, columns), F32),
+        ],
+        cost_estimate=cheap(part.size),
+        name="finish",
+    )(part, high)
+
+
 def weave(parts):
     lead = parts[0].shape[0]
     parts = [part.reshape(lead, -1, PAIR) for part in parts]
@@ -567,16 +608,16 @@
     outer_gather = Gather(after(outer_shard, inner_gather.first, inner_gather.second))
     inner_gather.far((((0, qkv_width), (qkv_width, heads_width)),))
     arrived = inner_gather.last()
-    other = to_core(after(own, *arrived))
+    other = to_core(own)
     vectors = to_first(after(jnp.concatenate([query_bias, value_bias, up_bias]), own, *arrived))
     if planes == 4:
-        outer_gather.near(*inner_gather.over_x, *inner_gather.over_y)
+        outer_gather.near(inner_gather.over_x, inner_gather.over_y, other)
     else:
         outer_gather.near()
     mine_grad = lax.dynamic_index_in_dim(out_grad, low, 0, keepdims=False)
     own_grad = to_turned(after(mine_grad, own))
     qkv_weight, out_t = inner_gather.placed(key, 0)
-    own = after(own, *outer_gather.arrived)
+    own = after(own, outer_gather.unit)
 
     out_b, down_b, gain1, bias1, gain2, bias2 = (
         out_bias, down_bias, norm_gain, norm_bias, final_gain, final_bias
@@ -603,7 +644,7 @@
     qkv = ((product(x, qkv_weight) + qkv_b) * scales).astype(BF16)
     merged, logs = attend(qkv, bias)
     if planes == 4:
-        merged = after(merged, own_grad, *outer_gather.over_x, *outer_gather.over_y)
+        merged = after(merged, own_grad)
     outer_gather.far((((0, hidden), (hidden, hidden)),))
     attn_other = to_core(product_back(merged[rows:], out_t, BF16))
     attn = product_back(merged[:rows], out_t)
@@ -635,12 +676,13 @@
     down_scatter = Scatter([(d_ffn_own, d_ffn_other, activated)], half)
     d_ffn = jnp.concatenate([d_ffn_own, after(d_ffn_other, *down_scatter.blocks)], axis=0)
     d_upper = (product(d_ffn, down_t) * slope.astype(F32)).astype(BF16)
-    up_scatter = Scatter([(normed_own, normed_other, d_upper)], half, TAIL)
+    up_bias_grad = jnp.sum(d_upper.astype(F32), axis=0)
+    sent = down_scatter.near(d_upper)
+    up_scatter = Scatter([(normed_own, normed_other, after(d_upper, *sent))], half)
     d_upper = after(d_upper, *up_scatter.blocks)
     back_other = to_core(product_back(d_upper[rows:], up, BF16))
-    sent = down_scatter.near(d_upper)
-    back = product_back(after(d_upper, *sent)[:rows], up)
-    d_normed = d_second + after(back, result, *down_scatter.early()) + back_other.astype(F32)
+    back = product_back(d_upper[:rows], up)
+    d_normed = d_second + after(back, result, *down_scatter.arrivals()) + back_other.astype(F32)
     norm_gain_grad = jnp.sum(d_normed * unit1, axis=0)
     norm_bias_grad = jnp.sum(d_normed, axis=0)
     d_first = norm_back(d_normed, gain1, unit1, scale1)
@@ -660,21 +702,23 @@
     extra = None
     if planes == 4:
         features = (features + to_core(features)).reshape(3, -1)
-        extra = jnp.pad(features, ((1, TAIL - 4), (0, 4 * heads_width - features.shape[1])))
+        extra = jnp.concatenate([features, up_bias_grad[None]], axis=0)
+        extra = jnp.pad(extra, ((1, TAIL - 5), (0, 0)))
     d_attn = jnp.concatenate([d_attn_own, d_attn_other], axis=0)
     d_merged = product(d_attn, out_t, BF16)
+    down_pair = down_scatter.own()
     pairs = heads_width // PAIR
     part = pairs // 2
     back_args = (qkv, bias, merged, logs)
+    d_merged = after(d_merged, *down_pair)
     d_qkv = attend_back(*back_args, d_merged, part, 0)
-    down_pair = down_scatter.own(d_qkv)
-    sent = up_scatter.near(*down_pair)
-    d_merged = after(d_merged, d_qkv, result_pair, *sent)
-    d_qkv = attend_back(*back_args, d_merged, pairs - part, part, (d_qkv,))
+    sent = up_scatter.near(d_qkv)
     down_part = down_scatter.part(d_qkv)
     down_high = to_high(down_part)
+    d_merged = after(d_merged, d_qkv, result_pair, down_part, *sent)
+    d_qkv = attend_back(*back_args, d_merged, pairs - part, part, (d_qkv,))
     inner_scatter = Scatter(
-        [(own, other, after(d_qkv, down_part)), (d_attn_own, d_attn_other, merged)], half, TAIL, extra
+        [(own, other, d_qkv), (d_attn_own, d_attn_other, merged)], half, TAIL, extra
     )
     pair = up_scatter.own(*inner_scatter.blocks)
     d_qkv = after(d_qkv, *pair)
@@ -689,7 +733,7 @@
     total = to_turned(total)
     pair = inner_scatter.own()
     total_pair = to_low(total)
-    inner_part = inner_scatter.part(total_pair)
+    inner_part = inner_scatter.part(up_high)
     result_pair = after(result_pair, *pair)
     layer_out = jnp.where(
         low == 0, jnp.stack([result, result_pair]), jnp.stack([result_pair, result])
@@ -702,16 +746,18 @@
     down_grad = summed(down_part, down_high).T
     up_sums = summed(up_part, up_high)
     up_grad = up_sums[:half]
-    inner_sums = summed(inner_part, inner_high)
-    query_grad, key_grad, value_grad = unweave(inner_sums[:half, :qkv_width])
-    out_weight_grad = inner_sums[:half, qkv_width:].T
+    inner_high = after(inner_high, total_pair)
     if planes == 4:
-        features = inner_sums[half + 1 : half + 4, : 2 * width].reshape(6, width)
-        up_bias_grad = up_sums[half]
-        query_bias_grad, _, value_bias_grad = (
-            row[0] for row in unweave(inner_sums[half : half + 1, :qkv_width])
+        query_grad, key_grad, value_grad, out_weight_grad, tail = finish(
+            inner_part, inner_high, half, heads_width
         )
+        features = tail[1:4, : 2 * width].reshape(6, width)
+        up_bias_grad = tail[4]
+        query_bias_grad, _, value_bias_grad = (row[0] for row in unweave(tail[:1, :qkv_width]))
     else:
+        inner_sums = summed(inner_part, inner_high)
+        query_grad, key_grad, value_grad = unweave(inner_sums[:half, :qkv_width])
+        out_weight_grad = inner_sums[:half, qkv_width:].T
 
         def spread(vector):
             empty = jnp.zeros_like(vector)
@@ -721,7 +767,7 @@
 
         sums = jnp.sum(d_qkv.astype(F32), axis=0, keepdims=True)
         query_sum, _, value_sum = (row[0] for row in unweave(sums))
-        up_sum = jnp.sum(d_upper.astype(F32), axis=0)
+        up_sum = up_bias_grad
         small = jnp.concatenate(
             [features.reshape(-1), spread(query_sum), spread(value_sum), spread(up_sum)]
         )

time: 452 us -> 438 us (0.969)
  waiting for transfers between devices: 139 us -> 125 us
  starting transfers between devices: 76.3 us -> 71.3 us
    ppermute x60 -> x50, waiting for transfers between devices: 139 us -> 125 us  [send(): moved = lax.ppermute(value, AXES, pairs)]
    slice x6 -> x12, local copies, waits for them, and re-layouts: 2.91 us -> 11.7 us  [the longest x2 3.17 us: far(): self.over_y[self.half:, start:stop]]
    concatenate x0 -> x3, other arithmetic: none -> 5.1 us  [the longest x2 4.42 us: __init__(): self.unit = jnp.concatenate([self.first, self.second], axis=0)]
    ppermute x60 -> x50, starting transfers between devices: 76.3 us -> 71.3 us  [send(): moved = lax.ppermute(value, AXES, pairs)]
    unnamed x122 -> x106, local copies, waits for them, and re-layouts: 12.8 us -> 9.85 us
    convert_element_type x6 -> x3, other arithmetic: 9.2 us -> 7.55 us  [own(): total = total.astype(BF16)]
  transfers between devices with their start and end apart: 60 -> 50, of which waited for: 22 -> 22; matrix products, arithmetic and copies ran while one was open for 20% -> 22% of each run, Pallas kernels for 21% -> 22%
where the time goes in v4:
time: 438 us; the launch traced here: 432 us
  waiting for transfers between devices  125 us (29%)
  Pallas kernels  108 us (25%)
  starting transfers between devices  71.3 us (16%)
  other arithmetic  55.3 us (13%)
  matrix products  42.9 us (10%)
  local copies, waits for them, and re-layouts  26.7 us (6%)
    ppermute x50, waiting for transfers between devices, send(): moved = lax.ppermute(value, AXES, pairs)  125 us
    ppermute x50, starting transfers between devices, send(): moved = lax.ppermute(value, AXES, pairs)  71.3 us
    pallas_call x3, Pallas kernels, row_blocks(): pl.pallas_call(functools.partial(rows_kernel, starts=tuple(starts), half=...  31 us
    pallas_call x2, Pallas kernels, attend_back(): pl.pallas_call(kernel, grid=(pairs,), in_specs=[wide, pl.BlockSpec((1, ro...  29 us
    dot_general x8, matrix products, product_back(): lax.dot_general(left, right, (((1,), (1,)), ((), ())), preferred_element_...  21.6 us
    dot_general x3, matrix products, product(): return jnp.dot(left, right, preferred_element_type=F32).astype(out)  21.3 us
    pallas_call x1, Pallas kernels, attend(): pl.pallas_call(attend_kernel, grid=(pairs,), in_specs=[pl.BlockSpec((rows...  18.8 us
    pallas_call x4, Pallas kernels, place(): pl.pallas_call(functools.partial(place_kernel, homes=homes, half=half, sp...  14.4 us
  transfers between devices with their start and end apart: 50, of which 22 were waited for; matrix products, arithmetic and copies ran while one was open for 22% of the time, Pallas kernels for 22%

profile of v4, /device:TPU:8, one launch (start us, length us, event | category | flops | bytes accessed | tf_op | source)
XLA Modules:
  0.0 431.9 jit_solution(13380552710309292741)
XLA Ops:
  15.2 9.7 %collective-permute-done.1 = bf16[128,2048]{1,0:T(8,128)(2,1)} collective-permute-done((bf16[128,2048]{1,0:T(8,128)(2,1)}, bf16[128,2048]{1,0:T(8,128)(2,1)}, u32[]{:S(2)}, u32[]{:S(2)}) %collective-permute-start.1) | collective-permute-done | bytes 524320 | tf_op jit(solution)/shard_map/ppermute | solution.py:35
  30.4 3.5 collective-permute-start.3
  39.4 3.9 collective-permute-start.7
  43.3 9.2 %collective-permute-done.5.refs_1_ = bf16[256,2048]{1,0:T(8,128)(2,1)S(1)} collective-permute-done((bf16[256,2048]{1,0:T(8,128)(2,1)S(1)}, bf16[256,2048]{1,0:T(8,128)(2,1)S(1)}, u32[]{:S(2)}, u32[]{:S(2)}) %collective-permute-start.5) | collective-permute-done | bytes 1048608 | tf_op jit(solution)/shard_map/ppermute | solution.py:35
  60.0 3.7 place.4
  71.7 5.9 %collective-permute-start.10 = (f32[3072]{0:T(1024)S(1)}, f32[3072]{0:T(1024)S(1)}, u32[]{:S(2)}, u32[]{:S(2)}) collective-permute-start(f32[3072]{0:T(1024)S(1)} %pad_maximum_fusion.5), channel_id=1, source_target_pairs={{1,4},{3,6},{4,1},{6,3},{9,12},{11,14},{12,9},{14,11},{17,20},{19,... | collective-permute-start | bytes 36872 | tf_op jit(solution)/shard_map/ppermute | solution.py:35
  80.1 7.2 %multiply_convert_fusion.1.qkv_ref.refs_0_ = bf16[1024,1536]{1,0:T(8,128)(2,1)} fusion(bf16[1024,1536]{1,0:T(8,128)(2,1)} %get-tuple-element.98, f32[1536]{0:T(1024)S(1)} %copy-done.49, f32[1536]{0:T(1024)S(1)} %add.207, bf16[512,1024]{1,0:T(8,128)(2,1)} %collective-permute-done.7.refs_1_, bf16[512,1024]{1,0:T(8,128)(2,1)S(1)} %broadcast_select_fusion.4.refs_0_), kind=kOutput, calls=%fused_computation.2 | convolution fusion | flops 3230138368 | bytes 8400896 | tf_op jit(solution)/shard_map/dot_general | solution.py:382
  87.4 18.8 %attend.1 = (bf16[1024,512]{1,0:T(8,128)(2,1)}, f32[1024,512]{1,0:T(8,128)}) custom-call(bf16[1024,1536]{1,0:T(8,128)(2,1)} %multiply_convert_fusion.1.qkv_ref.refs_0_, f32[1,1024]{1,0:T(1,128)} %compare_select_fusion.bias_ref.refs_1_), custom_call_target="tpu_custom_call" | custom-call | flops 33554432 | bytes 524288 | tf_op jit(solution)/shard_map/attend/pallas_call | solution.py:427
  111.7 4.1 collective-permute-done.15.refs_1_
  124.4 5.6 %place.6 = (bf16[1024,2048]{1,0:T(8,128)(2,1)}, bf16[1024,2048]{1,0:T(8,128)(2,1)}) custom-call(s32[1]{0:T(128)} %bitcast.7.key_ref, bf16[256,4096]{1,0:T(8,128)(2,1)} %pad_maximum_fusion.refs_0_, bf16[256,4096]{1,0:T(8,128)(2,1)} %collective-permute-done.15.refs_1_, bf16[256,4096]{1,0:T(8,128)(2,1)} %collective-permute-done.16.refs_2_), custom_call_target="tpu_custom_call" | custom-call | tf_op jit(solution)/shard_map/place/pallas_call | solution.py:124
  130.0 15.0 %collective-permute-done.17.refs_0_ = bf16[128,4096]{1,0:T(8,128)(2,1)} collective-permute-done((bf16[128,4096]{1,0:T(8,128)(2,1)}, bf16[128,4096]{1,0:T(8,128)(2,1)}, u32[]{:S(2)}, u32[]{:S(2)}) %collective-permute-start.17) | collective-permute-done | bytes 1048608 | tf_op jit(solution)/shard_map/ppermute | solution.py:35
  148.1 12.8 %up.1 = (bf16[1024,2048]{1,0:T(8,128)(2,1)}, bf16[1024,2048]{1,0:T(8,128)(2,1)}) custom-call(bf16[512,1024]{1,0:T(8,128)(2,1)} %fusion.22.own_ref.refs_0_, bf16[512,1024]{1,0:T(8,128)(2,1)} %collective-permute-done.14.other_ref.refs_1_, bf16[1024,2048]{1,0:T(8,128)(2,1)} %get-tuple-element.108.weight_ref, f32[1,2048]{1,0:T(1,128)} %bitcast.64), custom_call_target="tpu_custom_call" | custom-call | flops 2097152 | bytes 524288 | tf_op jit(solution)/shard_map/up/pallas_call | solution.py:350
  160.9 5.3 %fusion.33 = bf16[512,1024]{1,0:T(8,128)(2,1)S(1)} fusion(bf16[1024,2048]{1,0:T(8,128)(2,1)} %get-tuple-element.110, bf16[1024,2048]{1,0:T(8,128)(2,1)} %get-tuple-element.109.refs_2_), kind=kOutput, calls=%fused_computation.65 | convolution fusion | flops 2148007936 | bytes 7340032 | tf_op jit(solution)/shard_map/dot_general | solution.py:386
  178.0 10.1 %row_blocks.3 = (bf16[256,2048]{1,0:T(8,128)(2,1)}, bf16[256,2048]{1,0:T(8,128)(2,1)}, bf16[256,2048]{1,0:T(8,128)(2,1)}, bf16[128,2048]{1,0:T(8,128)(2,1)}, bf16[128,2048]{1,0:T(8,128)(2,1)}) custom-call(s32[2]{0:T(128)} %pad_add_fusion.at_ref, bf16[512,1024]{1,0:T(8,128)(2,1)} %copy-done.19, bf16[512,1024]{1,0:T(8,128)(2,1)} %collective-permute-done.22.refs_1_, ...), custom_call_target="tpu_custom_call" | custom-call | flops 2097152 | bytes 524288 | tf_op jit(solution)/shard_map/row_blocks/pallas_call | solution.py:261
  190.2 10.6 %convert_reduce_fusion = (f32[2048]{0:T(1024)S(1)}, bf16[1024,2048]{1,0:T(8,128)(2,1)}) fusion(bf16[1024,2048]{1,0:T(8,128)(2,1)} %get-tuple-element.117, bf16[1024,2048]{1,0:T(8,128)(2,1)} %get-tuple-element.110, bf16[512,1024]{1,0:T(8,128)(2,1)} %collective-permute-done.22.refs_1_, bf16[512,1024]{1,0:T(8,128)(2,1)} %copy-done.19), kind=kOutput, calls=%fused_computation | convolution fusion | flops 4309645312 | bytes 14688256 | tf_op jit(solution)/shard_map/dot_general | solution.py:382
  207.3 9.7 %row_blocks.4 = (bf16[256,2048]{1,0:T(8,128)(2,1)}, bf16[256,2048]{1,0:T(8,128)(2,1)}, bf16[256,2048]{1,0:T(8,128)(2,1)}, bf16[128,2048]{1,0:T(8,128)(2,1)}, bf16[128,2048]{1,0:T(8,128)(2,1)}) custom-call(s32[2]{0:T(128)} %pad_add_fusion.at_ref, bf16[512,1024]{1,0:T(8,128)(2,1)} %fusion.22.own_ref.refs_0_, ...), custom_call_target="tpu_custom_call" | custom-call | flops 2097152 | bytes 524288 | tf_op jit(solution)/shard_map/row_blocks/pallas_call | solution.py:261
  217.0 5.3 %fusion.36 = bf16[512,1024]{1,0:T(8,128)(2,1)S(1)} fusion(bf16[1024,2048]{1,0:T(8,128)(2,1)} %get-tuple-element.108.weight_ref, bf16[1024,2048]{1,0:T(8,128)(2,1)} %get-tuple-element.128.refs_2_), kind=kOutput, calls=%fused_computation.66 | convolution fusion | flops 2148007936 | bytes 7340032 | tf_op jit(solution)/shard_map/dot_general | solution.py:386
  227.1 3.4 collective-permute-done.25
  235.7 3.5 collective-permute-start.21
  247.0 3.4 fusion.30.refs_4_
  250.5 14.5 %attend_back.2.refs_5_ = bf16[1024,1536]{1,0:T(8,128)(2,1)} custom-call(bf16[1024,1536]{1,0:T(8,128)(2,1)} %multiply_convert_fusion.1.qkv_ref.refs_0_, f32[1,1024]{1,0:T(1,128)} %compare_select_fusion.bias_ref.refs_1_, bf16[1024,512]{1,0:T(8,128)(2,1)} %get-tuple-element.102.refs_2_.refs_5_, f32[1024,512]{1,0:T(8,128)} %get-tuple-element.130.refs_3_, ...), custom_call_target="tpu_custom_call" | custom-call | flops 1048576 | bytes 262144 | tf_op jit(solution)/shard_map/attend_back/pallas_call | solution.py:500
  275.2 14.5 %attend_back.3.refs_4_ = bf16[1024,1536]{1,0:T(8,128)(2,1)} custom-call(bf16[1024,1536]{1,0:T(8,128)(2,1)} %multiply_convert_fusion.1.qkv_ref.refs_0_, f32[1,1024]{1,0:T(1,128)} %compare_select_fusion.bias_ref.refs_1_, bf16[1024,512]{1,0:T(8,128)(2,1)} %get-tuple-element.102.refs_2_.refs_5_, ...), custom_call_target="tpu_custom_call", output_to_operand_aliasing={{}: (5, {})} | custom-call | flops 1048576 | bytes 262144 | tf_op jit(solution)/shard_map/attend_back/pallas_call | solution.py:500
  289.7 11.3 %row_blocks.5 = (bf16[272,2048]{1,0:T(8,128)(2,1)}, bf16[272,2048]{1,0:T(8,128)(2,1)}, bf16[272,2048]{1,0:T(8,128)(2,1)}, bf16[144,2048]{1,0:T(8,128)(2,1)}, bf16[128,2048]{1,0:T(8,128)(2,1)}) custom-call(s32[2]{0:T(128)} %pad_add_fusion.at_ref, bf16[512,1024]{1,0:T(8,128)(2,1)} %copy-done.7, bf16[512,1024]{1,0:T(8,128)(2,1)} %collective-permute-done.7.refs_1_, ...), custom_call_target="tpu_custom_call" | custom-call | flops 2097152 | bytes 524288 | tf_op jit(solution)/shard_map/row_blocks/pallas_call | solution.py:261
  316.3 3.7 collective-permute-done.39
  328.4 23.0 %collective-permute-done.42 = bf16[272,2048]{1,0:T(8,128)(2,1)S(1)} collective-permute-done((bf16[272,2048]{1,0:T(8,128)(2,1)}, bf16[272,2048]{1,0:T(8,128)(2,1)S(1)}, u32[]{:S(2)}, u32[]{:S(2)}) %collective-permute-start.42) | collective-permute-done | bytes 1114144 | tf_op jit(solution)/shard_map/ppermute | solution.py:35
  365.1 8.0 %collective-permute-done.46 = bf16[144,2048]{1,0:T(8,128)(2,1)} collective-permute-done((bf16[144,2048]{1,0:T(8,128)(2,1)S(1)}, bf16[144,2048]{1,0:T(8,128)(2,1)}, u32[]{:S(2)}, u32[]{:S(2)}) %collective-permute-start.46) | collective-permute-done | bytes 589856 | tf_op jit(solution)/shard_map/ppermute | solution.py:35
  374.2 11.9 %collective-permute-done.47 = bf16[128,2048]{1,0:T(8,128)(2,1)S(1)} collective-permute-done((bf16[128,2048]{1,0:T(8,128)(2,1)}, bf16[128,2048]{1,0:T(8,128)(2,1)S(1)}, u32[]{:S(2)}, u32[]{:S(2)}) %collective-permute-start.47) | collective-permute-done | bytes 524320 | tf_op jit(solution)/shard_map/ppermute | solution.py:35
  386.1 5.7 %collective-permute-done.48 = bf16[144,2048]{1,0:T(8,128)(2,1)S(1)} collective-permute-done((bf16[144,2048]{1,0:T(8,128)(2,1)}, bf16[144,2048]{1,0:T(8,128)(2,1)S(1)}, u32[]{:S(2)}, u32[]{:S(2)}) %collective-permute-start.48) | collective-permute-done | bytes 589856 | tf_op jit(solution)/shard_map/ppermute | solution.py:35
  392.0 6.1 %collective-permute-start.49 = (bf16[144,2048]{1,0:T(8,128)(2,1)S(1)}, bf16[144,2048]{1,0:T(8,128)(2,1)S(1)}, u32[]{:S(2)}, u32[]{:S(2)}) collective-permute-start(bf16[144,2048]{1,0:T(8,128)(2,1)S(1)} %add_convert_fusion.11.part_ref), channel_id=1, source_target_pairs={{0,2},{1,3},{2,0},{3,1},{4,6},{5,7},{6,4},{7,5},{8,10},{9,11},{10,... | collective-permute-start | bytes 1769480 | tf_op jit(solution)/shard_map/ppermute | solution.py:35
  399.2 4.0 maximum_select_fusion
  403.2 14.6 %collective-permute-done.45 = bf16[512,1024]{1,0:T(8,128)(2,1)S(1)} collective-permute-done((bf16[512,1024]{1,0:T(8,128)(2,1)S(1)}, bf16[512,1024]{1,0:T(8,128)(2,1)S(1)}, u32[]{:S(2)}, u32[]{:S(2)}) %collective-permute-start.45) | collective-permute-done | bytes 1048608 | tf_op jit(solution)/shard_map/ppermute | solution.py:35
  420.3 3.8 collective-permute-done.49.high_ref
  (281 shorter events, 158.0 us)
Async XLA Ops:
  9.4 29.8 %collective-permute-start = (bf16[512,1024]{1,0:T(8,128)(2,1)}, bf16[512,1024]{1,0:T(8,128)(2,1)}, u32[]{:S(2)}, u32[]{:S(2)}) collective-permute-start(bf16[512,1024]{1,0:T(8,128)(2,1)} %dynamic-slice_bitcast_fusion.1), channel_id=1, source_target_pairs={{2,4},{3,5},{4,2},{5,3},{10,12},{11,13},{12,10},{13,11},{18,20},{1... | collective-permute-start | bytes 3145736 | tf_op jit(solution)/shard_map/ppermute | solution.py:35
  11.1 23.0 %collective-permute-start.11 = (s32[2]{0:T(128)S(1)}, s32[2]{0:T(128)S(1)}, u32[]{:S(2)}, u32[]{:S(2)}) collective-permute-start(s32[2]{0:T(128)S(1)} %copy-done.48), channel_id=1, source_target_pairs={{2,4},{3,5},{4,2},{5,3},{10,12},{11,13},{12,10},{13,11},{18,20},{1... | collective-permute-start | bytes 32 | tf_op jit(solution)/shard_map/ppermute | solution.py:35
  27.4 25.2 %collective-permute-start.5 = (bf16[256,2048]{1,0:T(8,128)(2,1)S(1)}, bf16[256,2048]{1,0:T(8,128)(2,1)S(1)}, u32[]{:S(2)}, u32[]{:S(2)}) collective-permute-start(bf16[256,2048]{1,0:T(8,128)(2,1)S(1)} %pad_maximum_fusion.2.refs_0_), channel_id=1, source_target_pairs={{0,8},{1,9},{2,10},{3,11},{4,12},{5,13},{6,14},{7,15},{8,0},{9,1},... | collective-permute-start | bytes 3145736 | tf_op jit(solution)/shard_map/ppermute | solution.py:35
  28.9 26.1 %collective-permute-start.6 = (bf16[256,2048]{1,0:T(8,128)(2,1)S(1)}, bf16[256,2048]{1,0:T(8,128)(2,1)S(1)}, u32[]{:S(2)}, u32[]{:S(2)}) collective-permute-start(bf16[256,2048]{1,0:T(8,128)(2,1)S(1)} %pad_maximum_fusion.2.refs_0_), channel_id=1, source_target_pairs={{0,16},{1,17},{2,18},{3,19},{4,20},{5,21},{6,22},{7,23},{8,24},{9,... | collective-permute-start | bytes 3145736 | tf_op jit(solution)/shard_map/ppermute | solution.py:35
  30.4 27.0 %collective-permute-start.3 = (bf16[128,4096]{1,0:T(8,128)(2,1)}, bf16[128,4096]{1,0:T(8,128)(2,1)S(1)}, u32[]{:S(2)}, u32[]{:S(2)}) collective-permute-start(bf16[128,4096]{1,0:T(8,128)(2,1)} %pad_maximum_fusion.1), channel_id=1, source_target_pairs={{1,4},{3,6},{4,1},{6,3},{9,12},{11,14},{12,9},{14,11},{17,20},{19,... | collective-permute-start | bytes 3145736 | tf_op jit(solution)/shard_map/ppermute | solution.py:35
  36.0 27.7 %collective-permute-start.4 = (bf16[128,4096]{1,0:T(8,128)(2,1)}, bf16[128,4096]{1,0:T(8,128)(2,1)}, u32[]{:S(2)}, u32[]{:S(2)}) collective-permute-start(bf16[128,4096]{1,0:T(8,128)(2,1)} %pad_maximum_fusion.1), channel_id=1, source_target_pairs={{0,1},{1,5},{2,3},{3,7},{4,0},{5,4},{6,2},{7,6},{8,9},{9,13},{10,1... | collective-permute-start | bytes 3145736 | tf_op jit(solution)/shard_map/ppermute | solution.py:35
  39.4 27.5 %collective-permute-start.7 = (bf16[512,1024]{1,0:T(8,128)(2,1)S(1)}, bf16[512,1024]{1,0:T(8,128)(2,1)}, u32[]{:S(2)}, u32[]{:S(2)}) collective-permute-start(bf16[512,1024]{1,0:T(8,128)(2,1)S(1)} %broadcast_select_fusion.4.refs_0_), channel_id=1, source_target_pairs={{0,4},{1,5},{2,6},{3,7},{4,0},{5,1},{6,2},{7,3},{8,12},{9,13},{10,... | collective-permute-start | bytes 3145736 | tf_op jit(solution)/shard_map/ppermute | solution.py:35
  52.5 25.1 %collective-permute-start.12 = (bf16[512,1024]{1,0:T(8,128)(2,1)S(1)}, bf16[512,1024]{1,0:T(8,128)(2,1)}, u32[]{:S(2)}, u32[]{:S(2)}) collective-permute-start(bf16[512,1024]{1,0:T(8,128)(2,1)S(1)} %dynamic-slice_bitcast_fusion), channel_id=1, source_target_pairs={{2,4},{3,5},{4,2},{5,3},{10,12},{11,13},{12,10},{13,11},{18,20},{1... | collective-permute-start | bytes 3145736 | tf_op jit(solution)/shard_map/ppermute | solution.py:35
  66.9 48.9 %collective-permute-start.15 = (bf16[256,4096]{1,0:T(8,128)(2,1)}, bf16[256,4096]{1,0:T(8,128)(2,1)}, u32[]{:S(2)}, u32[]{:S(2)}) collective-permute-start(bf16[256,4096]{1,0:T(8,128)(2,1)} %pad_maximum_fusion.refs_0_), channel_id=1, source_target_pairs={{0,8},{1,9},{2,10},{3,11},{4,12},{5,13},{6,14},{7,15},{8,0},{9,1},... | collective-permute-start | bytes 6291464 | tf_op jit(solution)/shard_map/ppermute | solution.py:35
  67.4 50.7 %collective-permute-start.16 = (bf16[256,4096]{1,0:T(8,128)(2,1)}, bf16[256,4096]{1,0:T(8,128)(2,1)}, u32[]{:S(2)}, u32[]{:S(2)}) collective-permute-start(bf16[256,4096]{1,0:T(8,128)(2,1)} %pad_maximum_fusion.refs_0_), channel_id=1, source_target_pairs={{0,16},{1,17},{2,18},{3,19},{4,20},{5,21},{6,22},{7,23},{8,24},{9,... | collective-permute-start | bytes 6291464 | tf_op jit(solution)/shard_map/ppermute | solution.py:35
  120.3 24.7 %collective-permute-start.17 = (bf16[128,4096]{1,0:T(8,128)(2,1)}, bf16[128,4096]{1,0:T(8,128)(2,1)}, u32[]{:S(2)}, u32[]{:S(2)}) collective-permute-start(bf16[128,4096]{1,0:T(8,128)(2,1)} %slice.162), channel_id=1, source_target_pairs={{0,16},{1,17},{2,18},{3,19},{4,20},{5,21},{6,22},{7,23},{8,24},{9,... | collective-permute-start | bytes 3145736 | tf_op jit(solution)/shard_map/ppermute | solution.py:35
  120.9 24.3 %collective-permute-start.18 = (bf16[128,4096]{1,0:T(8,128)(2,1)}, bf16[128,4096]{1,0:T(8,128)(2,1)}, u32[]{:S(2)}, u32[]{:S(2)}) collective-permute-start(bf16[128,4096]{1,0:T(8,128)(2,1)} %slice.163), channel_id=1, source_target_pairs={{0,8},{1,9},{2,10},{3,11},{4,12},{5,13},{6,14},{7,15},{8,0},{9,1},... | collective-permute-start | bytes 3145736 | tf_op jit(solution)/shard_map/ppermute | solution.py:35
  123.8 24.3 %collective-permute-start.14 = (bf16[512,1024]{1,0:T(8,128)(2,1)}, bf16[512,1024]{1,0:T(8,128)(2,1)}, u32[]{:S(2)}, u32[]{:S(2)}) collective-permute-start(bf16[512,1024]{1,0:T(8,128)(2,1)} %fusion.22.own_ref.refs_0_), channel_id=1, source_target_pairs={{0,4},{1,5},{2,6},{3,7},{4,0},{5,1},{6,2},{7,3},{8,12},{9,13},{10,... | collective-permute-start | bytes 3145736 | tf_op jit(solution)/shard_map/ppermute | solution.py:35
  176.2 46.3 %collective-permute-start.20 = (bf16[512,1024]{1,0:T(8,128)(2,1)}, bf16[512,1024]{1,0:T(8,128)(2,1)}, u32[]{:S(2)}, u32[]{:S(2)}) collective-permute-start(bf16[512,1024]{1,0:T(8,128)(2,1)} %get-tuple-element.217), channel_id=1, source_target_pairs={{2,4},{3,5},{4,2},{5,3},{10,12},{11,13},{12,10},{13,11},{18,20},{1... | collective-permute-start | bytes 3145736 | tf_op jit(solution)/shard_map/ppermute | solution.py:35
  204.5 26.1 %collective-permute-start.25 = (bf16[256,2048]{1,0:T(8,128)(2,1)}, bf16[256,2048]{1,0:T(8,128)(2,1)}, u32[]{:S(2)}, u32[]{:S(2)}) collective-permute-start(bf16[256,2048]{1,0:T(8,128)(2,1)} %add_convert_fusion.9), channel_id=1, source_target_pairs={{0,8},{1,9},{2,10},{3,11},{4,12},{5,13},{6,14},{7,15},{8,0},{9,1},... | collective-permute-start | bytes 3145736 | tf_op jit(solution)/shard_map/ppermute | solution.py:35
  205.7 25.6 %collective-permute-start.26 = (bf16[256,2048]{1,0:T(8,128)(2,1)}, bf16[256,2048]{1,0:T(8,128)(2,1)}, u32[]{:S(2)}, u32[]{:S(2)}) collective-permute-start(bf16[256,2048]{1,0:T(8,128)(2,1)} %add_convert_fusion.8), channel_id=1, source_target_pairs={{0,16},{1,17},{2,18},{3,19},{4,20},{5,21},{6,22},{7,23},{8,24},{9,... | collective-permute-start | bytes 3145736 | tf_op jit(solution)/shard_map/ppermute | solution.py:35
  235.7 39.4 %collective-permute-start.21 = (bf16[512,1024]{1,0:T(8,128)(2,1)}, bf16[512,1024]{1,0:T(8,128)(2,1)}, u32[]{:S(2)}, u32[]{:S(2)}) collective-permute-start(bf16[512,1024]{1,0:T(8,128)(2,1)} %broadcast_select_fusion.2), channel_id=1, source_target_pairs={{0,1},{1,0},{2,3},{3,2},{4,5},{5,4},{6,7},{7,6},{8,9},{9,8},{10,11... | collective-permute-start | bytes 3145736 | tf_op jit(solution)/shard_map/ppermute | solution.py:35
  239.3 25.7 %collective-permute-start.32 = (bf16[128,2048]{1,0:T(8,128)(2,1)}, bf16[128,2048]{1,0:T(8,128)(2,1)}, u32[]{:S(2)}, u32[]{:S(2)}) collective-permute-start(bf16[128,2048]{1,0:T(8,128)(2,1)} %get-tuple-element.127), channel_id=1, source_target_pairs={{0,8},{1,9},{2,10},{3,11},{4,12},{5,13},{6,14},{7,15},{8,0},{9,1},... | collective-permute-start | bytes 1572872 | tf_op jit(solution)/shard_map/ppermute | solution.py:35
  239.8 26.5 %collective-permute-start.31 = (bf16[128,2048]{1,0:T(8,128)(2,1)}, bf16[128,2048]{1,0:T(8,128)(2,1)}, u32[]{:S(2)}, u32[]{:S(2)}) collective-permute-start(bf16[128,2048]{1,0:T(8,128)(2,1)} %get-tuple-element.126), channel_id=1, source_target_pairs={{0,16},{1,17},{2,18},{3,19},{4,20},{5,21},{6,22},{7,23},{8,24},{9,... | collective-permute-start | bytes 1572872 | tf_op jit(solution)/shard_map/ppermute | solution.py:35
  244.8 26.7 %collective-permute-start.29 = (bf16[128,2048]{1,0:T(8,128)(2,1)}, bf16[128,2048]{1,0:T(8,128)(2,1)}, u32[]{:S(2)}, u32[]{:S(2)}) collective-permute-start(bf16[128,2048]{1,0:T(8,128)(2,1)} %get-tuple-element.131), channel_id=1, source_target_pairs={{1,4},{3,6},{4,1},{6,3},{9,12},{11,14},{12,9},{14,11},{17,20},{19,... | collective-permute-start | bytes 1572872 | tf_op jit(solution)/shard_map/ppermute | solution.py:35
  246.9 27.0 %collective-permute-start.30 = (bf16[128,2048]{1,0:T(8,128)(2,1)}, bf16[128,2048]{1,0:T(8,128)(2,1)}, u32[]{:S(2)}, u32[]{:S(2)}) collective-permute-start(bf16[128,2048]{1,0:T(8,128)(2,1)} %get-tuple-element.132), channel_id=1, source_target_pairs={{0,4},{1,0},{2,6},{3,2},{4,5},{5,1},{6,7},{7,3},{8,12},{9,8},{10,1... | collective-permute-start | bytes 1572872 | tf_op jit(solution)/shard_map/ppermute | solution.py:35
  268.6 34.2 %collective-permute-start.34 = (bf16[256,2048]{1,0:T(8,128)(2,1)}, bf16[256,2048]{1,0:T(8,128)(2,1)}, u32[]{:S(2)}, u32[]{:S(2)}) collective-permute-start(bf16[256,2048]{1,0:T(8,128)(2,1)} %add_convert_fusion.6), channel_id=1, source_target_pairs={{0,8},{1,9},{2,10},{3,11},{4,12},{5,13},{6,14},{7,15},{8,0},{9,1},... | collective-permute-start | bytes 3145736 | tf_op jit(solution)/shard_map/ppermute | solution.py:35
  270.0 32.8 %collective-permute-start.35 = (bf16[256,2048]{1,0:T(8,128)(2,1)S(1)}, bf16[256,2048]{1,0:T(8,128)(2,1)}, u32[]{:S(2)}, u32[]{:S(2)}) collective-permute-start(bf16[256,2048]{1,0:T(8,128)(2,1)S(1)} %add_convert_fusion.5), channel_id=1, source_target_pairs={{0,16},{1,17},{2,18},{3,19},{4,20},{5,21},{6,22},{7,23},{8,24},{9,... | collective-permute-start | bytes 3145736 | tf_op jit(solution)/shard_map/ppermute | solution.py:35
  275.1 34.1 %collective-permute-start.36 = (bf16[128,2048]{1,0:T(8,128)(2,1)S(1)}, bf16[128,2048]{1,0:T(8,128)(2,1)S(1)}, u32[]{:S(2)}, u32[]{:S(2)}) collective-permute-start(bf16[128,2048]{1,0:T(8,128)(2,1)S(1)} %add_convert_fusion.13), channel_id=1, source_target_pairs={{0,2},{1,3},{2,0},{3,1},{4,6},{5,7},{6,4},{7,5},{8,10},{9,11},{10,... | collective-permute-start | bytes 1572872 | tf_op jit(solution)/shard_map/ppermute | solution.py:35
  301.6 21.7 %collective-permute-start.40 = (bf16[144,2048]{1,0:T(8,128)(2,1)}, bf16[144,2048]{1,0:T(8,128)(2,1)S(1)}, u32[]{:S(2)}, u32[]{:S(2)}) collective-permute-start(bf16[144,2048]{1,0:T(8,128)(2,1)} %get-tuple-element.143), channel_id=1, source_target_pairs={{0,16},{1,17},{2,18},{3,19},{4,20},{5,21},{6,22},{7,23},{8,24},{9,... | collective-permute-start | bytes 1769480 | tf_op jit(solution)/shard_map/ppermute | solution.py:35
  324.5 26.9 %collective-permute-start.42 = (bf16[272,2048]{1,0:T(8,128)(2,1)}, bf16[272,2048]{1,0:T(8,128)(2,1)S(1)}, u32[]{:S(2)}, u32[]{:S(2)}) collective-permute-start(bf16[272,2048]{1,0:T(8,128)(2,1)} %add_convert_fusion.2), channel_id=1, source_target_pairs={{0,8},{1,9},{2,10},{3,11},{4,12},{5,13},{6,14},{7,15},{8,0},{9,1},... | collective-permute-start | bytes 3342344 | tf_op jit(solution)/shard_map/ppermute | solution.py:35
  326.0 27.3 %collective-permute-start.43 = (bf16[272,2048]{1,0:T(8,128)(2,1)}, bf16[272,2048]{1,0:T(8,128)(2,1)}, u32[]{:S(2)}, u32[]{:S(2)}) collective-permute-start(bf16[272,2048]{1,0:T(8,128)(2,1)} %add_convert_fusion.1), channel_id=1, source_target_pairs={{0,16},{1,17},{2,18},{3,19},{4,20},{5,21},{6,22},{7,23},{8,24},{9,... | collective-permute-start | bytes 3342344 | tf_op jit(solution)/shard_map/ppermute | solution.py:35
  326.7 36.6 %collective-permute-start.44 = (bf16[512,1024]{1,0:T(8,128)(2,1)S(1)}, bf16[512,1024]{1,0:T(8,128)(2,1)}, u32[]{:S(2)}, u32[]{:S(2)}) collective-permute-start(bf16[512,1024]{1,0:T(8,128)(2,1)S(1)} %add_convert_fusion.3), channel_id=1, source_target_pairs={{2,4},{3,5},{4,2},{5,3},{10,12},{11,13},{12,10},{13,11},{18,20},{1... | collective-permute-start | bytes 3145736 | tf_op jit(solution)/shard_map/ppermute | solution.py:35
  360.1 26.0 %collective-permute-start.47 = (bf16[128,2048]{1,0:T(8,128)(2,1)}, bf16[128,2048]{1,0:T(8,128)(2,1)S(1)}, u32[]{:S(2)}, u32[]{:S(2)}) collective-permute-start(bf16[128,2048]{1,0:T(8,128)(2,1)} %add_convert_fusion.12), channel_id=1, source_target_pairs={{0,2},{1,3},{2,0},{3,1},{4,6},{5,7},{6,4},{7,5},{8,10},{9,11},{10,... | collective-permute-start | bytes 1572872 | tf_op jit(solution)/shard_map/ppermute | solution.py:35
  363.0 28.8 %collective-permute-start.48 = (bf16[144,2048]{1,0:T(8,128)(2,1)}, bf16[144,2048]{1,0:T(8,128)(2,1)S(1)}, u32[]{:S(2)}, u32[]{:S(2)}) collective-permute-start(bf16[144,2048]{1,0:T(8,128)(2,1)} %get-tuple-element.156), channel_id=1, source_target_pairs={{0,4},{1,0},{2,6},{3,2},{4,5},{5,1},{6,7},{7,3},{8,12},{9,8},{10,1... | collective-permute-start | bytes 1769480 | tf_op jit(solution)/shard_map/ppermute | solution.py:35
  363.5 54.4 %collective-permute-start.45 = (bf16[512,1024]{1,0:T(8,128)(2,1)S(1)}, bf16[512,1024]{1,0:T(8,128)(2,1)S(1)}, u32[]{:S(2)}, u32[]{:S(2)}) collective-permute-start(bf16[512,1024]{1,0:T(8,128)(2,1)S(1)} %broadcast_select_fusion.1), channel_id=1, source_target_pairs={{0,1},{1,0},{2,3},{3,2},{4,5},{5,4},{6,7},{7,6},{8,9},{9,8},{10,11... | collective-permute-start | bytes 3145736 | tf_op jit(solution)/shard_map/ppermute | solution.py:35
  392.0 32.0 %collective-permute-start.49 = (bf16[144,2048]{1,0:T(8,128)(2,1)S(1)}, bf16[144,2048]{1,0:T(8,128)(2,1)S(1)}, u32[]{:S(2)}, u32[]{:S(2)}) collective-permute-start(bf16[144,2048]{1,0:T(8,128)(2,1)S(1)} %add_convert_fusion.11.part_ref), channel_id=1, source_target_pairs={{0,2},{1,3},{2,0},{3,1},{4,6},{5,7},{6,4},{7,5},{8,10},{9,11},{10,... | collective-permute-start | bytes 1769480 | tf_op jit(solution)/shard_map/ppermute | solution.py:35
  (68 other events, 663.8 us)

commit v5 on v4

--- a/solution.py
+++ b/solution.py
@@ -527,7 +527,10 @@
     )
 
 
-def finish_kernel(part_ref, high_ref, query_ref, key_ref, value_ref, out_ref, tail_ref, *, half):
+def finish_kernel(
+    part_ref, high_ref, query_ref, key_ref, value_ref, out_ref,
+    features_ref, query_sum_ref, value_sum_ref, up_sum_ref, *, half,
+):
     total = part_ref[...].astype(F32) + high_ref[...].astype(F32)
     width = query_ref.shape[1]
     for pair in range(width // PAIR):
@@ -535,19 +538,32 @@
         for place_of, ref in enumerate((query_ref, key_ref, value_ref)):
             start = (3 * pair + place_of) * PAIR
             ref[:, at] = total[:half, start : start + PAIR]
+        start = 3 * pair * PAIR
+        query_sum_ref[:, at] = total[half : half + 1, start : start + PAIR]
+        start = start + 2 * PAIR
+        value_sum_ref[:, at] = total[half : half + 1, start : start + PAIR]
     out_ref[...] = total[:half, 3 * width :].T
-    tail_ref[...] = total[half:]
+    wide = features_ref.shape[1]
+    for row in range(3):
+        for side in range(2):
+            at = 2 * row + side
+            features_ref[at : at + 1, :] = total[
+                half + 1 + row : half + 2 + row, side * wide : (side + 1) * wide
+            ]
+    up_sum_ref[...] = total[half + 4 : half + 5]
 
 
 def finish(part, high, half, width):
     columns = part.shape[1]
-    tail = part.shape[0] - half
     return pl.pallas_call(
         functools.partial(finish_kernel, half=half),
         out_shape=[jax.ShapeDtypeStruct((half, width), F32)] * 3
         + [
             jax.ShapeDtypeStruct((columns - 3 * width, half), F32),
-            jax.ShapeDtypeStruct((tail, columns), F32),
+            jax.ShapeDtypeStruct((6, columns // 2), F32),
+            jax.ShapeDtypeStruct((1, width), F32),
+            jax.ShapeDtypeStruct((1, width), F32),
+            jax.ShapeDtypeStruct((1, columns), F32),
         ],
         cost_estimate=cheap(part.size),
         name="finish",
@@ -732,8 +748,8 @@
     inner_scatter.near(total, up_part)
     total = to_turned(total)
     pair = inner_scatter.own()
-    total_pair = to_low(total)
-    inner_part = inner_scatter.part(up_high)
+    inner_part = inner_scatter.part()
+    total_pair = to_low(after(total, inner_part))
     result_pair = after(result_pair, *pair)
     layer_out = jnp.where(
         low == 0, jnp.stack([result, result_pair]), jnp.stack([result_pair, result])
@@ -748,12 +764,11 @@
     up_grad = up_sums[:half]
     inner_high = after(inner_high, total_pair)
     if planes == 4:
-        query_grad, key_grad, value_grad, out_weight_grad, tail = finish(
+        query_grad, key_grad, value_grad, out_weight_grad, *sums = finish(
             inner_part, inner_high, half, heads_width
         )
-        features = tail[1:4, : 2 * width].reshape(6, width)
-        up_bias_grad = tail[4]
-        query_bias_grad, _, value_bias_grad = (row[0] for row in unweave(tail[:1, :qkv_width]))
+        features = sums[0]
+        query_bias_grad, value_bias_grad, up_bias_grad = (row[0] for row in sums[1:])
     else:
         inner_sums = summed(inner_part, inner_high)
         query_grad, key_grad, value_grad = unweave(inner_sums[:half, :qkv_width])

time: 438 us -> 436 us (level)
  transfers between devices with their start and end apart: 50 -> 50, of which waited for: 22 -> 20; matrix products, arithmetic and copies ran while one was open for 22% -> 21% of each run, Pallas kernels for 22% -> 22%
where the time goes in v5:
time: 436 us; the launch traced here: 431 us
  waiting for transfers between devices  125 us (29%)
  Pallas kernels  108 us (25%)
  starting transfers between devices  72.8 us (17%)
  other arithmetic  55.6 us (13%)
  matrix products  42.9 us (10%)
  local copies, waits for them, and re-layouts  23.9 us (5%)
    ppermute x50, waiting for transfers between devices, send(): moved = lax.ppermute(value, AXES, pairs)  125 us
    ppermute x50, starting transfers between devices, send(): moved = lax.ppermute(value, AXES, pairs)  72.8 us
    pallas_call x3, Pallas kernels, row_blocks(): pl.pallas_call(functools.partial(rows_kernel, starts=tuple(starts), half=...  31.1 us
    pallas_call x2, Pallas kernels, attend_back(): pl.pallas_call(kernel, grid=(pairs,), in_specs=[wide, pl.BlockSpec((1, ro...  29 us
    dot_general x8, matrix products, product_back(): lax.dot_general(left, right, (((1,), (1,)), ((), ())), preferred_element_...  21.6 us
    dot_general x3, matrix products, product(): return jnp.dot(left, right, preferred_element_type=F32).astype(out)  21.3 us
    pallas_call x1, Pallas kernels, attend(): pl.pallas_call(attend_kernel, grid=(pairs,), in_specs=[pl.BlockSpec((rows...  18.8 us
    pallas_call x4, Pallas kernels, place(): pl.pallas_call(functools.partial(place_kernel, homes=homes, half=half, sp...  14.4 us
  transfers between devices with their start and end apart: 50, of which 20 were waited for; matrix products, arithmetic and copies ran while one was open for 21% of the time, Pallas kernels for 22%

profile of v5, /device:TPU:8, one launch (start us, length us, event | category | flops | bytes accessed | tf_op | source)
XLA Modules:
  0.0 430.6 jit_solution(14777358555863828316)
XLA Ops:
  15.2 9.7 %collective-permute-done.1 = bf16[128,2048]{1,0:T(8,128)(2,1)} collective-permute-done((bf16[128,2048]{1,0:T(8,128)(2,1)}, bf16[128,2048]{1,0:T(8,128)(2,1)}, u32[]{:S(2)}, u32[]{:S(2)}) %collective-permute-start.1) | collective-permute-done | bytes 524320 | tf_op jit(solution)/shard_map/ppermute | solution.py:35
  30.4 3.5 collective-permute-start.3
  39.4 3.9 collective-permute-start.7
  43.3 9.2 %collective-permute-done.5.refs_1_ = bf16[256,2048]{1,0:T(8,128)(2,1)S(1)} collective-permute-done((bf16[256,2048]{1,0:T(8,128)(2,1)S(1)}, bf16[256,2048]{1,0:T(8,128)(2,1)S(1)}, u32[]{:S(2)}, u32[]{:S(2)}) %collective-permute-start.5) | collective-permute-done | bytes 1048608 | tf_op jit(solution)/shard_map/ppermute | solution.py:35
  60.0 3.6 place.4
  71.7 5.9 %collective-permute-start.10 = (f32[3072]{0:T(1024)S(1)}, f32[3072]{0:T(1024)S(1)}, u32[]{:S(2)}, u32[]{:S(2)}) collective-permute-start(f32[3072]{0:T(1024)S(1)} %pad_maximum_fusion.5), channel_id=1, source_target_pairs={{1,4},{3,6},{4,1},{6,3},{9,12},{11,14},{12,9},{14,11},{17,20},{19,... | collective-permute-start | bytes 36872 | tf_op jit(solution)/shard_map/ppermute | solution.py:35
  80.1 7.2 %multiply_convert_fusion.1.qkv_ref.refs_0_ = bf16[1024,1536]{1,0:T(8,128)(2,1)} fusion(bf16[1024,1536]{1,0:T(8,128)(2,1)} %get-tuple-element.101, f32[1536]{0:T(1024)S(1)} %copy-done.49, f32[1536]{0:T(1024)S(1)} %add.207, bf16[512,1024]{1,0:T(8,128)(2,1)} %collective-permute-done.7.refs_1_, bf16[512,1024]{1,0:T(8,128)(2,1)S(1)} %broadcast_select_fusion.4.refs_0_), kind=kOutput, calls=%fused_computation.2 | convolution fusion | flops 3230138368 | bytes 8400896 | tf_op jit(solution)/shard_map/dot_general | solution.py:382
  87.3 18.8 %attend.1 = (bf16[1024,512]{1,0:T(8,128)(2,1)}, f32[1024,512]{1,0:T(8,128)}) custom-call(bf16[1024,1536]{1,0:T(8,128)(2,1)} %multiply_convert_fusion.1.qkv_ref.refs_0_, f32[1,1024]{1,0:T(1,128)} %compare_select_fusion.bias_ref.refs_1_), custom_call_target="tpu_custom_call" | custom-call | flops 33554432 | bytes 524288 | tf_op jit(solution)/shard_map/attend/pallas_call | solution.py:427
  111.7 4.1 collective-permute-done.15.refs_1_
  124.4 5.6 %place.6 = (bf16[1024,2048]{1,0:T(8,128)(2,1)}, bf16[1024,2048]{1,0:T(8,128)(2,1)}) custom-call(s32[1]{0:T(128)} %bitcast.7.key_ref, bf16[256,4096]{1,0:T(8,128)(2,1)} %pad_maximum_fusion.refs_0_, bf16[256,4096]{1,0:T(8,128)(2,1)} %collective-permute-done.15.refs_1_, bf16[256,4096]{1,0:T(8,128)(2,1)} %collective-permute-done.16.refs_2_), custom_call_target="tpu_custom_call" | custom-call | tf_op jit(solution)/shard_map/place/pallas_call | solution.py:124
  130.0 14.9 %collective-permute-done.17.refs_0_ = bf16[128,4096]{1,0:T(8,128)(2,1)} collective-permute-done((bf16[128,4096]{1,0:T(8,128)(2,1)}, bf16[128,4096]{1,0:T(8,128)(2,1)}, u32[]{:S(2)}, u32[]{:S(2)}) %collective-permute-start.17) | collective-permute-done | bytes 1048608 | tf_op jit(solution)/shard_map/ppermute | solution.py:35
  148.1 12.8 %up.1 = (bf16[1024,2048]{1,0:T(8,128)(2,1)}, bf16[1024,2048]{1,0:T(8,128)(2,1)}) custom-call(bf16[512,1024]{1,0:T(8,128)(2,1)} %fusion.22.own_ref.refs_0_, bf16[512,1024]{1,0:T(8,128)(2,1)} %collective-permute-done.14.other_ref.refs_1_, bf16[1024,2048]{1,0:T(8,128)(2,1)} %get-tuple-element.111.weight_ref, f32[1,2048]{1,0:T(1,128)} %bitcast.63), custom_call_target="tpu_custom_call" | custom-call | flops 2097152 | bytes 524288 | tf_op jit(solution)/shard_map/up/pallas_call | solution.py:350
  161.0 5.3 %fusion.33 = bf16[512,1024]{1,0:T(8,128)(2,1)S(1)} fusion(bf16[1024,2048]{1,0:T(8,128)(2,1)} %get-tuple-element.113, bf16[1024,2048]{1,0:T(8,128)(2,1)} %get-tuple-element.112.refs_2_), kind=kOutput, calls=%fused_computation.65 | convolution fusion | flops 2148007936 | bytes 7340032 | tf_op jit(solution)/shard_map/dot_general | solution.py:386
  178.0 10.1 %row_blocks.3 = (bf16[256,2048]{1,0:T(8,128)(2,1)}, bf16[256,2048]{1,0:T(8,128)(2,1)}, bf16[256,2048]{1,0:T(8,128)(2,1)}, bf16[128,2048]{1,0:T(8,128)(2,1)}, bf16[128,2048]{1,0:T(8,128)(2,1)}) custom-call(s32[2]{0:T(128)} %pad_add_fusion.at_ref, bf16[512,1024]{1,0:T(8,128)(2,1)} %copy-done.19, bf16[512,1024]{1,0:T(8,128)(2,1)} %collective-permute-done.22.refs_1_, ...), custom_call_target="tpu_custom_call" | custom-call | flops 2097152 | bytes 524288 | tf_op jit(solution)/shard_map/row_blocks/pallas_call | solution.py:261
  190.2 10.6 %convert_reduce_fusion = (f32[2048]{0:T(1024)S(1)}, bf16[1024,2048]{1,0:T(8,128)(2,1)}) fusion(bf16[1024,2048]{1,0:T(8,128)(2,1)} %get-tuple-element.120, bf16[1024,2048]{1,0:T(8,128)(2,1)} %get-tuple-element.113, bf16[512,1024]{1,0:T(8,128)(2,1)} %collective-permute-done.22.refs_1_, bf16[512,1024]{1,0:T(8,128)(2,1)} %copy-done.19), kind=kOutput, calls=%fused_computation | convolution fusion | flops 4309645312 | bytes 14688256 | tf_op jit(solution)/shard_map/dot_general | solution.py:382
  207.3 9.7 %row_blocks.4 = (bf16[256,2048]{1,0:T(8,128)(2,1)}, bf16[256,2048]{1,0:T(8,128)(2,1)}, bf16[256,2048]{1,0:T(8,128)(2,1)}, bf16[128,2048]{1,0:T(8,128)(2,1)}, bf16[128,2048]{1,0:T(8,128)(2,1)}) custom-call(s32[2]{0:T(128)} %pad_add_fusion.at_ref, bf16[512,1024]{1,0:T(8,128)(2,1)} %fusion.22.own_ref.refs_0_, ...), custom_call_target="tpu_custom_call" | custom-call | flops 2097152 | bytes 524288 | tf_op jit(solution)/shard_map/row_blocks/pallas_call | solution.py:261
  217.0 5.3 %fusion.36 = bf16[512,1024]{1,0:T(8,128)(2,1)S(1)} fusion(bf16[1024,2048]{1,0:T(8,128)(2,1)} %get-tuple-element.111.weight_ref, bf16[1024,2048]{1,0:T(8,128)(2,1)} %get-tuple-element.131.refs_2_), kind=kOutput, calls=%fused_computation.66 | convolution fusion | flops 2148007936 | bytes 7340032 | tf_op jit(solution)/shard_map/dot_general | solution.py:386
  227.2 3.4 collective-permute-done.25
  235.7 3.4 collective-permute-start.21
  247.1 3.4 fusion.30.refs_4_
  250.5 14.5 %attend_back.2.refs_5_ = bf16[1024,1536]{1,0:T(8,128)(2,1)} custom-call(bf16[1024,1536]{1,0:T(8,128)(2,1)} %multiply_convert_fusion.1.qkv_ref.refs_0_, f32[1,1024]{1,0:T(1,128)} %compare_select_fusion.bias_ref.refs_1_, bf16[1024,512]{1,0:T(8,128)(2,1)} %get-tuple-element.105.refs_2_.refs_5_, f32[1024,512]{1,0:T(8,128)} %get-tuple-element.133.refs_3_, ...), custom_call_target="tpu_custom_call" | custom-call | flops 1048576 | bytes 262144 | tf_op jit(solution)/shard_map/attend_back/pallas_call | solution.py:500
  275.1 14.5 %attend_back.3.refs_4_ = bf16[1024,1536]{1,0:T(8,128)(2,1)} custom-call(bf16[1024,1536]{1,0:T(8,128)(2,1)} %multiply_convert_fusion.1.qkv_ref.refs_0_, f32[1,1024]{1,0:T(1,128)} %compare_select_fusion.bias_ref.refs_1_, bf16[1024,512]{1,0:T(8,128)(2,1)} %get-tuple-element.105.refs_2_.refs_5_, ...), custom_call_target="tpu_custom_call", output_to_operand_aliasing={{}: (5, {})} | custom-call | flops 1048576 | bytes 262144 | tf_op jit(solution)/shard_map/attend_back/pallas_call | solution.py:500
  289.6 11.4 %row_blocks.5 = (bf16[272,2048]{1,0:T(8,128)(2,1)}, bf16[272,2048]{1,0:T(8,128)(2,1)}, bf16[272,2048]{1,0:T(8,128)(2,1)}, bf16[144,2048]{1,0:T(8,128)(2,1)}, bf16[128,2048]{1,0:T(8,128)(2,1)}) custom-call(s32[2]{0:T(128)} %pad_add_fusion.at_ref, bf16[512,1024]{1,0:T(8,128)(2,1)} %copy-done.7, bf16[512,1024]{1,0:T(8,128)(2,1)} %collective-permute-done.7.refs_1_, ...), custom_call_target="tpu_custom_call" | custom-call | flops 2097152 | bytes 524288 | tf_op jit(solution)/shard_map/row_blocks/pallas_call | solution.py:261
  313.0 3.3 collective-permute-done.38
  316.3 3.7 collective-permute-done.39
  327.3 23.0 %collective-permute-done.42 = bf16[272,2048]{1,0:T(8,128)(2,1)S(1)} collective-permute-done((bf16[272,2048]{1,0:T(8,128)(2,1)S(1)}, bf16[272,2048]{1,0:T(8,128)(2,1)S(1)}, u32[]{:S(2)}, u32[]{:S(2)}) %collective-permute-start.42) | collective-permute-done | bytes 1114144 | tf_op jit(solution)/shard_map/ppermute | solution.py:35
  360.1 9.0 %collective-permute-done.45 = bf16[144,2048]{1,0:T(8,128)(2,1)} collective-permute-done((bf16[144,2048]{1,0:T(8,128)(2,1)S(1)}, bf16[144,2048]{1,0:T(8,128)(2,1)}, u32[]{:S(2)}, u32[]{:S(2)}) %collective-permute-start.45) | collective-permute-done | bytes 589856 | tf_op jit(solution)/shard_map/ppermute | solution.py:35
  370.2 6.2 %collective-permute-done.46 = bf16[144,2048]{1,0:T(8,128)(2,1)S(1)} collective-permute-done((bf16[144,2048]{1,0:T(8,128)(2,1)}, bf16[144,2048]{1,0:T(8,128)(2,1)S(1)}, u32[]{:S(2)}, u32[]{:S(2)}) %collective-permute-start.46) | collective-permute-done | bytes 589856 | tf_op jit(solution)/shard_map/ppermute | solution.py:35
  380.5 6.9 %collective-permute-start.48 = (bf16[144,2048]{1,0:T(8,128)(2,1)S(1)}, bf16[144,2048]{1,0:T(8,128)(2,1)S(1)}, u32[]{:S(2)}, u32[]{:S(2)}) collective-permute-start(bf16[144,2048]{1,0:T(8,128)(2,1)S(1)} %add_convert_fusion.11.part_ref), channel_id=1, source_target_pairs={{0,2},{1,3},{2,0},{3,1},{4,6},{5,7},{6,4},{7,5},{8,10},{9,11},{10,... | collective-permute-start | bytes 1769480 | tf_op jit(solution)/shard_map/ppermute | solution.py:35
  389.7 4.0 maximum_select_fusion
  393.8 27.6 %collective-permute-done.48.high_ref = bf16[144,2048]{1,0:T(8,128)(2,1)S(1)} collective-permute-done((bf16[144,2048]{1,0:T(8,128)(2,1)S(1)}, bf16[144,2048]{1,0:T(8,128)(2,1)S(1)}, u32[]{:S(2)}, u32[]{:S(2)}) %collective-permute-start.48) | collective-permute-done | bytes 589856 | tf_op jit(solution)/shard_map/ppermute | solution.py:35
  426.2 4.1 fusion.10
  (275 shorter events, 150.0 us)
Async XLA Ops:
  9.4 29.8 %collective-permute-start = (bf16[512,1024]{1,0:T(8,128)(2,1)}, bf16[512,1024]{1,0:T(8,128)(2,1)}, u32[]{:S(2)}, u32[]{:S(2)}) collective-permute-start(bf16[512,1024]{1,0:T(8,128)(2,1)} %dynamic-slice_bitcast_fusion.1), channel_id=1, source_target_pairs={{2,4},{3,5},{4,2},{5,3},{10,12},{11,13},{12,10},{13,11},{18,20},{1... | collective-permute-start | bytes 3145736 | tf_op jit(solution)/shard_map/ppermute | solution.py:35
  11.1 23.0 %collective-permute-start.11 = (s32[2]{0:T(128)S(1)}, s32[2]{0:T(128)S(1)}, u32[]{:S(2)}, u32[]{:S(2)}) collective-permute-start(s32[2]{0:T(128)S(1)} %copy-done.48), channel_id=1, source_target_pairs={{2,4},{3,5},{4,2},{5,3},{10,12},{11,13},{12,10},{13,11},{18,20},{1... | collective-permute-start | bytes 32 | tf_op jit(solution)/shard_map/ppermute | solution.py:35
  27.4 25.2 %collective-permute-start.5 = (bf16[256,2048]{1,0:T(8,128)(2,1)S(1)}, bf16[256,2048]{1,0:T(8,128)(2,1)S(1)}, u32[]{:S(2)}, u32[]{:S(2)}) collective-permute-start(bf16[256,2048]{1,0:T(8,128)(2,1)S(1)} %pad_maximum_fusion.2.refs_0_), channel_id=1, source_target_pairs={{0,8},{1,9},{2,10},{3,11},{4,12},{5,13},{6,14},{7,15},{8,0},{9,1},... | collective-permute-start | bytes 3145736 | tf_op jit(solution)/shard_map/ppermute | solution.py:35
  28.9 26.1 %collective-permute-start.6 = (bf16[256,2048]{1,0:T(8,128)(2,1)S(1)}, bf16[256,2048]{1,0:T(8,128)(2,1)S(1)}, u32[]{:S(2)}, u32[]{:S(2)}) collective-permute-start(bf16[256,2048]{1,0:T(8,128)(2,1)S(1)} %pad_maximum_fusion.2.refs_0_), channel_id=1, source_target_pairs={{0,16},{1,17},{2,18},{3,19},{4,20},{5,21},{6,22},{7,23},{8,24},{9,... | collective-permute-start | bytes 3145736 | tf_op jit(solution)/shard_map/ppermute | solution.py:35
  30.4 27.0 %collective-permute-start.3 = (bf16[128,4096]{1,0:T(8,128)(2,1)}, bf16[128,4096]{1,0:T(8,128)(2,1)S(1)}, u32[]{:S(2)}, u32[]{:S(2)}) collective-permute-start(bf16[128,4096]{1,0:T(8,128)(2,1)} %pad_maximum_fusion.1), channel_id=1, source_target_pairs={{1,4},{3,6},{4,1},{6,3},{9,12},{11,14},{12,9},{14,11},{17,20},{19,... | collective-permute-start | bytes 3145736 | tf_op jit(solution)/shard_map/ppermute | solution.py:35
  36.0 27.6 %collective-permute-start.4 = (bf16[128,4096]{1,0:T(8,128)(2,1)}, bf16[128,4096]{1,0:T(8,128)(2,1)}, u32[]{:S(2)}, u32[]{:S(2)}) collective-permute-start(bf16[128,4096]{1,0:T(8,128)(2,1)} %pad_maximum_fusion.1), channel_id=1, source_target_pairs={{0,1},{1,5},{2,3},{3,7},{4,0},{5,4},{6,2},{7,6},{8,9},{9,13},{10,1... | collective-permute-start | bytes 3145736 | tf_op jit(solution)/shard_map/ppermute | solution.py:35
  39.4 27.4 %collective-permute-start.7 = (bf16[512,1024]{1,0:T(8,128)(2,1)S(1)}, bf16[512,1024]{1,0:T(8,128)(2,1)}, u32[]{:S(2)}, u32[]{:S(2)}) collective-permute-start(bf16[512,1024]{1,0:T(8,128)(2,1)S(1)} %broadcast_select_fusion.4.refs_0_), channel_id=1, source_target_pairs={{0,4},{1,5},{2,6},{3,7},{4,0},{5,1},{6,2},{7,3},{8,12},{9,13},{10,... | collective-permute-start | bytes 3145736 | tf_op jit(solution)/shard_map/ppermute | solution.py:35
  52.5 25.1 %collective-permute-start.12 = (bf16[512,1024]{1,0:T(8,128)(2,1)S(1)}, bf16[512,1024]{1,0:T(8,128)(2,1)}, u32[]{:S(2)}, u32[]{:S(2)}) collective-permute-start(bf16[512,1024]{1,0:T(8,128)(2,1)S(1)} %dynamic-slice_bitcast_fusion), channel_id=1, source_target_pairs={{2,4},{3,5},{4,2},{5,3},{10,12},{11,13},{12,10},{13,11},{18,20},{1... | collective-permute-start | bytes 3145736 | tf_op jit(solution)/shard_map/ppermute | solution.py:35
  66.8 48.9 %collective-permute-start.15 = (bf16[256,4096]{1,0:T(8,128)(2,1)}, bf16[256,4096]{1,0:T(8,128)(2,1)}, u32[]{:S(2)}, u32[]{:S(2)}) collective-permute-start(bf16[256,4096]{1,0:T(8,128)(2,1)} %pad_maximum_fusion.refs_0_), channel_id=1, source_target_pairs={{0,8},{1,9},{2,10},{3,11},{4,12},{5,13},{6,14},{7,15},{8,0},{9,1},... | collective-permute-start | bytes 6291464 | tf_op jit(solution)/shard_map/ppermute | solution.py:35
  67.4 50.6 %collective-permute-start.16 = (bf16[256,4096]{1,0:T(8,128)(2,1)}, bf16[256,4096]{1,0:T(8,128)(2,1)}, u32[]{:S(2)}, u32[]{:S(2)}) collective-permute-start(bf16[256,4096]{1,0:T(8,128)(2,1)} %pad_maximum_fusion.refs_0_), channel_id=1, source_target_pairs={{0,16},{1,17},{2,18},{3,19},{4,20},{5,21},{6,22},{7,23},{8,24},{9,... | collective-permute-start | bytes 6291464 | tf_op jit(solution)/shard_map/ppermute | solution.py:35
  120.3 24.6 %collective-permute-start.17 = (bf16[128,4096]{1,0:T(8,128)(2,1)}, bf16[128,4096]{1,0:T(8,128)(2,1)}, u32[]{:S(2)}, u32[]{:S(2)}) collective-permute-start(bf16[128,4096]{1,0:T(8,128)(2,1)} %slice.142), channel_id=1, source_target_pairs={{0,16},{1,17},{2,18},{3,19},{4,20},{5,21},{6,22},{7,23},{8,24},{9,... | collective-permute-start | bytes 3145736 | tf_op jit(solution)/shard_map/ppermute | solution.py:35
  120.8 24.4 %collective-permute-start.18 = (bf16[128,4096]{1,0:T(8,128)(2,1)}, bf16[128,4096]{1,0:T(8,128)(2,1)}, u32[]{:S(2)}, u32[]{:S(2)}) collective-permute-start(bf16[128,4096]{1,0:T(8,128)(2,1)} %slice.143), channel_id=1, source_target_pairs={{0,8},{1,9},{2,10},{3,11},{4,12},{5,13},{6,14},{7,15},{8,0},{9,1},... | collective-permute-start | bytes 3145736 | tf_op jit(solution)/shard_map/ppermute | solution.py:35
  123.8 24.3 %collective-permute-start.14 = (bf16[512,1024]{1,0:T(8,128)(2,1)}, bf16[512,1024]{1,0:T(8,128)(2,1)}, u32[]{:S(2)}, u32[]{:S(2)}) collective-permute-start(bf16[512,1024]{1,0:T(8,128)(2,1)} %fusion.22.own_ref.refs_0_), channel_id=1, source_target_pairs={{0,4},{1,5},{2,6},{3,7},{4,0},{5,1},{6,2},{7,3},{8,12},{9,13},{10,... | collective-permute-start | bytes 3145736 | tf_op jit(solution)/shard_map/ppermute | solution.py:35
  176.2 46.3 %collective-permute-start.20 = (bf16[512,1024]{1,0:T(8,128)(2,1)}, bf16[512,1024]{1,0:T(8,128)(2,1)}, u32[]{:S(2)}, u32[]{:S(2)}) collective-permute-start(bf16[512,1024]{1,0:T(8,128)(2,1)} %get-tuple-element.223), channel_id=1, source_target_pairs={{2,4},{3,5},{4,2},{5,3},{10,12},{11,13},{12,10},{13,11},{18,20},{1... | collective-permute-start | bytes 3145736 | tf_op jit(solution)/shard_map/ppermute | solution.py:35
  204.6 26.0 %collective-permute-start.25 = (bf16[256,2048]{1,0:T(8,128)(2,1)}, bf16[256,2048]{1,0:T(8,128)(2,1)}, u32[]{:S(2)}, u32[]{:S(2)}) collective-permute-start(bf16[256,2048]{1,0:T(8,128)(2,1)} %add_convert_fusion.9), channel_id=1, source_target_pairs={{0,8},{1,9},{2,10},{3,11},{4,12},{5,13},{6,14},{7,15},{8,0},{9,1},... | collective-permute-start | bytes 3145736 | tf_op jit(solution)/shard_map/ppermute | solution.py:35
  205.7 25.5 %collective-permute-start.26 = (bf16[256,2048]{1,0:T(8,128)(2,1)}, bf16[256,2048]{1,0:T(8,128)(2,1)}, u32[]{:S(2)}, u32[]{:S(2)}) collective-permute-start(bf16[256,2048]{1,0:T(8,128)(2,1)} %add_convert_fusion.8), channel_id=1, source_target_pairs={{0,16},{1,17},{2,18},{3,19},{4,20},{5,21},{6,22},{7,23},{8,24},{9,... | collective-permute-start | bytes 3145736 | tf_op jit(solution)/shard_map/ppermute | solution.py:35
  235.7 39.3 %collective-permute-start.21 = (bf16[512,1024]{1,0:T(8,128)(2,1)}, bf16[512,1024]{1,0:T(8,128)(2,1)}, u32[]{:S(2)}, u32[]{:S(2)}) collective-permute-start(bf16[512,1024]{1,0:T(8,128)(2,1)} %broadcast_select_fusion.2), channel_id=1, source_target_pairs={{0,1},{1,0},{2,3},{3,2},{4,5},{5,4},{6,7},{7,6},{8,9},{9,8},{10,11... | collective-permute-start | bytes 3145736 | tf_op jit(solution)/shard_map/ppermute | solution.py:35
  239.2 25.9 %collective-permute-start.32 = (bf16[128,2048]{1,0:T(8,128)(2,1)}, bf16[128,2048]{1,0:T(8,128)(2,1)}, u32[]{:S(2)}, u32[]{:S(2)}) collective-permute-start(bf16[128,2048]{1,0:T(8,128)(2,1)} %get-tuple-element.130), channel_id=1, source_target_pairs={{0,8},{1,9},{2,10},{3,11},{4,12},{5,13},{6,14},{7,15},{8,0},{9,1},... | collective-permute-start | bytes 1572872 | tf_op jit(solution)/shard_map/ppermute | solution.py:35
  239.8 26.6 %collective-permute-start.31 = (bf16[128,2048]{1,0:T(8,128)(2,1)}, bf16[128,2048]{1,0:T(8,128)(2,1)}, u32[]{:S(2)}, u32[]{:S(2)}) collective-permute-start(bf16[128,2048]{1,0:T(8,128)(2,1)} %get-tuple-element.129), channel_id=1, source_target_pairs={{0,16},{1,17},{2,18},{3,19},{4,20},{5,21},{6,22},{7,23},{8,24},{9,... | collective-permute-start | bytes 1572872 | tf_op jit(solution)/shard_map/ppermute | solution.py:35
  244.8 26.6 %collective-permute-start.29 = (bf16[128,2048]{1,0:T(8,128)(2,1)}, bf16[128,2048]{1,0:T(8,128)(2,1)}, u32[]{:S(2)}, u32[]{:S(2)}) collective-permute-start(bf16[128,2048]{1,0:T(8,128)(2,1)} %get-tuple-element.134), channel_id=1, source_target_pairs={{1,4},{3,6},{4,1},{6,3},{9,12},{11,14},{12,9},{14,11},{17,20},{19,... | collective-permute-start | bytes 1572872 | tf_op jit(solution)/shard_map/ppermute | solution.py:35
  247.0 26.8 %collective-permute-start.30 = (bf16[128,2048]{1,0:T(8,128)(2,1)}, bf16[128,2048]{1,0:T(8,128)(2,1)}, u32[]{:S(2)}, u32[]{:S(2)}) collective-permute-start(bf16[128,2048]{1,0:T(8,128)(2,1)} %get-tuple-element.135), channel_id=1, source_target_pairs={{0,4},{1,0},{2,6},{3,2},{4,5},{5,1},{6,7},{7,3},{8,12},{9,8},{10,1... | collective-permute-start | bytes 1572872 | tf_op jit(solution)/shard_map/ppermute | solution.py:35
  268.6 34.3 %collective-permute-start.34 = (bf16[256,2048]{1,0:T(8,128)(2,1)}, bf16[256,2048]{1,0:T(8,128)(2,1)}, u32[]{:S(2)}, u32[]{:S(2)}) collective-permute-start(bf16[256,2048]{1,0:T(8,128)(2,1)} %add_convert_fusion.6), channel_id=1, source_target_pairs={{0,8},{1,9},{2,10},{3,11},{4,12},{5,13},{6,14},{7,15},{8,0},{9,1},... | collective-permute-start | bytes 3145736 | tf_op jit(solution)/shard_map/ppermute | solution.py:35
  270.1 32.8 %collective-permute-start.35 = (bf16[256,2048]{1,0:T(8,128)(2,1)S(1)}, bf16[256,2048]{1,0:T(8,128)(2,1)}, u32[]{:S(2)}, u32[]{:S(2)}) collective-permute-start(bf16[256,2048]{1,0:T(8,128)(2,1)S(1)} %add_convert_fusion.5), channel_id=1, source_target_pairs={{0,16},{1,17},{2,18},{3,19},{4,20},{5,21},{6,22},{7,23},{8,24},{9,... | collective-permute-start | bytes 3145736 | tf_op jit(solution)/shard_map/ppermute | solution.py:35
  275.0 34.3 %collective-permute-start.36 = (bf16[128,2048]{1,0:T(8,128)(2,1)S(1)}, bf16[128,2048]{1,0:T(8,128)(2,1)S(1)}, u32[]{:S(2)}, u32[]{:S(2)}) collective-permute-start(bf16[128,2048]{1,0:T(8,128)(2,1)S(1)} %add_convert_fusion.13), channel_id=1, source_target_pairs={{0,2},{1,3},{2,0},{3,1},{4,6},{5,7},{6,4},{7,5},{8,10},{9,11},{10,... | collective-permute-start | bytes 1572872 | tf_op jit(solution)/shard_map/ppermute | solution.py:35
  300.9 20.7 %collective-permute-start.41 = (bf16[128,2048]{1,0:T(8,128)(2,1)}, bf16[128,2048]{1,0:T(8,128)(2,1)S(1)}, u32[]{:S(2)}, u32[]{:S(2)}) collective-permute-start(bf16[128,2048]{1,0:T(8,128)(2,1)} %get-tuple-element.147), channel_id=1, source_target_pairs={{0,8},{1,9},{2,10},{3,11},{4,12},{5,13},{6,14},{7,15},{8,0},{9,1},... | collective-permute-start | bytes 1572872 | tf_op jit(solution)/shard_map/ppermute | solution.py:35
  301.5 20.9 %collective-permute-start.40 = (bf16[144,2048]{1,0:T(8,128)(2,1)}, bf16[144,2048]{1,0:T(8,128)(2,1)S(1)}, u32[]{:S(2)}, u32[]{:S(2)}) collective-permute-start(bf16[144,2048]{1,0:T(8,128)(2,1)} %get-tuple-element.146), channel_id=1, source_target_pairs={{0,16},{1,17},{2,18},{3,19},{4,20},{5,21},{6,22},{7,23},{8,24},{9,... | collective-permute-start | bytes 1769480 | tf_op jit(solution)/shard_map/ppermute | solution.py:35
  323.5 26.8 %collective-permute-start.42 = (bf16[272,2048]{1,0:T(8,128)(2,1)S(1)}, bf16[272,2048]{1,0:T(8,128)(2,1)S(1)}, u32[]{:S(2)}, u32[]{:S(2)}) collective-permute-start(bf16[272,2048]{1,0:T(8,128)(2,1)S(1)} %add_convert_fusion.2), channel_id=1, source_target_pairs={{0,8},{1,9},{2,10},{3,11},{4,12},{5,13},{6,14},{7,15},{8,0},{9,1},... | collective-permute-start | bytes 3342344 | tf_op jit(solution)/shard_map/ppermute | solution.py:35
  325.0 27.0 %collective-permute-start.43 = (bf16[272,2048]{1,0:T(8,128)(2,1)S(1)}, bf16[272,2048]{1,0:T(8,128)(2,1)S(1)}, u32[]{:S(2)}, u32[]{:S(2)}) collective-permute-start(bf16[272,2048]{1,0:T(8,128)(2,1)S(1)} %add_convert_fusion.1), channel_id=1, source_target_pairs={{0,16},{1,17},{2,18},{3,19},{4,20},{5,21},{6,22},{7,23},{8,24},{9,... | collective-permute-start | bytes 3342344 | tf_op jit(solution)/shard_map/ppermute | solution.py:35
  325.7 33.1 %collective-permute-start.44 = (bf16[512,1024]{1,0:T(8,128)(2,1)S(1)}, bf16[512,1024]{1,0:T(8,128)(2,1)}, u32[]{:S(2)}, u32[]{:S(2)}) collective-permute-start(bf16[512,1024]{1,0:T(8,128)(2,1)S(1)} %add_convert_fusion.3), channel_id=1, source_target_pairs={{2,4},{3,5},{4,2},{5,3},{10,12},{11,13},{12,10},{13,11},{18,20},{1... | collective-permute-start | bytes 3145736 | tf_op jit(solution)/shard_map/ppermute | solution.py:35
  355.5 31.9 %collective-permute-start.49 = (bf16[128,2048]{1,0:T(8,128)(2,1)}, bf16[128,2048]{1,0:T(8,128)(2,1)}, u32[]{:S(2)}, u32[]{:S(2)}) collective-permute-start(bf16[128,2048]{1,0:T(8,128)(2,1)} %add_convert_fusion.12), channel_id=1, source_target_pairs={{0,2},{1,3},{2,0},{3,1},{4,6},{5,7},{6,4},{7,5},{8,10},{9,11},{10,... | collective-permute-start | bytes 1572872 | tf_op jit(solution)/shard_map/ppermute | solution.py:35
  376.6 44.8 %collective-permute-start.47 = (bf16[512,1024]{1,0:T(8,128)(2,1)S(1)}, bf16[512,1024]{1,0:T(8,128)(2,1)}, u32[]{:S(2)}, u32[]{:S(2)}) collective-permute-start(bf16[512,1024]{1,0:T(8,128)(2,1)S(1)} %broadcast_select_fusion.1), channel_id=1, source_target_pairs={{0,1},{1,0},{2,3},{3,2},{4,5},{5,4},{6,7},{7,6},{8,9},{9,8},{10,11... | collective-permute-start | bytes 3145736 | tf_op jit(solution)/shard_map/ppermute | solution.py:35
  380.5 40.9 %collective-permute-start.48 = (bf16[144,2048]{1,0:T(8,128)(2,1)S(1)}, bf16[144,2048]{1,0:T(8,128)(2,1)S(1)}, u32[]{:S(2)}, u32[]{:S(2)}) collective-permute-start(bf16[144,2048]{1,0:T(8,128)(2,1)S(1)} %add_convert_fusion.11.part_ref), channel_id=1, source_target_pairs={{0,2},{1,3},{2,0},{3,1},{4,6},{5,7},{6,4},{7,5},{8,10},{9,11},{10,... | collective-permute-start | bytes 1769480 | tf_op jit(solution)/shard_map/ppermute | solution.py:35
  (68 other events, 673.8 us)
